TPU v7x, 1024 devices: a whole 4x8x16 slice. The times are simulated.
1024 devices in a mesh: ctx: 128 (over y, z_hi, x, core), tp: 8 (over z_lo).
Axes of the slice: x: 4, y: 8, z: 16 (z_hi: 2, z_lo: 8; z = z_hi * 8 + z_lo), core: 2. Of those that a mesh axis runs over, the one named last changes fastest.
Arguments:
- residual: bfloat16 [32768, 4096], P('ctx', 'tp'), may hold values from -6 to 6
- proj: bfloat16 [32768, 3, 4096], P('ctx', None, 'tp'), may hold values from -5 to 5
- short_filter: bfloat16 [7, 3, 4096], P(None, None, 'tp'), may hold values from -2.5 to 2.5
- medium_filter: bfloat16 [128, 4096], P(None, 'tp'), may hold values from -4 to 4
- skip: float32 [4096], P('tp'), may hold values from -3 to 3
- out_weight: bfloat16 [4096, 4096], P('ctx', 'tp'), may hold values from -0.09375 to 0.09375
Outputs:
- block_out: bfloat16 [32768, 4096], P('ctx', 'tp')
All inputs are finite; a program needn't handle non-finite values.
Results may differ from a plain program's by a relative error of at most 0.0085.
Values may be sent and summed in bfloat16 or wider, within the bound.
No kernel may reach another device: no remote copies, remote signals or barrier semaphores. Data moves between devices by JAX's collectives and lax.ppermute only.
A program may use at most 64 MiB of HBM per device.

v0:
```python
import jax
import jax.numpy as jnp
import numpy as np
from jax import lax
from jax.experimental import pallas as pl
from jax.experimental.pallas import tpu as pltpu
from jax.sharding import Mesh, PartitionSpec as P


SPAN = 256
HALF = 128
HEAD = 144
TAIL = 16
WROWS = 32
PACK = HALF + 3 * TAIL

F32 = jnp.float32
BF16 = jnp.bfloat16


def split(matrix):
    high = matrix.astype(np.float32).astype(BF16)
    low = (matrix - high.astype(np.float64)).astype(np.float32).astype(BF16)
    return high, low


def dft_matrices():
    n = np.arange(SPAN)
    k = np.arange(HALF)[:, None]
    angle = 2.0 * np.pi * ((k * n) % SPAN) / SPAN
    cos, sin = np.cos(angle), np.sin(angle)
    nyquist = np.where(n % 2 == 0, 1.0, -1.0)
    forward = np.concatenate([cos, -sin], 0)
    forward[HALF] = nyquist
    inverse = np.concatenate([2.0 * cos, -2.0 * sin], 0)
    inverse[0] = 1.0
    inverse[HALF] = nyquist
    inverse = inverse.T[HALF:] / SPAN
    fh, fl = split(forward)
    ih, il = split(inverse)
    return np.concatenate([fh, fl], 0), np.concatenate([ih, ih, il], 1)


def dot(a, b):
    return jnp.dot(a, b, preferred_element_type=F32)


def spectrum(forward, values):
    both = dot(forward, values)
    return both[:SPAN] + both[SPAN:]


def times(x, f):
    xr, xi, fr, fi = x[:HALF], x[HALF:], f[:HALF], f[HALF:]
    real = lax.broadcasted_iota(jnp.int32, xr.shape, 0) == 0
    rr, ii = xr * fr, xi * fi
    out_r = jnp.where(real, rr, rr - ii)
    out_i = jnp.where(real, ii, xr * fi + xi * fr)
    y = jnp.concatenate([out_r, out_i], 0)
    high = y.astype(BF16)
    low = (y - high.astype(F32)).astype(BF16)
    return jnp.concatenate([high, low, high], 0)


def taps(ext, filt, start, count):
    total = None
    for j in range(filt.shape[0]):
        term = filt[j : j + 1] * ext[pl.ds(start - j, count), :]
        total = term if total is None else total + term
    return total


def local_kernel(p, sf, pack, prod, q, ext):
    rows = p.shape[1]
    step = 64
    filt = sf[...].astype(F32)
    ext[...] = jnp.zeros_like(ext)
    for c in range(3):
        ext[c, pl.ds(8, rows), :] = p[c].astype(F32)
    for r in reversed(range(0, rows, step)):
        mixed = [taps(ext.at[c], filt[c], 8 + r, step) for c in range(3)]
        q[pl.ds(r, step), :] = mixed[0]
        prod[pl.ds(r, step), :] = (mixed[1] * mixed[2]).astype(BF16)
    pack[pl.ds(0, HALF), :] = prod[pl.ds(rows - HALF, HALF), :]
    for c in range(3):
        pack[pl.ds(HALF + c * TAIL, TAIL), :] = p[c, pl.ds(rows - TAIL, TAIL), :]


def late_kernel(prod, q, mf, skip, fwd, inv, out, spec):
    f = spectrum(fwd[:, pl.ds(0, HALF)], mf[...])
    spec[...] = f
    y = times(spectrum(fwd[...], prod[...]), f)
    skipped = HEAD - HALF
    rows = prod.shape[0] - HEAD
    filtered = dot(inv[pl.ds(skipped, rows), :], y)
    filtered = filtered + skip[...] * prod[pl.ds(HEAD, rows), :].astype(F32)
    out[...] = (q[pl.ds(HEAD, rows), :] * filtered).astype(BF16)


def early_kernel(p, halo, sf, prod, q, late, spec, skip, fwd, inv, out, ext, win):
    filt = sf[...].astype(F32)
    mixed = []
    for c in range(3):
        ext[c, pl.ds(0, TAIL), :] = halo[pl.ds(HALF + c * TAIL, TAIL), :].astype(F32)
        ext[c, pl.ds(TAIL, TAIL), :] = p[c, pl.ds(0, TAIL), :].astype(F32)
        mixed.append(taps(ext.at[c], filt[c], TAIL, TAIL))
    win[pl.ds(0, HALF), :] = halo[pl.ds(0, HALF), :]
    win[pl.ds(HALF, TAIL), :] = (mixed[1] * mixed[2]).astype(BF16)
    win[pl.ds(HALF + TAIL, SPAN - TAIL), :] = prod[pl.ds(TAIL, SPAN - TAIL), :]
    f = spec[...]
    first = dot(inv[...], times(spectrum(fwd[...], win[pl.ds(0, SPAN), :]), f))
    second = times(spectrum(fwd[...], win[pl.ds(HALF, SPAN), :]), f)
    second = dot(inv[pl.ds(0, HEAD - HALF), :], second)
    cur = win[pl.ds(HALF, HEAD), :].astype(F32) * skip[...]
    mid = HALF - TAIL
    rest = HEAD - HALF
    pieces = [
        (0, TAIL, mixed[0] * (first[:TAIL] + cur[:TAIL])),
        (TAIL, mid, q[pl.ds(TAIL, mid), :] * (first[TAIL:] + cur[TAIL:HALF])),
        (HALF, rest, q[pl.ds(HALF, rest), :] * (second + cur[HALF:])),
        (HEAD, late.shape[0], late[...]),
    ]
    for at, count, value in pieces:
        value = value.astype(BF16)
        for i in range(out.shape[0]):
            out[i, pl.ds(at, count), :] = value


def final_kernel(place, near, far, residual, *refs):
    weights, (out, wv, sem) = refs[:8], refs[8:]
    half, zh, y = place[0], place[1], place[2]
    copies = []
    for i, weight in enumerate(weights):
        for other in range(2):
            target = wv.at[lax.rem(y + i, 8), lax.rem(zh + other, 2)]
            copies.append(pltpu.make_async_copy(weight.at[:, other], target, sem.at[i, other]))
    for copy in copies:
        copy.start()
    total = residual[...].astype(F32)
    for copy in copies:
        copy.wait()
    for s in range(8):
        owner = 4 * (half if s < 4 else 1 - half) + s % 4
        part = near[s] if s < 4 else far[s - 4]
        total = total + dot(part, wv[owner].reshape(512, 512))
    out[...] = total.astype(BF16)


def sds(shape, dtype):
    return jax.ShapeDtypeStruct(shape, dtype)


def cost(flops, nbytes):
    return pl.CostEstimate(flops=flops, bytes_accessed=nbytes, transcendentals=0)


def to_all(copies, axis):
    return lax.all_to_all(copies, axis, 0, 0)


def around_y(own):
    up, down, ups, downs = own, own, [], []
    for step in range(4):
        up = lax.ppermute(up, "y", [(i, (i + 1) % 8) for i in range(8)])
        ups.append(up)
        if step < 3:
            down = lax.ppermute(down, "y", [((i + 1) % 8, i) for i in range(8)])
            downs.append(down)
    return [own] + downs + ups[::-1]


def on_device(residual, proj, short_filter, medium_filter, skip, out_weight):
    rows, chans = residual.shape
    fwd, inv = (jnp.asarray(m) for m in dft_matrices())
    p = jnp.transpose(proj, (1, 0, 2))
    sf = jnp.transpose(short_filter, (1, 0, 2))
    skip = skip.reshape(1, chans)
    half, zh, y = (lax.axis_index(a) for a in ("half", "zh", "y"))

    over = lax.ppermute(out_weight, "zh", [(0, 1), (1, 0)])

    pack, prod, q = pl.pallas_call(
        local_kernel,
        out_shape=(sds((PACK, chans), BF16), sds((rows, chans), BF16), sds((rows, chans), F32)),
        scratch_shapes=[pltpu.VMEM((3, rows + 8, chans), F32)],
        cost_estimate=cost(6_000_000, 2_000_000),
        name="local",
    )(p, sf)

    halo = lax.ppermute(pack, ("y", "zh", "x", "core"), [(i, i + 1) for i in range(127)])

    late, spec = pl.pallas_call(
        late_kernel,
        out_shape=(sds((rows - HEAD, chans), BF16), sds((SPAN, chans), F32)),
        cost_estimate=cost(300_000_000, 3_000_000),
        name="late",
    )(prod, q, medium_filter, skip, fwd, inv)

    over, late = lax.optimization_barrier((over, late))

    mine = jnp.broadcast_to(jnp.stack([out_weight, over]), (8, 2, WROWS, chans))
    row = to_all(mine, ("x", "core"))

    gated = pl.pallas_call(
        early_kernel,
        out_shape=sds((4, rows, chans), BF16),
        scratch_shapes=[
            pltpu.VMEM((3, 2 * TAIL, chans), F32),
            pltpu.VMEM((HALF + SPAN, chans), BF16),
        ],
        cost_estimate=cost(600_000_000, 3_000_000),
        name="early",
    )(p, halo, sf, prod, q, late, spec, skip, fwd, inv)
    gated, row = lax.optimization_barrier((gated, row))

    weights = around_y(row)

    across = lax.ppermute(gated[0], "half", [(0, 1), (1, 0)])
    near = to_all(gated, "quarter")
    far = to_all(jnp.broadcast_to(across, (4, rows, chans)), "quarter")

    place = jnp.stack([half, zh, y]).astype(jnp.int32)
    vmem = pl.BlockSpec(memory_space=pltpu.VMEM)
    return pl.pallas_call(
        final_kernel,
        out_shape=sds((rows, chans), BF16),
        in_specs=[pl.BlockSpec(memory_space=pltpu.SMEM)]
        + [vmem] * 3
        + [pl.BlockSpec(memory_space=pl.ANY)] * 8,
        out_specs=vmem,
        scratch_shapes=[
            pltpu.VMEM((8, 2, 8, WROWS, chans), BF16),
            pltpu.SemaphoreType.DMA((8, 2)),
        ],
        cost_estimate=cost(2 * rows * 8 * chans * chans, 8_000_000),
        name="project",
    )(place, near, far, residual, *weights)


def solution(mesh):
    devices = np.asarray(mesh.devices).reshape(8, 2, 4, 2, 2, 4)
    fine = Mesh(devices, ("y", "zh", "x", "core", "half", "quarter"))
    ctx = ("y", "zh", "x", "core")
    tp = ("half", "quarter")
    in_specs = (
        P(ctx, tp),
        P(ctx, None, tp),
        P(None, None, tp),
        P(None, tp),
        P(tp),
        P(ctx, tp),
    )

    return jax.shard_map(
        on_device, mesh=fine, in_specs=in_specs, out_specs=P(ctx, tp), check_vma=False
    )
```

profile of v0, /device:TPU:38, one launch (start us, length us, event | category | flops | bytes accessed | tf_op | source)
XLA Modules:
  0.0 168.1 jit_solution(9242991543303756458)
XLA Ops:
  0.0 19.4 %collective-permute-start.1 = (bf16[32,512]{1,0:T(8,128)(2,1)}, bf16[32,512]{1,0:T(8,128)(2,1)S(1)}, u32[]{:S(2)}, u32[]{:S(2)}) collective-permute-start(bf16[32,512]{1,0:T(8,128)(2,1)} %param.13), channel_id=1, source_target_pairs={{0,64},{64,0},{1,65},{65,1},{2,66},{66,2},{3,67},{67,3},{4,68},{68... | collective-permute-start | bytes 98312 | tf_op jit(solution)/shard_map/ppermute | solution.py:180
  19.4 3.6 %local.1 = (bf16[176,512]{1,0:T(8,128)(2,1)}, bf16[256,512]{1,0:T(8,128)(2,1)}, f32[256,512]{1,0:T(8,128)}) custom-call(bf16[3,256,512]{2,1,0:T(8,128)(2,1)} %bitcast.10, bf16[3,7,512]{2,1,0:T(8,128)(2,1)} %bitcast.12), custom_call_target="tpu_custom_call" | custom-call | flops 6000000 | bytes 2000000 | tf_op jit(solution)/shard_map/local/pallas_call | solution.py:182
  22.9 0.0 copy-start.8
  22.9 2.7 %late.1 = (bf16[112,512]{1,0:T(8,128)(2,1)}, f32[256,512]{1,0:T(8,128)}) custom-call(bf16[256,512]{1,0:T(8,128)(2,1)} %get-tuple-element.15.prod, f32[256,512]{1,0:T(8,128)} %get-tuple-element.16.q, bf16[128,512]{1,0:T(8,128)(2,1)} %mf.1, f32[1,512]{1,0:T(1,128)} %bitcast.16, bf16[512,256]{1,0:T(8,128)(2,1)} %constant.19.clone.fwd, ...), custom_call_target="tpu_custom_call" | custom-call | flops 300000000 | bytes 3000000 | tf_op jit(solution)/shard_map/late/pallas_call | solution.py:192
  25.6 0.0 collective-permute-done.1
  25.6 0.0 copy-done.8
  25.6 0.9 broadcast_in_dim.6
  26.5 0.0 copy-start.9
  26.5 4.9 %all-to-all-start = ((bf16[8,2,32,512]{3,2,1,0:T(8,128)(2,1)}), bf16[8,2,32,512]{3,2,1,0:T(8,128)(2,1)S(1)}, u32[]{:S(2)}, u32[]{:S(2)}) async-start(bf16[8,2,32,512]{3,2,1,0:T(8,128)(2,1)} %broadcast_in_dim.6), calls=%async_computation | async-start | bytes 1048576 | tf_op jit(solution)/shard_map/all_to_all | solution.py:158
  31.4 0.0 copy-done.9
  31.4 2.0 %collective-permute-start = (bf16[176,512]{1,0:T(8,128)(2,1)S(1)}, bf16[176,512]{1,0:T(8,128)(2,1)S(1)}, u32[]{:S(2)}, u32[]{:S(2)}) collective-permute-start(bf16[176,512]{1,0:T(8,128)(2,1)S(1)} %copy-done.9), channel_id=1, source_target_pairs={{0,8},{8,16},{16,24},{24,32},{32,40},{40,48},{48,56},{56,64},{64,7... | collective-permute-start | bytes 540680 | tf_op jit(solution)/shard_map/ppermute | solution.py:190
  33.4 7.6 %collective-permute-done.halo = bf16[176,512]{1,0:T(8,128)(2,1)S(1)} collective-permute-done((bf16[176,512]{1,0:T(8,128)(2,1)S(1)}, bf16[176,512]{1,0:T(8,128)(2,1)S(1)}, u32[]{:S(2)}, u32[]{:S(2)}) %collective-permute-start) | collective-permute-done | bytes 180256 | tf_op jit(solution)/shard_map/ppermute | solution.py:190
  41.0 0.0 copy-start.7
  41.0 0.7 copy-done.7
  41.7 3.9 %early.1 = bf16[4,256,512]{2,1,0:T(8,128)(2,1)} custom-call(bf16[3,256,512]{2,1,0:T(8,128)(2,1)} %bitcast.11, bf16[176,512]{1,0:T(8,128)(2,1)} %copy-done.7, bf16[3,7,512]{2,1,0:T(8,128)(2,1)} %bitcast.13, bf16[256,512]{1,0:T(8,128)(2,1)} %get-tuple-element.15.prod, f32[256,512]{1,0:T(8,128)} %get-tuple-element.16.q, ...), custom_call_target="tpu_custom_call" | custom-call | flops 600000000 | bytes 3000000 | tf_op jit(solution)/shard_map/early/pallas_call | solution.py:204
  45.6 0.0 all-to-all-done.refs_0_
  45.6 0.0 copy-start.2
  45.6 4.6 %all-to-all-start.1 = ((bf16[4,256,512]{2,1,0:T(8,128)(2,1)}), bf16[4,256,512]{2,1,0:T(8,128)(2,1)S(1)}, u32[]{:S(2)}, u32[]{:S(2)}) async-start(bf16[4,256,512]{2,1,0:T(8,128)(2,1)} %early.1), calls=%async_computation.1 | async-start | bytes 2097152 | tf_op jit(solution)/shard_map/all_to_all | solution.py:158
  50.2 1.0 slice_bitcast_fusion
  51.2 6.1 %collective-permute-start.2 = (bf16[256,512]{1,0:T(8,128)(2,1)S(1)}, bf16[256,512]{1,0:T(8,128)(2,1)S(1)}, u32[]{:S(2)}, u32[]{:S(2)}) collective-permute-start(bf16[256,512]{1,0:T(8,128)(2,1)S(1)} %slice_bitcast_fusion), channel_id=1, source_target_pairs={{0,4},{4,0},{1,5},{5,1},{2,6},{6,2},{3,7},{7,3},{8,12},{12,8},{9,1... | collective-permute-start | bytes 786440 | tf_op jit(solution)/shard_map/ppermute | solution.py:218
  57.3 14.0 %collective-permute-done.2 = bf16[256,512]{1,0:T(8,128)(2,1)S(1)} collective-permute-done((bf16[256,512]{1,0:T(8,128)(2,1)S(1)}, bf16[256,512]{1,0:T(8,128)(2,1)S(1)}, u32[]{:S(2)}, u32[]{:S(2)}) %collective-permute-start.2) | collective-permute-done | bytes 262176 | tf_op jit(solution)/shard_map/ppermute | solution.py:218
  71.3 16.3 %all-to-all-done.1.near = bf16[4,256,512]{2,1,0:T(8,128)(2,1)S(1)} async-done(((bf16[4,256,512]{2,1,0:T(8,128)(2,1)}), bf16[4,256,512]{2,1,0:T(8,128)(2,1)S(1)}, u32[]{:S(2)}, u32[]{:S(2)}) %all-to-all-start.1) | async-done | bytes 1048608 | tf_op jit(solution)/shard_map/all_to_all | solution.py:158
  87.6 0.0 copy-start
  87.6 1.1 broadcast_in_dim.7
  88.7 0.2 copy-done
  88.9 4.0 %all-to-all-start.2 = ((bf16[4,256,512]{2,1,0:T(8,128)(2,1)}), bf16[4,256,512]{2,1,0:T(8,128)(2,1)S(1)}, u32[]{:S(2)}, u32[]{:S(2)}) async-start(bf16[4,256,512]{2,1,0:T(8,128)(2,1)} %broadcast_in_dim.7), calls=%async_computation.2 | async-start | bytes 2097152 | tf_op jit(solution)/shard_map/all_to_all | solution.py:158
  92.9 2.6 %collective-permute-start.6 = (bf16[8,2,32,512]{3,2,1,0:T(8,128)(2,1)S(1)}, bf16[8,2,32,512]{3,2,1,0:T(8,128)(2,1)S(1)}, u32[]{:S(2)}, u32[]{:S(2)}) collective-permute-start(bf16[8,2,32,512]{3,2,1,0:T(8,128)(2,1)S(1)} %all-to-all-done.refs_0_), channel_id=1, source_target_pairs={{0,128},{128,256},{256,384},{384,512},{512,640},{640,768},{768,896... | collective-permute-start | bytes 1572872 | tf_op jit(solution)/shard_map/ppermute | solution.py:164
  95.5 0.0 copy-done.2
  95.5 4.5 %collective-permute-start.3 = (bf16[8,2,32,512]{3,2,1,0:T(8,128)(2,1)S(1)}, bf16[8,2,32,512]{3,2,1,0:T(8,128)(2,1)S(1)}, u32[]{:S(2)}, u32[]{:S(2)}) collective-permute-start(bf16[8,2,32,512]{3,2,1,0:T(8,128)(2,1)S(1)} %all-to-all-done.refs_0_), channel_id=1, source_target_pairs={{128,0},{256,128},{384,256},{512,384},{640,512},{768,640},{896,768... | collective-permute-start | bytes 1572872 | tf_op jit(solution)/shard_map/ppermute | solution.py:167
  100.0 9.8 %collective-permute-done.6.refs_7_ = bf16[8,2,32,512]{3,2,1,0:T(8,128)(2,1)S(1)} collective-permute-done((bf16[8,2,32,512]{3,2,1,0:T(8,128)(2,1)S(1)}, bf16[8,2,32,512]{3,2,1,0:T(8,128)(2,1)S(1)}, u32[]{:S(2)}, u32[]{:S(2)}) %collective-permute-start.6) | collective-permute-done | bytes 524320 | tf_op jit(solution)/shard_map/ppermute | solution.py:164
  109.7 0.0 copy-start.3
  109.7 1.9 %collective-permute-start.7 = (bf16[8,2,32,512]{3,2,1,0:T(8,128)(2,1)S(1)}, bf16[8,2,32,512]{3,2,1,0:T(8,128)(2,1)S(1)}, u32[]{:S(2)}, u32[]{:S(2)}) collective-permute-start(bf16[8,2,32,512]{3,2,1,0:T(8,128)(2,1)S(1)} %collective-permute-done.6.refs_7_), channel_id=1, source_target_pairs={{0,128},{128,256},{256,384},{384,512},{512,640},{640,768},{768,896... | collective-permute-start | bytes 1572872 | tf_op jit(solution)/shard_map/ppermute | solution.py:164
  111.7 0.0 collective-permute-done.3.refs_1_
  111.7 0.0 copy-start.4
  111.7 5.4 %collective-permute-start.4 = (bf16[8,2,32,512]{3,2,1,0:T(8,128)(2,1)S(1)}, bf16[8,2,32,512]{3,2,1,0:T(8,128)(2,1)S(1)}, u32[]{:S(2)}, u32[]{:S(2)}) collective-permute-start(bf16[8,2,32,512]{3,2,1,0:T(8,128)(2,1)S(1)} %collective-permute-done.3.refs_1_), channel_id=1, source_target_pairs={{128,0},{256,128},{384,256},{512,384},{640,512},{768,640},{896,768... | collective-permute-start | bytes 1572872 | tf_op jit(solution)/shard_map/ppermute | solution.py:167
  117.1 10.5 %collective-permute-done.7.refs_6_ = bf16[8,2,32,512]{3,2,1,0:T(8,128)(2,1)S(1)} collective-permute-done((bf16[8,2,32,512]{3,2,1,0:T(8,128)(2,1)S(1)}, bf16[8,2,32,512]{3,2,1,0:T(8,128)(2,1)S(1)}, u32[]{:S(2)}, u32[]{:S(2)}) %collective-permute-start.7) | collective-permute-done | bytes 524320 | tf_op jit(solution)/shard_map/ppermute | solution.py:164
  127.6 0.0 copy-start.5
  127.6 1.9 %collective-permute-start.8 = (bf16[8,2,32,512]{3,2,1,0:T(8,128)(2,1)S(1)}, bf16[8,2,32,512]{3,2,1,0:T(8,128)(2,1)}, u32[]{:S(2)}, u32[]{:S(2)}) collective-permute-start(bf16[8,2,32,512]{3,2,1,0:T(8,128)(2,1)S(1)} %collective-permute-done.7.refs_6_), channel_id=1, source_target_pairs={{0,128},{128,256},{256,384},{384,512},{512,640},{640,768},{768,896... | collective-permute-start | bytes 1572872 | tf_op jit(solution)/shard_map/ppermute | solution.py:164
  129.5 0.0 collective-permute-done.4.refs_2_
  129.5 0.0 copy-start.6
  129.5 5.2 %collective-permute-start.5 = (bf16[8,2,32,512]{3,2,1,0:T(8,128)(2,1)S(1)}, bf16[8,2,32,512]{3,2,1,0:T(8,128)(2,1)}, u32[]{:S(2)}, u32[]{:S(2)}) collective-permute-start(bf16[8,2,32,512]{3,2,1,0:T(8,128)(2,1)S(1)} %collective-permute-done.4.refs_2_), channel_id=1, source_target_pairs={{128,0},{256,128},{384,256},{512,384},{640,512},{768,640},{896,768... | collective-permute-start | bytes 1572872 | tf_op jit(solution)/shard_map/ppermute | solution.py:167
  134.7 10.0 %collective-permute-done.8.refs_5_ = bf16[8,2,32,512]{3,2,1,0:T(8,128)(2,1)} collective-permute-done((bf16[8,2,32,512]{3,2,1,0:T(8,128)(2,1)S(1)}, bf16[8,2,32,512]{3,2,1,0:T(8,128)(2,1)}, u32[]{:S(2)}, u32[]{:S(2)}) %collective-permute-start.8) | collective-permute-done | bytes 524320 | tf_op jit(solution)/shard_map/ppermute | solution.py:164
  144.7 1.9 %collective-permute-start.9 = (bf16[8,2,32,512]{3,2,1,0:T(8,128)(2,1)}, bf16[8,2,32,512]{3,2,1,0:T(8,128)(2,1)}, u32[]{:S(2)}, u32[]{:S(2)}) collective-permute-start(bf16[8,2,32,512]{3,2,1,0:T(8,128)(2,1)} %collective-permute-done.8.refs_5_), channel_id=1, source_target_pairs={{0,128},{128,256},{256,384},{384,512},{512,640},{640,768},{768,896... | collective-permute-start | bytes 1572872 | tf_op jit(solution)/shard_map/ppermute | solution.py:164
  146.7 0.6 pad_add_fusion.place
  147.3 0.0 collective-permute-done.5.refs_3_
  147.3 14.0 %collective-permute-done.9.refs_4_ = bf16[8,2,32,512]{3,2,1,0:T(8,128)(2,1)} collective-permute-done((bf16[8,2,32,512]{3,2,1,0:T(8,128)(2,1)}, bf16[8,2,32,512]{3,2,1,0:T(8,128)(2,1)}, u32[]{:S(2)}, u32[]{:S(2)}) %collective-permute-start.9) | collective-permute-done | bytes 524320 | tf_op jit(solution)/shard_map/ppermute | solution.py:164
  161.2 0.0 all-to-all-done.2.far
  161.3 0.0 copy-done.3
  161.3 0.0 copy-done.4
  161.3 0.0 copy-done.5
  161.3 0.0 copy-done.6
  161.3 0.0 copy-start.1
  161.3 0.9 copy-done.1
  162.2 5.8 %project.1 = bf16[256,512]{1,0:T(8,128)(2,1)} custom-call(s32[3]{0:T(128)} %pad_add_fusion.place, bf16[4,256,512]{2,1,0:T(8,128)(2,1)} %copy-done, bf16[4,256,512]{2,1,0:T(8,128)(2,1)} %copy-done.1, bf16[256,512]{1,0:T(8,128)(2,1)} %residual.1, bf16[8,2,32,512]{3,2,1,0:T(8,128)(2,1)} %copy-done.2, bf16[8,2,32,512]{3,2,1,0:T(8,128)(2,1)} %copy-done.4, ...), custom_call_target="tpu_custom_call" | custom-call | flops 1073741824 | bytes 8000000 | tf_op jit(solution)/shard_map/project/pallas_call | solution.py:224
  (1 shorter events, 0.0 us)
Async XLA Ops:
  0.0 25.6 %collective-permute-start.1 = (bf16[32,512]{1,0:T(8,128)(2,1)}, bf16[32,512]{1,0:T(8,128)(2,1)S(1)}, u32[]{:S(2)}, u32[]{:S(2)}) collective-permute-start(bf16[32,512]{1,0:T(8,128)(2,1)} %param.13), channel_id=1, source_target_pairs={{0,64},{64,0},{1,65},{65,1},{2,66},{66,2},{3,67},{67,3},{4,68},{68... | collective-permute-start | bytes 98312 | tf_op jit(solution)/shard_map/ppermute | solution.py:180
  22.9 2.7 %copy-start.8 = (bf16[32,512]{1,0:T(8,128)(2,1)S(1)}, bf16[32,512]{1,0:T(8,128)(2,1)}, u32[]{:S(2)}) copy-start(bf16[32,512]{1,0:T(8,128)(2,1)} %param.13) | copy-start | bytes 98308
  26.5 4.9 %copy-start.9 = (bf16[176,512]{1,0:T(8,128)(2,1)S(1)}, bf16[176,512]{1,0:T(8,128)(2,1)}, u32[]{:S(2)}) copy-start(bf16[176,512]{1,0:T(8,128)(2,1)} %get-tuple-element.14) | copy-start | bytes 540676
  26.5 19.1 %all-to-all-start = ((bf16[8,2,32,512]{3,2,1,0:T(8,128)(2,1)}), bf16[8,2,32,512]{3,2,1,0:T(8,128)(2,1)S(1)}, u32[]{:S(2)}, u32[]{:S(2)}) async-start(bf16[8,2,32,512]{3,2,1,0:T(8,128)(2,1)} %broadcast_in_dim.6), calls=%async_computation | async-start | bytes 1048576 | tf_op jit(solution)/shard_map/all_to_all | solution.py:158
  31.4 9.6 %collective-permute-start = (bf16[176,512]{1,0:T(8,128)(2,1)S(1)}, bf16[176,512]{1,0:T(8,128)(2,1)S(1)}, u32[]{:S(2)}, u32[]{:S(2)}) collective-permute-start(bf16[176,512]{1,0:T(8,128)(2,1)S(1)} %copy-done.9), channel_id=1, source_target_pairs={{0,8},{8,16},{16,24},{24,32},{32,40},{40,48},{48,56},{56,64},{64,7... | collective-permute-start | bytes 540680 | tf_op jit(solution)/shard_map/ppermute | solution.py:190
  41.0 0.7 copy-start.7
  45.6 49.9 %copy-start.2 = (bf16[8,2,32,512]{3,2,1,0:T(8,128)(2,1)}, bf16[8,2,32,512]{3,2,1,0:T(8,128)(2,1)S(1)}, u32[]{:S(2)}) copy-start(bf16[8,2,32,512]{3,2,1,0:T(8,128)(2,1)S(1)} %all-to-all-done.refs_0_) | copy-start | bytes 1572868
  45.6 41.9 %all-to-all-start.1 = ((bf16[4,256,512]{2,1,0:T(8,128)(2,1)}), bf16[4,256,512]{2,1,0:T(8,128)(2,1)S(1)}, u32[]{:S(2)}, u32[]{:S(2)}) async-start(bf16[4,256,512]{2,1,0:T(8,128)(2,1)} %early.1), calls=%async_computation.1 | async-start | bytes 2097152 | tf_op jit(solution)/shard_map/all_to_all | solution.py:158
  51.2 20.1 %collective-permute-start.2 = (bf16[256,512]{1,0:T(8,128)(2,1)S(1)}, bf16[256,512]{1,0:T(8,128)(2,1)S(1)}, u32[]{:S(2)}, u32[]{:S(2)}) collective-permute-start(bf16[256,512]{1,0:T(8,128)(2,1)S(1)} %slice_bitcast_fusion), channel_id=1, source_target_pairs={{0,4},{4,0},{1,5},{5,1},{2,6},{6,2},{3,7},{7,3},{8,12},{12,8},{9,1... | collective-permute-start | bytes 786440 | tf_op jit(solution)/shard_map/ppermute | solution.py:218
  87.6 1.3 copy-start
  88.9 72.4 %all-to-all-start.2 = ((bf16[4,256,512]{2,1,0:T(8,128)(2,1)}), bf16[4,256,512]{2,1,0:T(8,128)(2,1)S(1)}, u32[]{:S(2)}, u32[]{:S(2)}) async-start(bf16[4,256,512]{2,1,0:T(8,128)(2,1)} %broadcast_in_dim.7), calls=%async_computation.2 | async-start | bytes 2097152 | tf_op jit(solution)/shard_map/all_to_all | solution.py:158
  92.9 16.8 %collective-permute-start.6 = (bf16[8,2,32,512]{3,2,1,0:T(8,128)(2,1)S(1)}, bf16[8,2,32,512]{3,2,1,0:T(8,128)(2,1)S(1)}, u32[]{:S(2)}, u32[]{:S(2)}) collective-permute-start(bf16[8,2,32,512]{3,2,1,0:T(8,128)(2,1)S(1)} %all-to-all-done.refs_0_), channel_id=1, source_target_pairs={{0,128},{128,256},{256,384},{384,512},{512,640},{640,768},{768,896... | collective-permute-start | bytes 1572872 | tf_op jit(solution)/shard_map/ppermute | solution.py:164
  95.5 16.2 %collective-permute-start.3 = (bf16[8,2,32,512]{3,2,1,0:T(8,128)(2,1)S(1)}, bf16[8,2,32,512]{3,2,1,0:T(8,128)(2,1)S(1)}, u32[]{:S(2)}, u32[]{:S(2)}) collective-permute-start(bf16[8,2,32,512]{3,2,1,0:T(8,128)(2,1)S(1)} %all-to-all-done.refs_0_), channel_id=1, source_target_pairs={{128,0},{256,128},{384,256},{512,384},{640,512},{768,640},{896,768... | collective-permute-start | bytes 1572872 | tf_op jit(solution)/shard_map/ppermute | solution.py:167
  109.7 51.5 %copy-start.3 = (bf16[8,2,32,512]{3,2,1,0:T(8,128)(2,1)}, bf16[8,2,32,512]{3,2,1,0:T(8,128)(2,1)S(1)}, u32[]{:S(2)}) copy-start(bf16[8,2,32,512]{3,2,1,0:T(8,128)(2,1)S(1)} %collective-permute-done.6.refs_7_) | copy-start | bytes 1572868
  109.7 17.9 %collective-permute-start.7 = (bf16[8,2,32,512]{3,2,1,0:T(8,128)(2,1)S(1)}, bf16[8,2,32,512]{3,2,1,0:T(8,128)(2,1)S(1)}, u32[]{:S(2)}, u32[]{:S(2)}) collective-permute-start(bf16[8,2,32,512]{3,2,1,0:T(8,128)(2,1)S(1)} %collective-permute-done.6.refs_7_), channel_id=1, source_target_pairs={{0,128},{128,256},{256,384},{384,512},{512,640},{640,768},{768,896... | collective-permute-start | bytes 1572872 | tf_op jit(solution)/shard_map/ppermute | solution.py:164
  111.7 49.6 %copy-start.4 = (bf16[8,2,32,512]{3,2,1,0:T(8,128)(2,1)}, bf16[8,2,32,512]{3,2,1,0:T(8,128)(2,1)S(1)}, u32[]{:S(2)}) copy-start(bf16[8,2,32,512]{3,2,1,0:T(8,128)(2,1)S(1)} %collective-permute-done.3.refs_1_) | copy-start | bytes 1572868
  111.7 17.8 %collective-permute-start.4 = (bf16[8,2,32,512]{3,2,1,0:T(8,128)(2,1)S(1)}, bf16[8,2,32,512]{3,2,1,0:T(8,128)(2,1)S(1)}, u32[]{:S(2)}, u32[]{:S(2)}) collective-permute-start(bf16[8,2,32,512]{3,2,1,0:T(8,128)(2,1)S(1)} %collective-permute-done.3.refs_1_), channel_id=1, source_target_pairs={{128,0},{256,128},{384,256},{512,384},{640,512},{768,640},{896,768... | collective-permute-start | bytes 1572872 | tf_op jit(solution)/shard_map/ppermute | solution.py:167
  127.6 33.7 %copy-start.5 = (bf16[8,2,32,512]{3,2,1,0:T(8,128)(2,1)}, bf16[8,2,32,512]{3,2,1,0:T(8,128)(2,1)S(1)}, u32[]{:S(2)}) copy-start(bf16[8,2,32,512]{3,2,1,0:T(8,128)(2,1)S(1)} %collective-permute-done.7.refs_6_) | copy-start | bytes 1572868
  127.6 17.1 %collective-permute-start.8 = (bf16[8,2,32,512]{3,2,1,0:T(8,128)(2,1)S(1)}, bf16[8,2,32,512]{3,2,1,0:T(8,128)(2,1)}, u32[]{:S(2)}, u32[]{:S(2)}) collective-permute-start(bf16[8,2,32,512]{3,2,1,0:T(8,128)(2,1)S(1)} %collective-permute-done.7.refs_6_), channel_id=1, source_target_pairs={{0,128},{128,256},{256,384},{384,512},{512,640},{640,768},{768,896... | collective-permute-start | bytes 1572872 | tf_op jit(solution)/shard_map/ppermute | solution.py:164
  129.5 31.7 %copy-start.6 = (bf16[8,2,32,512]{3,2,1,0:T(8,128)(2,1)}, bf16[8,2,32,512]{3,2,1,0:T(8,128)(2,1)S(1)}, u32[]{:S(2)}) copy-start(bf16[8,2,32,512]{3,2,1,0:T(8,128)(2,1)S(1)} %collective-permute-done.4.refs_2_) | copy-start | bytes 1572868
  129.5 17.7 %collective-permute-start.5 = (bf16[8,2,32,512]{3,2,1,0:T(8,128)(2,1)S(1)}, bf16[8,2,32,512]{3,2,1,0:T(8,128)(2,1)}, u32[]{:S(2)}, u32[]{:S(2)}) collective-permute-start(bf16[8,2,32,512]{3,2,1,0:T(8,128)(2,1)S(1)} %collective-permute-done.4.refs_2_), channel_id=1, source_target_pairs={{128,0},{256,128},{384,256},{512,384},{640,512},{768,640},{896,768... | collective-permute-start | bytes 1572872 | tf_op jit(solution)/shard_map/ppermute | solution.py:167
  144.7 16.5 %collective-permute-start.9 = (bf16[8,2,32,512]{3,2,1,0:T(8,128)(2,1)}, bf16[8,2,32,512]{3,2,1,0:T(8,128)(2,1)}, u32[]{:S(2)}, u32[]{:S(2)}) collective-permute-start(bf16[8,2,32,512]{3,2,1,0:T(8,128)(2,1)} %collective-permute-done.8.refs_5_), channel_id=1, source_target_pairs={{0,128},{128,256},{256,384},{384,512},{512,640},{640,768},{768,896... | collective-permute-start | bytes 1572872 | tf_op jit(solution)/shard_map/ppermute | solution.py:164
  161.3 0.9 copy-start.1
where the time goes:
time: 169 us; the launch traced here: 168 us
  waiting for transfers between devices  82.1 us (49%)
  starting transfers between devices  64.3 us (38%)
  Pallas kernels  16 us (9%)
  local copies, waits for them, and re-layouts  4.79 us (3%)
    ppermute x4, waiting for transfers between devices, around_y(): up = lax.ppermute(up, 'y', [(i, (i + 1) % 8) for i in range(8)])  44.3 us
    ppermute x1, starting transfers between devices, on_device(): over = lax.ppermute(out_weight, 'zh', [(0, 1), (1, 0)])  19.4 us
    all_to_all x3, waiting for transfers between devices, to_all(): return lax.all_to_all(copies, axis, 0, 0)  16.3 us
    ppermute x3, starting transfers between devices, around_y(): down = lax.ppermute(down, 'y', [((i + 1) % 8, i) for i in range(8)])  15.1 us
    ppermute x1, waiting for transfers between devices, on_device(): across = lax.ppermute(gated[0], 'half', [(0, 1), (1, 0)])  14 us
    all_to_all x3, starting transfers between devices, to_all(): return lax.all_to_all(copies, axis, 0, 0)  13.5 us
    ppermute x4, starting transfers between devices, around_y(): up = lax.ppermute(up, 'y', [(i, (i + 1) % 8) for i in range(8)])  8.3 us
    ppermute x1, waiting for transfers between devices, on_device(): lax.ppermute(pack, ('y', 'zh', 'x', 'core'), [(i, i + 1) for i in range(1...  7.55 us
  transfers between devices with their start and end apart: 13, of which 7 were waited for; matrix products, arithmetic and copies ran while one was open for 1% of the time, Pallas kernels for 6%

commit v1 on v0

--- a/solution.py
+++ b/solution.py
@@ -97,7 +97,7 @@
     out[...] = (q[pl.ds(HEAD, rows), :] * filtered).astype(BF16)
 
 
-def early_kernel(p, halo, sf, prod, q, late, spec, skip, fwd, inv, out, ext, win):
+def early_kernel(p, halo, sf, prod, q, late, spec, skip, fwd, inv, one, out, ext, win):
     filt = sf[...].astype(F32)
     mixed = []
     for c in range(3):
@@ -122,27 +122,41 @@
     ]
     for at, count, value in pieces:
         value = value.astype(BF16)
+        one[pl.ds(at, count), :] = value
         for i in range(out.shape[0]):
             out[i, pl.ds(at, count), :] = value
 
 
+def arrange_kernel(place, mine, over, *refs):
+    arrived, out = refs[:3], refs[3]
+    zh, x = place[1], place[3]
+    for rel in range(4):
+        for other in range(2):
+            piece = (mine, over)[other][...] if rel == 0 else arrived[rel - 1][other]
+            out[lax.rem(zh + other, 2), lax.rem(x + rel, 4)] = piece
+
+
 def final_kernel(place, near, far, residual, *refs):
-    weights, (out, wv, sem) = refs[:8], refs[8:]
-    half, zh, y = place[0], place[1], place[2]
-    copies = []
+    weights, (out, gv, wv, gsem, wsem) = refs[:16], refs[16:]
+    half, y, core = place[0], place[2], place[4]
+    gated = [
+        pltpu.make_async_copy(near, gv.at[pl.ds(4 * half, 4)], gsem.at[0]),
+        pltpu.make_async_copy(far, gv.at[pl.ds(4 * (1 - half), 4)], gsem.at[1]),
+    ]
+    rows = []
     for i, weight in enumerate(weights):
-        for other in range(2):
-            target = wv.at[lax.rem(y + i, 8), lax.rem(zh + other, 2)]
-            copies.append(pltpu.make_async_copy(weight.at[:, other], target, sem.at[i, other]))
-    for copy in copies:
+        target = wv.at[lax.rem(y + i // 2, 8), :, :, lax.rem(core + i % 2, 2)]
+        rows.append(pltpu.make_async_copy(weight, target, wsem.at[i]))
+    for copy in gated + rows:
         copy.start()
     total = residual[...].astype(F32)
-    for copy in copies:
+    for copy in gated:
         copy.wait()
-    for s in range(8):
-        owner = 4 * (half if s < 4 else 1 - half) + s % 4
-        part = near[s] if s < 4 else far[s - 4]
-        total = total + dot(part, wv[owner].reshape(512, 512))
+    for i in range(8):
+        rows[2 * i].wait()
+        rows[2 * i + 1].wait()
+        k = lax.rem(y + i, 8)
+        total = total + dot(gv[k], wv[k].reshape(512, 512))
     out[...] = total.astype(BF16)
 
 
@@ -152,10 +166,6 @@
 
 def cost(flops, nbytes):
     return pl.CostEstimate(flops=flops, bytes_accessed=nbytes, transcendentals=0)
-
-
-def to_all(copies, axis):
-    return lax.all_to_all(copies, axis, 0, 0)
 
 
 def around_y(own):
@@ -175,7 +185,8 @@
     p = jnp.transpose(proj, (1, 0, 2))
     sf = jnp.transpose(short_filter, (1, 0, 2))
     skip = skip.reshape(1, chans)
-    half, zh, y = (lax.axis_index(a) for a in ("half", "zh", "y"))
+    place = jnp.stack([lax.axis_index(a) for a in ("half", "zh", "y", "x", "core")])
+    place = place.astype(jnp.int32)
 
     over = lax.ppermute(out_weight, "zh", [(0, 1), (1, 0)])
 
@@ -198,12 +209,14 @@
 
     over, late = lax.optimization_barrier((over, late))
 
-    mine = jnp.broadcast_to(jnp.stack([out_weight, over]), (8, 2, WROWS, chans))
-    row = to_all(mine, ("x", "core"))
-
-    gated = pl.pallas_call(
+    mine = jnp.stack([out_weight, over])
+    arrived = []
+    for by in (1, 2, 3):
+        arrived.append(lax.ppermute(mine, "x", [((i + by) % 4, i) for i in range(4)]))
+
+    gated, copies = pl.pallas_call(
         early_kernel,
-        out_shape=sds((4, rows, chans), BF16),
+        out_shape=(sds((rows, chans), BF16), sds((4, rows, chans), BF16)),
         scratch_shapes=[
             pltpu.VMEM((3, 2 * TAIL, chans), F32),
             pltpu.VMEM((HALF + SPAN, chans), BF16),
@@ -211,26 +224,36 @@
         cost_estimate=cost(600_000_000, 3_000_000),
         name="early",
     )(p, halo, sf, prod, q, late, spec, skip, fwd, inv)
-    gated, row = lax.optimization_barrier((gated, row))
-
-    weights = around_y(row)
-
-    across = lax.ppermute(gated[0], "half", [(0, 1), (1, 0)])
-    near = to_all(gated, "quarter")
-    far = to_all(jnp.broadcast_to(across, (4, rows, chans)), "quarter")
-
-    place = jnp.stack([half, zh, y]).astype(jnp.int32)
+
+    across = lax.ppermute(gated, "half", [(0, 1), (1, 0)])
+    near = lax.all_to_all(copies, "quarter", 0, 0)
+    far = lax.all_to_all(jnp.broadcast_to(across, (4, rows, chans)), "quarter", 0, 0)
+
+    smem = pl.BlockSpec(memory_space=pltpu.SMEM)
     vmem = pl.BlockSpec(memory_space=pltpu.VMEM)
+    anywhere = pl.BlockSpec(memory_space=pl.ANY)
+    block = pl.pallas_call(
+        arrange_kernel,
+        out_shape=sds((2, 4, WROWS, chans), BF16),
+        in_specs=[smem] + [vmem] * 5,
+        out_specs=vmem,
+        cost_estimate=cost(0, 500_000),
+        name="arrange",
+    )(place, out_weight, over, *arrived)
+    weights = []
+    for own in around_y(block):
+        weights += [own, lax.ppermute(own, "core", [(0, 1), (1, 0)])]
+
     return pl.pallas_call(
         final_kernel,
         out_shape=sds((rows, chans), BF16),
-        in_specs=[pl.BlockSpec(memory_space=pltpu.SMEM)]
-        + [vmem] * 3
-        + [pl.BlockSpec(memory_space=pl.ANY)] * 8,
+        in_specs=[smem, anywhere, anywhere, vmem] + [anywhere] * 16,
         out_specs=vmem,
         scratch_shapes=[
-            pltpu.VMEM((8, 2, 8, WROWS, chans), BF16),
-            pltpu.SemaphoreType.DMA((8, 2)),
+            pltpu.VMEM((8, rows, chans), BF16),
+            pltpu.VMEM((8, 2, 4, 2, WROWS, chans), BF16),
+            pltpu.SemaphoreType.DMA((2,)),
+            pltpu.SemaphoreType.DMA((16,)),
         ],
         cost_estimate=cost(2 * rows * 8 * chans * chans, 8_000_000),
         name="project",

time: 169 us -> 162 us (0.959)
  the two profiles are of different devices: /device:TPU:38 before, /device:TPU:1 now
where the time goes in v1:
time: 162 us; the launch traced here: 160 us
  starting transfers between devices  94.1 us (58%)
  waiting for transfers between devices  41.4 us (26%)
  Pallas kernels  18.2 us (11%)
  local copies, waits for them, and re-layouts  5.91 us (4%)
    ppermute x8, starting transfers between devices, on_device(): weights += [own, lax.ppermute(own, 'core', [(0, 1), (1, 0)])]  20.3 us
    ppermute x1, starting transfers between devices, on_device(): over = lax.ppermute(out_weight, 'zh', [(0, 1), (1, 0)])  19.1 us
    all_to_all x1, waiting for transfers between devices, on_device(): near = lax.all_to_all(copies, 'quarter', 0, 0)  16.4 us
    ppermute x1, waiting for transfers between devices, on_device(): across = lax.ppermute(gated, 'half', [(0, 1), (1, 0)])  14.3 us
    ppermute x3, starting transfers between devices, around_y(): down = lax.ppermute(down, 'y', [((i + 1) % 8, i) for i in range(8)])  13.2 us
    ppermute x3, starting transfers between devices, on_device(): lax.ppermute(mine, 'x', [((i + by) % 4, i) for i in range(4)])  11.8 us
    ppermute x4, starting transfers between devices, around_y(): up = lax.ppermute(up, 'y', [(i, (i + 1) % 8) for i in range(8)])  8.94 us
    ppermute x4, waiting for transfers between devices, around_y(): up = lax.ppermute(up, 'y', [(i, (i + 1) % 8) for i in range(8)])  6.85 us
  transfers between devices with their start and end apart: 23, of which 6 were waited for; matrix products, arithmetic and copies ran while one was open for 0% of the time, Pallas kernels for 3%

profile of v1, /device:TPU:1, one launch (start us, length us, event | category | flops | bytes accessed | tf_op | source)
XLA Modules:
  0.0 160.1 jit_solution(11272092968479107825)
XLA Ops:
  0.0 3.6 %local.1 = (bf16[176,512]{1,0:T(8,128)(2,1)}, bf16[256,512]{1,0:T(8,128)(2,1)}, f32[256,512]{1,0:T(8,128)}) custom-call(bf16[3,256,512]{2,1,0:T(8,128)(2,1)} %bitcast.10, bf16[3,7,512]{2,1,0:T(8,128)(2,1)} %bitcast.14), custom_call_target="tpu_custom_call" | custom-call | flops 6000000 | bytes 2000000 | tf_op jit(solution)/shard_map/local/pallas_call | solution.py:193
  3.6 4.5 %collective-permute-start = (bf16[176,512]{1,0:T(8,128)(2,1)}, bf16[176,512]{1,0:T(8,128)(2,1)S(1)}, u32[]{:S(2)}, u32[]{:S(2)}) collective-permute-start(bf16[176,512]{1,0:T(8,128)(2,1)} %get-tuple-element.14), channel_id=1, source_target_pairs={{0,8},{8,16},{16,24},{24,32},{32,40},{40,48},{48,56},{56,64},{64,7... | collective-permute-start | bytes 540680 | tf_op jit(solution)/shard_map/ppermute | solution.py:201
  8.1 0.0 copy-done.17
  8.1 19.1 %collective-permute-start.1 = (bf16[32,512]{1,0:T(8,128)(2,1)S(1)}, bf16[32,512]{1,0:T(8,128)(2,1)S(1)}, u32[]{:S(2)}, u32[]{:S(2)}) collective-permute-start(bf16[32,512]{1,0:T(8,128)(2,1)S(1)} %copy-done.17), channel_id=1, source_target_pairs={{0,64},{64,0},{1,65},{65,1},{2,66},{66,2},{3,67},{67,3},{4,68},{68... | collective-permute-start | bytes 98312 | tf_op jit(solution)/shard_map/ppermute | solution.py:191
  27.2 2.7 %late.1 = (bf16[112,512]{1,0:T(8,128)(2,1)}, f32[256,512]{1,0:T(8,128)}) custom-call(bf16[256,512]{1,0:T(8,128)(2,1)} %get-tuple-element.15.prod, f32[256,512]{1,0:T(8,128)} %get-tuple-element.16.q, bf16[128,512]{1,0:T(8,128)(2,1)} %mf.1, f32[1,512]{1,0:T(1,128)} %bitcast.16, bf16[512,256]{1,0:T(8,128)(2,1)} %constant.26.clone.fwd, ...), custom_call_target="tpu_custom_call" | custom-call | flops 300000000 | bytes 3000000 | tf_op jit(solution)/shard_map/late/pallas_call | solution.py:203
  29.9 0.0 collective-permute-done.1.over
  29.9 0.0 collective-permute-done.halo
  29.9 0.7 copy-done.16
  30.6 4.0 %early.1 = (bf16[256,512]{1,0:T(8,128)(2,1)}, bf16[4,256,512]{2,1,0:T(8,128)(2,1)}) custom-call(bf16[3,256,512]{2,1,0:T(8,128)(2,1)} %bitcast.11, bf16[176,512]{1,0:T(8,128)(2,1)} %copy-done.16, bf16[3,7,512]{2,1,0:T(8,128)(2,1)} %bitcast.15, bf16[256,512]{1,0:T(8,128)(2,1)} %get-tuple-element.15.prod, f32[256,512]{1,0:T(8,128)} %get-tuple-element.16.q, ...), custom_call_target="tpu_custom_call" | custom-call | flops 600000000 | bytes 3000000 | tf_op jit(solution)/shard_map/early/pallas_call | solution.py:217
  34.6 4.4 %all-to-all-start = ((bf16[4,256,512]{2,1,0:T(8,128)(2,1)}), bf16[4,256,512]{2,1,0:T(8,128)(2,1)S(1)}, u32[]{:S(2)}, u32[]{:S(2)}) async-start(bf16[4,256,512]{2,1,0:T(8,128)(2,1)} %get-tuple-element.20), calls=%async_computation | async-start | bytes 2097152 | tf_op jit(solution)/shard_map/all_to_all | solution.py:229
  39.0 5.8 %collective-permute-start.2 = (bf16[256,512]{1,0:T(8,128)(2,1)S(1)}, bf16[256,512]{1,0:T(8,128)(2,1)S(1)}, u32[]{:S(2)}, u32[]{:S(2)}) collective-permute-start(bf16[256,512]{1,0:T(8,128)(2,1)S(1)} %copy-done.22), channel_id=1, source_target_pairs={{0,4},{4,0},{1,5},{5,1},{2,6},{6,2},{3,7},{7,3},{8,12},{12,8},{9,1... | collective-permute-start | bytes 786440 | tf_op jit(solution)/shard_map/ppermute | solution.py:228
  44.8 14.3 %collective-permute-done.2 = bf16[256,512]{1,0:T(8,128)(2,1)S(1)} collective-permute-done((bf16[256,512]{1,0:T(8,128)(2,1)S(1)}, bf16[256,512]{1,0:T(8,128)(2,1)S(1)}, u32[]{:S(2)}, u32[]{:S(2)}) %collective-permute-start.2) | collective-permute-done | bytes 262176 | tf_op jit(solution)/shard_map/ppermute | solution.py:228
  59.1 16.4 %all-to-all-done.near = bf16[4,256,512]{2,1,0:T(8,128)(2,1)S(1)} async-done(((bf16[4,256,512]{2,1,0:T(8,128)(2,1)}), bf16[4,256,512]{2,1,0:T(8,128)(2,1)S(1)}, u32[]{:S(2)}, u32[]{:S(2)}) %all-to-all-start) | async-done | bytes 1048608 | tf_op jit(solution)/shard_map/all_to_all | solution.py:229
  75.5 1.2 broadcast_in_dim.3
  76.7 0.2 copy-done
  76.9 6.1 %all-to-all-start.1 = ((bf16[4,256,512]{2,1,0:T(8,128)(2,1)}), bf16[4,256,512]{2,1,0:T(8,128)(2,1)S(1)}, u32[]{:S(2)}, u32[]{:S(2)}) async-start(bf16[4,256,512]{2,1,0:T(8,128)(2,1)} %broadcast_in_dim.3), calls=%async_computation.1 | async-start | bytes 2097152 | tf_op jit(solution)/shard_map/all_to_all | solution.py:230
  82.9 7.4 %collective-permute-start.3 = (bf16[2,32,512]{2,1,0:T(8,128)(2,1)S(1)}, bf16[2,32,512]{2,1,0:T(8,128)(2,1)S(1)}, u32[]{:S(2)}, u32[]{:S(2)}) collective-permute-start(bf16[2,32,512]{2,1,0:T(8,128)(2,1)S(1)} %pad_maximum_fusion), channel_id=1, source_target_pairs={{16,0},{32,16},{48,32},{0,48},{17,1},{33,17},{49,33},{1,49},{18,2}... | collective-permute-start | bytes 196616 | tf_op jit(solution)/shard_map/ppermute | solution.py:215
  90.3 1.9 %collective-permute-start.4 = (bf16[2,32,512]{2,1,0:T(8,128)(2,1)S(1)}, bf16[2,32,512]{2,1,0:T(8,128)(2,1)S(1)}, u32[]{:S(2)}, u32[]{:S(2)}) collective-permute-start(bf16[2,32,512]{2,1,0:T(8,128)(2,1)S(1)} %pad_maximum_fusion), channel_id=1, source_target_pairs={{32,0},{48,16},{0,32},{16,48},{33,1},{49,17},{1,33},{17,49},{34,2}... | collective-permute-start | bytes 196616 | tf_op jit(solution)/shard_map/ppermute | solution.py:215
  92.2 2.5 %collective-permute-start.5 = (bf16[2,32,512]{2,1,0:T(8,128)(2,1)S(1)}, bf16[2,32,512]{2,1,0:T(8,128)(2,1)S(1)}, u32[]{:S(2)}, u32[]{:S(2)}) collective-permute-start(bf16[2,32,512]{2,1,0:T(8,128)(2,1)S(1)} %pad_maximum_fusion), channel_id=1, source_target_pairs={{48,0},{0,16},{16,32},{32,48},{49,1},{1,17},{17,33},{33,49},{50,2}... | collective-permute-start | bytes 196616 | tf_op jit(solution)/shard_map/ppermute | solution.py:215
  94.8 0.7 stack.32.place
  95.4 0.0 collective-permute-done.3.refs_0_
  95.4 2.2 %collective-permute-done.4.refs_1_ = bf16[2,32,512]{2,1,0:T(8,128)(2,1)S(1)} collective-permute-done((bf16[2,32,512]{2,1,0:T(8,128)(2,1)S(1)}, bf16[2,32,512]{2,1,0:T(8,128)(2,1)S(1)}, u32[]{:S(2)}, u32[]{:S(2)}) %collective-permute-start.4) | collective-permute-done | bytes 65568 | tf_op jit(solution)/shard_map/ppermute | solution.py:215
  97.6 1.6 %collective-permute-done.5.refs_2_ = bf16[2,32,512]{2,1,0:T(8,128)(2,1)S(1)} collective-permute-done((bf16[2,32,512]{2,1,0:T(8,128)(2,1)S(1)}, bf16[2,32,512]{2,1,0:T(8,128)(2,1)S(1)}, u32[]{:S(2)}, u32[]{:S(2)}) %collective-permute-start.5) | collective-permute-done | bytes 65568 | tf_op jit(solution)/shard_map/ppermute | solution.py:215
  99.3 0.0 copy-done.19
  99.3 0.6 copy-done.21
  99.9 1.7 %arrange.1.refs_0_ = bf16[2,4,32,512]{3,2,1,0:T(8,128)(2,1)} custom-call(s32[5]{0:T(128)} %stack.32.place, bf16[32,512]{1,0:T(8,128)(2,1)} %mine.1, bf16[32,512]{1,0:T(8,128)(2,1)} %copy-done.18, bf16[2,32,512]{2,1,0:T(8,128)(2,1)} %copy-done.19, bf16[2,32,512]{2,1,0:T(8,128)(2,1)} %copy-done.20, bf16[2,32,512]{2,1,0:T(8,128)(2,1)} %copy-done.21), custom_call_target="tpu_custom_call" | custom-call | bytes 500000 | tf_op jit(solution)/shard_map/arrange/pallas_call | solution.py:235
  101.6 3.2 %collective-permute-start.13 = (bf16[2,4,32,512]{3,2,1,0:T(8,128)(2,1)}, bf16[2,4,32,512]{3,2,1,0:T(8,128)(2,1)S(1)}, u32[]{:S(2)}, u32[]{:S(2)}) collective-permute-start(bf16[2,4,32,512]{3,2,1,0:T(8,128)(2,1)} %arrange.1.refs_0_), channel_id=1, source_target_pairs={{0,128},{128,256},{256,384},{384,512},{512,640},{640,768},{768,896... | collective-permute-start | bytes 786440 | tf_op jit(solution)/shard_map/ppermute | solution.py:174
  104.8 3.8 %collective-permute-start.7 = (bf16[2,4,32,512]{3,2,1,0:T(8,128)(2,1)}, bf16[2,4,32,512]{3,2,1,0:T(8,128)(2,1)S(1)}, u32[]{:S(2)}, u32[]{:S(2)}) collective-permute-start(bf16[2,4,32,512]{3,2,1,0:T(8,128)(2,1)} %arrange.1.refs_0_), channel_id=1, source_target_pairs={{128,0},{256,128},{384,256},{512,384},{640,512},{768,640},{896,768... | collective-permute-start | bytes 786440 | tf_op jit(solution)/shard_map/ppermute | solution.py:177
  108.6 4.0 %collective-permute-done.13.refs_14_ = bf16[2,4,32,512]{3,2,1,0:T(8,128)(2,1)S(1)} collective-permute-done((bf16[2,4,32,512]{3,2,1,0:T(8,128)(2,1)}, bf16[2,4,32,512]{3,2,1,0:T(8,128)(2,1)S(1)}, u32[]{:S(2)}, u32[]{:S(2)}) %collective-permute-start.13) | collective-permute-done | bytes 262176 | tf_op jit(solution)/shard_map/ppermute | solution.py:174
  112.6 1.9 %collective-permute-start.14 = (bf16[2,4,32,512]{3,2,1,0:T(8,128)(2,1)S(1)}, bf16[2,4,32,512]{3,2,1,0:T(8,128)(2,1)S(1)}, u32[]{:S(2)}, u32[]{:S(2)}) collective-permute-start(bf16[2,4,32,512]{3,2,1,0:T(8,128)(2,1)S(1)} %collective-permute-done.13.refs_14_), channel_id=1, source_target_pairs={{0,128},{128,256},{256,384},{384,512},{512,640},{640,768},{768,896... | collective-permute-start | bytes 786440 | tf_op jit(solution)/shard_map/ppermute | solution.py:174
  114.5 0.0 collective-permute-done.7.refs_2_
  114.5 4.6 %collective-permute-start.9 = (bf16[2,4,32,512]{3,2,1,0:T(8,128)(2,1)S(1)}, bf16[2,4,32,512]{3,2,1,0:T(8,128)(2,1)S(1)}, u32[]{:S(2)}, u32[]{:S(2)}) collective-permute-start(bf16[2,4,32,512]{3,2,1,0:T(8,128)(2,1)S(1)} %collective-permute-done.7.refs_2_), channel_id=1, source_target_pairs={{128,0},{256,128},{384,256},{512,384},{640,512},{768,640},{896,768... | collective-permute-start | bytes 786440 | tf_op jit(solution)/shard_map/ppermute | solution.py:177
  119.1 2.9 %collective-permute-done.14.refs_12_ = bf16[2,4,32,512]{3,2,1,0:T(8,128)(2,1)S(1)} collective-permute-done((bf16[2,4,32,512]{3,2,1,0:T(8,128)(2,1)S(1)}, bf16[2,4,32,512]{3,2,1,0:T(8,128)(2,1)S(1)}, u32[]{:S(2)}, u32[]{:S(2)}) %collective-permute-start.14) | collective-permute-done | bytes 262176 | tf_op jit(solution)/shard_map/ppermute | solution.py:174
  122.0 1.9 %collective-permute-start.15 = (bf16[2,4,32,512]{3,2,1,0:T(8,128)(2,1)S(1)}, bf16[2,4,32,512]{3,2,1,0:T(8,128)(2,1)S(1)}, u32[]{:S(2)}, u32[]{:S(2)}) collective-permute-start(bf16[2,4,32,512]{3,2,1,0:T(8,128)(2,1)S(1)} %collective-permute-done.14.refs_12_), channel_id=1, source_target_pairs={{0,128},{128,256},{256,384},{384,512},{512,640},{640,768},{768,896... | collective-permute-start | bytes 786440 | tf_op jit(solution)/shard_map/ppermute | solution.py:174
  123.9 4.3 %collective-permute-start.6 = (bf16[2,4,32,512]{3,2,1,0:T(8,128)(2,1)}, bf16[2,4,32,512]{3,2,1,0:T(8,128)(2,1)S(1)}, u32[]{:S(2)}, u32[]{:S(2)}) collective-permute-start(bf16[2,4,32,512]{3,2,1,0:T(8,128)(2,1)} %arrange.1.refs_0_), channel_id=1, source_target_pairs={{0,8},{8,0},{1,9},{9,1},{2,10},{10,2},{3,11},{11,3},{4,12},{12,4},... | collective-permute-start | bytes 786440 | tf_op jit(solution)/shard_map/ppermute | solution.py:245
  128.2 1.9 %collective-permute-start.8 = (bf16[2,4,32,512]{3,2,1,0:T(8,128)(2,1)S(1)}, bf16[2,4,32,512]{3,2,1,0:T(8,128)(2,1)S(1)}, u32[]{:S(2)}, u32[]{:S(2)}) collective-permute-start(bf16[2,4,32,512]{3,2,1,0:T(8,128)(2,1)S(1)} %collective-permute-done.7.refs_2_), channel_id=1, source_target_pairs={{0,8},{8,0},{1,9},{9,1},{2,10},{10,2},{3,11},{11,3},{4,12},{12,4},... | collective-permute-start | bytes 786440 | tf_op jit(solution)/shard_map/ppermute | solution.py:245
  130.2 2.4 %collective-permute-start.20 = (bf16[2,4,32,512]{3,2,1,0:T(8,128)(2,1)S(1)}, bf16[2,4,32,512]{3,2,1,0:T(8,128)(2,1)S(1)}, u32[]{:S(2)}, u32[]{:S(2)}) collective-permute-start(bf16[2,4,32,512]{3,2,1,0:T(8,128)(2,1)S(1)} %collective-permute-done.13.refs_14_), channel_id=1, source_target_pairs={{0,8},{8,0},{1,9},{9,1},{2,10},{10,2},{3,11},{11,3},{4,12},{12,4},... | collective-permute-start | bytes 786440 | tf_op jit(solution)/shard_map/ppermute | solution.py:245
  132.6 0.0 collective-permute-done.9.refs_4_
  132.6 4.9 %collective-permute-start.11 = (bf16[2,4,32,512]{3,2,1,0:T(8,128)(2,1)S(1)}, bf16[2,4,32,512]{3,2,1,0:T(8,128)(2,1)S(1)}, u32[]{:S(2)}, u32[]{:S(2)}) collective-permute-start(bf16[2,4,32,512]{3,2,1,0:T(8,128)(2,1)S(1)} %collective-permute-done.9.refs_4_), channel_id=1, source_target_pairs={{128,0},{256,128},{384,256},{512,384},{640,512},{768,640},{896,768... | collective-permute-start | bytes 786440 | tf_op jit(solution)/shard_map/ppermute | solution.py:177
  137.5 0.0 collective-permute-done.15.refs_10_
  137.5 1.9 %collective-permute-start.16 = (bf16[2,4,32,512]{3,2,1,0:T(8,128)(2,1)S(1)}, bf16[2,4,32,512]{3,2,1,0:T(8,128)(2,1)S(1)}, u32[]{:S(2)}, u32[]{:S(2)}) collective-permute-start(bf16[2,4,32,512]{3,2,1,0:T(8,128)(2,1)S(1)} %collective-permute-done.15.refs_10_), channel_id=1, source_target_pairs={{0,128},{128,256},{256,384},{384,512},{512,640},{640,768},{768,896... | collective-permute-start | bytes 786440 | tf_op jit(solution)/shard_map/ppermute | solution.py:174
  139.4 0.0 collective-permute-done.6.refs_1_
  139.4 2.2 %collective-permute-start.10 = (bf16[2,4,32,512]{3,2,1,0:T(8,128)(2,1)S(1)}, bf16[2,4,32,512]{3,2,1,0:T(8,128)(2,1)S(1)}, u32[]{:S(2)}, u32[]{:S(2)}) collective-permute-start(bf16[2,4,32,512]{3,2,1,0:T(8,128)(2,1)S(1)} %collective-permute-done.9.refs_4_), channel_id=1, source_target_pairs={{0,8},{8,0},{1,9},{9,1},{2,10},{10,2},{3,11},{11,3},{4,12},{12,4},... | collective-permute-start | bytes 786440 | tf_op jit(solution)/shard_map/ppermute | solution.py:245
  141.6 0.0 collective-permute-done.8.refs_3_
  141.7 2.1 %collective-permute-start.19 = (bf16[2,4,32,512]{3,2,1,0:T(8,128)(2,1)S(1)}, bf16[2,4,32,512]{3,2,1,0:T(8,128)(2,1)S(1)}, u32[]{:S(2)}, u32[]{:S(2)}) collective-permute-start(bf16[2,4,32,512]{3,2,1,0:T(8,128)(2,1)S(1)} %collective-permute-done.14.refs_12_), channel_id=1, source_target_pairs={{0,8},{8,0},{1,9},{9,1},{2,10},{10,2},{3,11},{11,3},{4,12},{12,4},... | collective-permute-start | bytes 786440 | tf_op jit(solution)/shard_map/ppermute | solution.py:245
  143.8 0.0 collective-permute-done.20.refs_15_
  143.8 2.2 %collective-permute-start.18 = (bf16[2,4,32,512]{3,2,1,0:T(8,128)(2,1)S(1)}, bf16[2,4,32,512]{3,2,1,0:T(8,128)(2,1)S(1)}, u32[]{:S(2)}, u32[]{:S(2)}) collective-permute-start(bf16[2,4,32,512]{3,2,1,0:T(8,128)(2,1)S(1)} %collective-permute-done.15.refs_10_), channel_id=1, source_target_pairs={{0,8},{8,0},{1,9},{9,1},{2,10},{10,2},{3,11},{11,3},{4,12},{12,4},... | collective-permute-start | bytes 786440 | tf_op jit(solution)/shard_map/ppermute | solution.py:245
  146.0 0.0 collective-permute-done.11.refs_6_
  146.1 2.1 %collective-permute-start.12 = (bf16[2,4,32,512]{3,2,1,0:T(8,128)(2,1)S(1)}, bf16[2,4,32,512]{3,2,1,0:T(8,128)(2,1)S(1)}, u32[]{:S(2)}, u32[]{:S(2)}) collective-permute-start(bf16[2,4,32,512]{3,2,1,0:T(8,128)(2,1)S(1)} %collective-permute-done.11.refs_6_), channel_id=1, source_target_pairs={{0,8},{8,0},{1,9},{9,1},{2,10},{10,2},{3,11},{11,3},{4,12},{12,4},... | collective-permute-start | bytes 786440 | tf_op jit(solution)/shard_map/ppermute | solution.py:245
  148.2 0.0 collective-permute-done.16.refs_8_
  148.2 3.0 %collective-permute-start.17 = (bf16[2,4,32,512]{3,2,1,0:T(8,128)(2,1)S(1)}, bf16[2,4,32,512]{3,2,1,0:T(8,128)(2,1)}, u32[]{:S(2)}, u32[]{:S(2)}) collective-permute-start(bf16[2,4,32,512]{3,2,1,0:T(8,128)(2,1)S(1)} %collective-permute-done.16.refs_8_), channel_id=1, source_target_pairs={{0,8},{8,0},{1,9},{9,1},{2,10},{10,2},{3,11},{11,3},{4,12},{12,4},... | collective-permute-start | bytes 786440 | tf_op jit(solution)/shard_map/ppermute | solution.py:245
  151.2 0.0 collective-permute-done.10.refs_5_
  151.2 0.0 collective-permute-done.19.refs_13_
  151.3 0.0 collective-permute-done.12.refs_7_
  151.3 0.0 copy-start.15
  151.3 0.0 collective-permute-done.18.refs_11_
  151.3 0.6 copy-done.12
  151.9 0.1 copy-done.13
  152.0 0.1 copy-done.15
  152.1 0.7 copy-done.14
  152.8 0.0 collective-permute-done.17.refs_9_
  152.8 0.0 all-to-all-done.1.far
  152.9 1.0 copy-done.1
  153.9 6.2 %project.1 = bf16[256,512]{1,0:T(8,128)(2,1)} custom-call(s32[5]{0:T(128)} %stack.32.place, bf16[4,256,512]{2,1,0:T(8,128)(2,1)} %copy-done, bf16[4,256,512]{2,1,0:T(8,128)(2,1)} %copy-done.1, bf16[256,512]{1,0:T(8,128)(2,1)} %residual.1, bf16[2,4,32,512]{3,2,1,0:T(8,128)(2,1)} %arrange.1.refs_0_, bf16[2,4,32,512]{3,2,1,0:T(8,128)(2,1)} %copy-done.7, ...), custom_call_target="tpu_custom_call" | custom-call | flops 1073741824 | bytes 8000000 | tf_op jit(solution)/shard_map/project/pallas_call | solution.py:247
  (36 shorter events, 0.1 us)
Async XLA Ops:
  0.0 8.1 %copy-start.17 = (bf16[32,512]{1,0:T(8,128)(2,1)S(1)}, bf16[32,512]{1,0:T(8,128)(2,1)}, u32[]{:S(2)}) copy-start(bf16[32,512]{1,0:T(8,128)(2,1)} %mine.1) | copy-start | bytes 98308
  3.6 26.3 %collective-permute-start = (bf16[176,512]{1,0:T(8,128)(2,1)}, bf16[176,512]{1,0:T(8,128)(2,1)S(1)}, u32[]{:S(2)}, u32[]{:S(2)}) collective-permute-start(bf16[176,512]{1,0:T(8,128)(2,1)} %get-tuple-element.14), channel_id=1, source_target_pairs={{0,8},{8,16},{16,24},{24,32},{32,40},{40,48},{48,56},{56,64},{64,7... | collective-permute-start | bytes 540680 | tf_op jit(solution)/shard_map/ppermute | solution.py:201
  8.1 21.8 %collective-permute-start.1 = (bf16[32,512]{1,0:T(8,128)(2,1)S(1)}, bf16[32,512]{1,0:T(8,128)(2,1)S(1)}, u32[]{:S(2)}, u32[]{:S(2)}) collective-permute-start(bf16[32,512]{1,0:T(8,128)(2,1)S(1)} %copy-done.17), channel_id=1, source_target_pairs={{0,64},{64,0},{1,65},{65,1},{2,66},{66,2},{3,67},{67,3},{4,68},{68... | collective-permute-start | bytes 98312 | tf_op jit(solution)/shard_map/ppermute | solution.py:191
  29.9 53.1 %copy-start.18 = (bf16[32,512]{1,0:T(8,128)(2,1)}, bf16[32,512]{1,0:T(8,128)(2,1)S(1)}, u32[]{:S(2)}) copy-start(bf16[32,512]{1,0:T(8,128)(2,1)S(1)} %collective-permute-done.1.over) | copy-start | bytes 98308
  29.9 0.7 copy-start.16
  34.6 4.4 %copy-start.22 = (bf16[256,512]{1,0:T(8,128)(2,1)S(1)}, bf16[256,512]{1,0:T(8,128)(2,1)}, u32[]{:S(2)}) copy-start(bf16[256,512]{1,0:T(8,128)(2,1)} %get-tuple-element.21) | copy-start | bytes 786436
  34.6 40.9 %all-to-all-start = ((bf16[4,256,512]{2,1,0:T(8,128)(2,1)}), bf16[4,256,512]{2,1,0:T(8,128)(2,1)S(1)}, u32[]{:S(2)}, u32[]{:S(2)}) async-start(bf16[4,256,512]{2,1,0:T(8,128)(2,1)} %get-tuple-element.20), calls=%async_computation | async-start | bytes 2097152 | tf_op jit(solution)/shard_map/all_to_all | solution.py:229
  39.0 20.1 %collective-permute-start.2 = (bf16[256,512]{1,0:T(8,128)(2,1)S(1)}, bf16[256,512]{1,0:T(8,128)(2,1)S(1)}, u32[]{:S(2)}, u32[]{:S(2)}) collective-permute-start(bf16[256,512]{1,0:T(8,128)(2,1)S(1)} %copy-done.22), channel_id=1, source_target_pairs={{0,4},{4,0},{1,5},{5,1},{2,6},{6,2},{3,7},{7,3},{8,12},{12,8},{9,1... | collective-permute-start | bytes 786440 | tf_op jit(solution)/shard_map/ppermute | solution.py:228
  75.5 1.4 copy-start
  76.9 76.0 %all-to-all-start.1 = ((bf16[4,256,512]{2,1,0:T(8,128)(2,1)}), bf16[4,256,512]{2,1,0:T(8,128)(2,1)S(1)}, u32[]{:S(2)}, u32[]{:S(2)}) async-start(bf16[4,256,512]{2,1,0:T(8,128)(2,1)} %broadcast_in_dim.3), calls=%async_computation.1 | async-start | bytes 2097152 | tf_op jit(solution)/shard_map/all_to_all | solution.py:230
  82.9 12.5 %collective-permute-start.3 = (bf16[2,32,512]{2,1,0:T(8,128)(2,1)S(1)}, bf16[2,32,512]{2,1,0:T(8,128)(2,1)S(1)}, u32[]{:S(2)}, u32[]{:S(2)}) collective-permute-start(bf16[2,32,512]{2,1,0:T(8,128)(2,1)S(1)} %pad_maximum_fusion), channel_id=1, source_target_pairs={{16,0},{32,16},{48,32},{0,48},{17,1},{33,17},{49,33},{1,49},{18,2}... | collective-permute-start | bytes 196616 | tf_op jit(solution)/shard_map/ppermute | solution.py:215
  90.3 7.3 %collective-permute-start.4 = (bf16[2,32,512]{2,1,0:T(8,128)(2,1)S(1)}, bf16[2,32,512]{2,1,0:T(8,128)(2,1)S(1)}, u32[]{:S(2)}, u32[]{:S(2)}) collective-permute-start(bf16[2,32,512]{2,1,0:T(8,128)(2,1)S(1)} %pad_maximum_fusion), channel_id=1, source_target_pairs={{32,0},{48,16},{0,32},{16,48},{33,1},{49,17},{1,33},{17,49},{34,2}... | collective-permute-start | bytes 196616 | tf_op jit(solution)/shard_map/ppermute | solution.py:215
  92.2 7.0 %collective-permute-start.5 = (bf16[2,32,512]{2,1,0:T(8,128)(2,1)S(1)}, bf16[2,32,512]{2,1,0:T(8,128)(2,1)S(1)}, u32[]{:S(2)}, u32[]{:S(2)}) collective-permute-start(bf16[2,32,512]{2,1,0:T(8,128)(2,1)S(1)} %pad_maximum_fusion), channel_id=1, source_target_pairs={{48,0},{0,16},{16,32},{32,48},{49,1},{1,17},{17,33},{33,49},{50,2}... | collective-permute-start | bytes 196616 | tf_op jit(solution)/shard_map/ppermute | solution.py:215
  95.4 3.8 %copy-start.19 = (bf16[2,32,512]{2,1,0:T(8,128)(2,1)}, bf16[2,32,512]{2,1,0:T(8,128)(2,1)S(1)}, u32[]{:S(2)}) copy-start(bf16[2,32,512]{2,1,0:T(8,128)(2,1)S(1)} %collective-permute-done.3.refs_0_) | copy-start | bytes 196612
  97.6 1.6 %copy-start.20 = (bf16[2,32,512]{2,1,0:T(8,128)(2,1)}, bf16[2,32,512]{2,1,0:T(8,128)(2,1)S(1)}, u32[]{:S(2)}) copy-start(bf16[2,32,512]{2,1,0:T(8,128)(2,1)S(1)} %collective-permute-done.4.refs_1_) | copy-start | bytes 196612
  99.3 0.6 copy-start.21
  101.6 11.0 %collective-permute-start.13 = (bf16[2,4,32,512]{3,2,1,0:T(8,128)(2,1)}, bf16[2,4,32,512]{3,2,1,0:T(8,128)(2,1)S(1)}, u32[]{:S(2)}, u32[]{:S(2)}) collective-permute-start(bf16[2,4,32,512]{3,2,1,0:T(8,128)(2,1)} %arrange.1.refs_0_), channel_id=1, source_target_pairs={{0,128},{128,256},{256,384},{384,512},{512,640},{640,768},{768,896... | collective-permute-start | bytes 786440 | tf_op jit(solution)/shard_map/ppermute | solution.py:174
  104.8 9.7 %collective-permute-start.7 = (bf16[2,4,32,512]{3,2,1,0:T(8,128)(2,1)}, bf16[2,4,32,512]{3,2,1,0:T(8,128)(2,1)S(1)}, u32[]{:S(2)}, u32[]{:S(2)}) collective-permute-start(bf16[2,4,32,512]{3,2,1,0:T(8,128)(2,1)} %arrange.1.refs_0_), channel_id=1, source_target_pairs={{128,0},{256,128},{384,256},{512,384},{640,512},{768,640},{896,768... | collective-permute-start | bytes 786440 | tf_op jit(solution)/shard_map/ppermute | solution.py:177
  112.6 40.2 %copy-start.2 = (bf16[2,4,32,512]{3,2,1,0:T(8,128)(2,1)}, bf16[2,4,32,512]{3,2,1,0:T(8,128)(2,1)S(1)}, u32[]{:S(2)}) copy-start(bf16[2,4,32,512]{3,2,1,0:T(8,128)(2,1)S(1)} %collective-permute-done.13.refs_14_) | copy-start | bytes 786436
  112.6 9.4 %collective-permute-start.14 = (bf16[2,4,32,512]{3,2,1,0:T(8,128)(2,1)S(1)}, bf16[2,4,32,512]{3,2,1,0:T(8,128)(2,1)S(1)}, u32[]{:S(2)}, u32[]{:S(2)}) collective-permute-start(bf16[2,4,32,512]{3,2,1,0:T(8,128)(2,1)S(1)} %collective-permute-done.13.refs_14_), channel_id=1, source_target_pairs={{0,128},{128,256},{256,384},{384,512},{512,640},{640,768},{768,896... | collective-permute-start | bytes 786440 | tf_op jit(solution)/shard_map/ppermute | solution.py:174
  114.5 38.3 %copy-start.3 = (bf16[2,4,32,512]{3,2,1,0:T(8,128)(2,1)}, bf16[2,4,32,512]{3,2,1,0:T(8,128)(2,1)S(1)}, u32[]{:S(2)}) copy-start(bf16[2,4,32,512]{3,2,1,0:T(8,128)(2,1)S(1)} %collective-permute-done.7.refs_2_) | copy-start | bytes 786436
  114.5 18.1 %collective-permute-start.9 = (bf16[2,4,32,512]{3,2,1,0:T(8,128)(2,1)S(1)}, bf16[2,4,32,512]{3,2,1,0:T(8,128)(2,1)S(1)}, u32[]{:S(2)}, u32[]{:S(2)}) collective-permute-start(bf16[2,4,32,512]{3,2,1,0:T(8,128)(2,1)S(1)} %collective-permute-done.7.refs_2_), channel_id=1, source_target_pairs={{128,0},{256,128},{384,256},{512,384},{640,512},{768,640},{896,768... | collective-permute-start | bytes 786440 | tf_op jit(solution)/shard_map/ppermute | solution.py:177
  122.0 30.9 %copy-start.4 = (bf16[2,4,32,512]{3,2,1,0:T(8,128)(2,1)}, bf16[2,4,32,512]{3,2,1,0:T(8,128)(2,1)S(1)}, u32[]{:S(2)}) copy-start(bf16[2,4,32,512]{3,2,1,0:T(8,128)(2,1)S(1)} %collective-permute-done.14.refs_12_) | copy-start | bytes 786436
  122.0 15.5 %collective-permute-start.15 = (bf16[2,4,32,512]{3,2,1,0:T(8,128)(2,1)S(1)}, bf16[2,4,32,512]{3,2,1,0:T(8,128)(2,1)S(1)}, u32[]{:S(2)}, u32[]{:S(2)}) collective-permute-start(bf16[2,4,32,512]{3,2,1,0:T(8,128)(2,1)S(1)} %collective-permute-done.14.refs_12_), channel_id=1, source_target_pairs={{0,128},{128,256},{256,384},{384,512},{512,640},{640,768},{768,896... | collective-permute-start | bytes 786440 | tf_op jit(solution)/shard_map/ppermute | solution.py:174
  123.9 15.5 %collective-permute-start.6 = (bf16[2,4,32,512]{3,2,1,0:T(8,128)(2,1)}, bf16[2,4,32,512]{3,2,1,0:T(8,128)(2,1)S(1)}, u32[]{:S(2)}, u32[]{:S(2)}) collective-permute-start(bf16[2,4,32,512]{3,2,1,0:T(8,128)(2,1)} %arrange.1.refs_0_), channel_id=1, source_target_pairs={{0,8},{8,0},{1,9},{9,1},{2,10},{10,2},{3,11},{11,3},{4,12},{12,4},... | collective-permute-start | bytes 786440 | tf_op jit(solution)/shard_map/ppermute | solution.py:245
  128.2 13.4 %collective-permute-start.8 = (bf16[2,4,32,512]{3,2,1,0:T(8,128)(2,1)S(1)}, bf16[2,4,32,512]{3,2,1,0:T(8,128)(2,1)S(1)}, u32[]{:S(2)}, u32[]{:S(2)}) collective-permute-start(bf16[2,4,32,512]{3,2,1,0:T(8,128)(2,1)S(1)} %collective-permute-done.7.refs_2_), channel_id=1, source_target_pairs={{0,8},{8,0},{1,9},{9,1},{2,10},{10,2},{3,11},{11,3},{4,12},{12,4},... | collective-permute-start | bytes 786440 | tf_op jit(solution)/shard_map/ppermute | solution.py:245
  130.2 13.6 %collective-permute-start.20 = (bf16[2,4,32,512]{3,2,1,0:T(8,128)(2,1)S(1)}, bf16[2,4,32,512]{3,2,1,0:T(8,128)(2,1)S(1)}, u32[]{:S(2)}, u32[]{:S(2)}) collective-permute-start(bf16[2,4,32,512]{3,2,1,0:T(8,128)(2,1)S(1)} %collective-permute-done.13.refs_14_), channel_id=1, source_target_pairs={{0,8},{8,0},{1,9},{9,1},{2,10},{10,2},{3,11},{11,3},{4,12},{12,4},... | collective-permute-start | bytes 786440 | tf_op jit(solution)/shard_map/ppermute | solution.py:245
  132.6 20.3 %copy-start.5 = (bf16[2,4,32,512]{3,2,1,0:T(8,128)(2,1)}, bf16[2,4,32,512]{3,2,1,0:T(8,128)(2,1)S(1)}, u32[]{:S(2)}) copy-start(bf16[2,4,32,512]{3,2,1,0:T(8,128)(2,1)S(1)} %collective-permute-done.9.refs_4_) | copy-start | bytes 786436
  132.6 13.4 %collective-permute-start.11 = (bf16[2,4,32,512]{3,2,1,0:T(8,128)(2,1)S(1)}, bf16[2,4,32,512]{3,2,1,0:T(8,128)(2,1)S(1)}, u32[]{:S(2)}, u32[]{:S(2)}) collective-permute-start(bf16[2,4,32,512]{3,2,1,0:T(8,128)(2,1)S(1)} %collective-permute-done.9.refs_4_), channel_id=1, source_target_pairs={{128,0},{256,128},{384,256},{512,384},{640,512},{768,640},{896,768... | collective-permute-start | bytes 786440 | tf_op jit(solution)/shard_map/ppermute | solution.py:177
  137.5 15.4 %copy-start.6 = (bf16[2,4,32,512]{3,2,1,0:T(8,128)(2,1)}, bf16[2,4,32,512]{3,2,1,0:T(8,128)(2,1)S(1)}, u32[]{:S(2)}) copy-start(bf16[2,4,32,512]{3,2,1,0:T(8,128)(2,1)S(1)} %collective-permute-done.15.refs_10_) | copy-start | bytes 786436
  137.5 10.7 %collective-permute-start.16 = (bf16[2,4,32,512]{3,2,1,0:T(8,128)(2,1)S(1)}, bf16[2,4,32,512]{3,2,1,0:T(8,128)(2,1)S(1)}, u32[]{:S(2)}, u32[]{:S(2)}) collective-permute-start(bf16[2,4,32,512]{3,2,1,0:T(8,128)(2,1)S(1)} %collective-permute-done.15.refs_10_), channel_id=1, source_target_pairs={{0,128},{128,256},{256,384},{384,512},{512,640},{640,768},{768,896... | collective-permute-start | bytes 786440 | tf_op jit(solution)/shard_map/ppermute | solution.py:174
  139.4 13.5 %copy-start.7 = (bf16[2,4,32,512]{3,2,1,0:T(8,128)(2,1)}, bf16[2,4,32,512]{3,2,1,0:T(8,128)(2,1)S(1)}, u32[]{:S(2)}) copy-start(bf16[2,4,32,512]{3,2,1,0:T(8,128)(2,1)S(1)} %collective-permute-done.6.refs_1_) | copy-start | bytes 786436
  139.4 11.8 %collective-permute-start.10 = (bf16[2,4,32,512]{3,2,1,0:T(8,128)(2,1)S(1)}, bf16[2,4,32,512]{3,2,1,0:T(8,128)(2,1)S(1)}, u32[]{:S(2)}, u32[]{:S(2)}) collective-permute-start(bf16[2,4,32,512]{3,2,1,0:T(8,128)(2,1)S(1)} %collective-permute-done.9.refs_4_), channel_id=1, source_target_pairs={{0,8},{8,0},{1,9},{9,1},{2,10},{10,2},{3,11},{11,3},{4,12},{12,4},... | collective-permute-start | bytes 786440 | tf_op jit(solution)/shard_map/ppermute | solution.py:245
  141.7 11.2 %copy-start.8 = (bf16[2,4,32,512]{3,2,1,0:T(8,128)(2,1)}, bf16[2,4,32,512]{3,2,1,0:T(8,128)(2,1)S(1)}, u32[]{:S(2)}) copy-start(bf16[2,4,32,512]{3,2,1,0:T(8,128)(2,1)S(1)} %collective-permute-done.8.refs_3_) | copy-start | bytes 786436
  141.7 9.6 %collective-permute-start.19 = (bf16[2,4,32,512]{3,2,1,0:T(8,128)(2,1)S(1)}, bf16[2,4,32,512]{3,2,1,0:T(8,128)(2,1)S(1)}, u32[]{:S(2)}, u32[]{:S(2)}) collective-permute-start(bf16[2,4,32,512]{3,2,1,0:T(8,128)(2,1)S(1)} %collective-permute-done.14.refs_12_), channel_id=1, source_target_pairs={{0,8},{8,0},{1,9},{9,1},{2,10},{10,2},{3,11},{11,3},{4,12},{12,4},... | collective-permute-start | bytes 786440 | tf_op jit(solution)/shard_map/ppermute | solution.py:245
  143.8 9.1 %copy-start.9 = (bf16[2,4,32,512]{3,2,1,0:T(8,128)(2,1)}, bf16[2,4,32,512]{3,2,1,0:T(8,128)(2,1)S(1)}, u32[]{:S(2)}) copy-start(bf16[2,4,32,512]{3,2,1,0:T(8,128)(2,1)S(1)} %collective-permute-done.20.refs_15_) | copy-start | bytes 786436
  143.8 7.5 %collective-permute-start.18 = (bf16[2,4,32,512]{3,2,1,0:T(8,128)(2,1)S(1)}, bf16[2,4,32,512]{3,2,1,0:T(8,128)(2,1)S(1)}, u32[]{:S(2)}, u32[]{:S(2)}) collective-permute-start(bf16[2,4,32,512]{3,2,1,0:T(8,128)(2,1)S(1)} %collective-permute-done.15.refs_10_), channel_id=1, source_target_pairs={{0,8},{8,0},{1,9},{9,1},{2,10},{10,2},{3,11},{11,3},{4,12},{12,4},... | collective-permute-start | bytes 786440 | tf_op jit(solution)/shard_map/ppermute | solution.py:245
  146.0 6.9 %copy-start.10 = (bf16[2,4,32,512]{3,2,1,0:T(8,128)(2,1)}, bf16[2,4,32,512]{3,2,1,0:T(8,128)(2,1)S(1)}, u32[]{:S(2)}) copy-start(bf16[2,4,32,512]{3,2,1,0:T(8,128)(2,1)S(1)} %collective-permute-done.11.refs_6_) | copy-start | bytes 786436
  146.1 5.2 %collective-permute-start.12 = (bf16[2,4,32,512]{3,2,1,0:T(8,128)(2,1)S(1)}, bf16[2,4,32,512]{3,2,1,0:T(8,128)(2,1)S(1)}, u32[]{:S(2)}, u32[]{:S(2)}) collective-permute-start(bf16[2,4,32,512]{3,2,1,0:T(8,128)(2,1)S(1)} %collective-permute-done.11.refs_6_), channel_id=1, source_target_pairs={{0,8},{8,0},{1,9},{9,1},{2,10},{10,2},{3,11},{11,3},{4,12},{12,4},... | collective-permute-start | bytes 786440 | tf_op jit(solution)/shard_map/ppermute | solution.py:245
  148.2 3.1 %copy-start.11 = (bf16[2,4,32,512]{3,2,1,0:T(8,128)(2,1)}, bf16[2,4,32,512]{3,2,1,0:T(8,128)(2,1)S(1)}, u32[]{:S(2)}) copy-start(bf16[2,4,32,512]{3,2,1,0:T(8,128)(2,1)S(1)} %collective-permute-done.16.refs_8_) | copy-start | bytes 786436
  148.2 4.6 %collective-permute-start.17 = (bf16[2,4,32,512]{3,2,1,0:T(8,128)(2,1)S(1)}, bf16[2,4,32,512]{3,2,1,0:T(8,128)(2,1)}, u32[]{:S(2)}, u32[]{:S(2)}) collective-permute-start(bf16[2,4,32,512]{3,2,1,0:T(8,128)(2,1)S(1)} %collective-permute-done.16.refs_8_), channel_id=1, source_target_pairs={{0,8},{8,0},{1,9},{9,1},{2,10},{10,2},{3,11},{11,3},{4,12},{12,4},... | collective-permute-start | bytes 786440 | tf_op jit(solution)/shard_map/ppermute | solution.py:245
  151.2 0.7 copy-start.12
  151.3 0.8 copy-start.13
  151.3 0.8 copy-start.15
  152.1 0.7 copy-start.14
  152.9 1.0 copy-start.1

commit v2 on v1

--- a/solution.py
+++ b/solution.py
@@ -97,7 +97,7 @@
     out[...] = (q[pl.ds(HEAD, rows), :] * filtered).astype(BF16)
 
 
-def early_kernel(p, halo, sf, prod, q, late, spec, skip, fwd, inv, one, out, ext, win):
+def early_kernel(p, halo, sf, prod, q, late, spec, skip, fwd, inv, out, ext, win):
     filt = sf[...].astype(F32)
     mixed = []
     for c in range(3):
@@ -121,10 +121,7 @@
         (HEAD, late.shape[0], late[...]),
     ]
     for at, count, value in pieces:
-        value = value.astype(BF16)
-        one[pl.ds(at, count), :] = value
-        for i in range(out.shape[0]):
-            out[i, pl.ds(at, count), :] = value
+        out[pl.ds(at, count), :] = value.astype(BF16)
 
 
 def arrange_kernel(place, mine, over, *refs):
@@ -136,26 +133,45 @@
             out[lax.rem(zh + other, 2), lax.rem(x + rel, 4)] = piece
 
 
-def final_kernel(place, near, far, residual, *refs):
-    weights, (out, gv, wv, gsem, wsem) = refs[:16], refs[16:]
-    half, y, core = place[0], place[2], place[4]
+ORDER = ((0, 7, 1), (6, 2), (5, 3, 4))
+
+
+def final_kernel(place, own, four, two, six, odd, seven, residual, *refs):
+    weights, swapped = refs[:8], refs[8:11]
+    out, gv, wv, gsem, wsem = refs[11:]
+    me, y, core = place[0], place[2], place[4]
+    pieces = [(own, 0), (four, 4), (two, 2), (six, 6), (seven, 7)]
+    pieces += [(odd.at[i], by) for i, by in enumerate((1, 5, 3))]
     gated = [
-        pltpu.make_async_copy(near, gv.at[pl.ds(4 * half, 4)], gsem.at[0]),
-        pltpu.make_async_copy(far, gv.at[pl.ds(4 * (1 - half), 4)], gsem.at[1]),
+        pltpu.make_async_copy(piece, gv.at[lax.bitwise_xor(me, by)], gsem.at[by])
+        for piece, by in pieces
     ]
     rows = []
-    for i, weight in enumerate(weights):
-        target = wv.at[lax.rem(y + i // 2, 8), :, :, lax.rem(core + i % 2, 2)]
-        rows.append(pltpu.make_async_copy(weight, target, wsem.at[i]))
-    for copy in gated + rows:
+    for batch, order in enumerate(ORDER):
+        for i, by in enumerate(order):
+            at = lax.rem(y + by, 8)
+            rows.append(
+                [
+                    pltpu.make_async_copy(
+                        weights[by], wv.at[at, :, :, core], wsem.at[by, 0]
+                    ),
+                    pltpu.make_async_copy(
+                        swapped[batch].at[i], wv.at[at, :, :, 1 - core], wsem.at[by, 1]
+                    ),
+                ]
+            )
+    for copy in gated:
         copy.start()
+    for pair in rows:
+        for copy in pair:
+            copy.start()
     total = residual[...].astype(F32)
     for copy in gated:
         copy.wait()
-    for i in range(8):
-        rows[2 * i].wait()
-        rows[2 * i + 1].wait()
-        k = lax.rem(y + i, 8)
+    for by, pair in zip(sum(ORDER, ()), rows):
+        for copy in pair:
+            copy.wait()
+        k = lax.rem(y + by, 8)
         total = total + dot(gv[k], wv[k].reshape(512, 512))
     out[...] = total.astype(BF16)
 
@@ -185,7 +201,7 @@
     p = jnp.transpose(proj, (1, 0, 2))
     sf = jnp.transpose(short_filter, (1, 0, 2))
     skip = skip.reshape(1, chans)
-    place = jnp.stack([lax.axis_index(a) for a in ("half", "zh", "y", "x", "core")])
+    place = jnp.stack([lax.axis_index(a) for a in ("tp", "zh", "y", "x", "core")])
     place = place.astype(jnp.int32)
 
     over = lax.ppermute(out_weight, "zh", [(0, 1), (1, 0)])
@@ -214,9 +230,9 @@
     for by in (1, 2, 3):
         arrived.append(lax.ppermute(mine, "x", [((i + by) % 4, i) for i in range(4)]))
 
-    gated, copies = pl.pallas_call(
+    gated = pl.pallas_call(
         early_kernel,
-        out_shape=(sds((rows, chans), BF16), sds((4, rows, chans), BF16)),
+        out_shape=sds((rows, chans), BF16),
         scratch_shapes=[
             pltpu.VMEM((3, 2 * TAIL, chans), F32),
             pltpu.VMEM((HALF + SPAN, chans), BF16),
@@ -225,9 +241,14 @@
         name="early",
     )(p, halo, sf, prod, q, late, spec, skip, fwd, inv)
 
-    across = lax.ppermute(gated, "half", [(0, 1), (1, 0)])
-    near = lax.all_to_all(copies, "quarter", 0, 0)
-    far = lax.all_to_all(jnp.broadcast_to(across, (4, rows, chans)), "quarter", 0, 0)
+    def exchange(piece, by):
+        return lax.ppermute(piece, "tp", [(i, i ^ by) for i in range(8)])
+
+    four = exchange(gated, 4)
+    two = exchange(gated, 2)
+    six = exchange(four, 2)
+    odd = exchange(jnp.stack([gated, four, two]), 1)
+    seven = exchange(six, 1)
 
     smem = pl.BlockSpec(memory_space=pltpu.SMEM)
     vmem = pl.BlockSpec(memory_space=pltpu.VMEM)
@@ -240,31 +261,33 @@
         cost_estimate=cost(0, 500_000),
         name="arrange",
     )(place, out_weight, over, *arrived)
-    weights = []
-    for own in around_y(block):
-        weights += [own, lax.ppermute(own, "core", [(0, 1), (1, 0)])]
+    weights = around_y(block)
+    swapped = []
+    for order in ORDER:
+        group = jnp.stack([weights[by] for by in order])
+        swapped.append(lax.ppermute(group, "core", [(0, 1), (1, 0)]))
 
     return pl.pallas_call(
         final_kernel,
         out_shape=sds((rows, chans), BF16),
-        in_specs=[smem, anywhere, anywhere, vmem] + [anywhere] * 16,
+        in_specs=[smem] + [anywhere] * 6 + [vmem] + [anywhere] * 11,
         out_specs=vmem,
         scratch_shapes=[
             pltpu.VMEM((8, rows, chans), BF16),
             pltpu.VMEM((8, 2, 4, 2, WROWS, chans), BF16),
-            pltpu.SemaphoreType.DMA((2,)),
-            pltpu.SemaphoreType.DMA((16,)),
+            pltpu.SemaphoreType.DMA((8,)),
+            pltpu.SemaphoreType.DMA((8, 2)),
         ],
         cost_estimate=cost(2 * rows * 8 * chans * chans, 8_000_000),
         name="project",
-    )(place, near, far, residual, *weights)
+    )(place, gated, four, two, six, odd, seven, residual, *weights, *swapped)
 
 
 def solution(mesh):
-    devices = np.asarray(mesh.devices).reshape(8, 2, 4, 2, 2, 4)
-    fine = Mesh(devices, ("y", "zh", "x", "core", "half", "quarter"))
+    devices = np.asarray(mesh.devices).reshape(8, 2, 4, 2, 8)
+    fine = Mesh(devices, ("y", "zh", "x", "core", "tp"))
     ctx = ("y", "zh", "x", "core")
-    tp = ("half", "quarter")
+    tp = "tp"
     in_specs = (
         P(ctx, tp),
         P(ctx, None, tp),

time: 162 us -> 152 us (0.938)
  waiting for transfers between devices: 41.4 us -> 25.3 us
  starting transfers between devices: 94.1 us -> 98.9 us
    ppermute x9 -> x8, starting transfers between devices: 26.1 us -> 43.8 us  [the longest x3 26.6 us: on_device(): swapped.append(lax.ppermute(group, 'core', [(0, 1), (1, 0)]))]
    all_to_all x2 -> x0, waiting for transfers between devices: 16.4 us -> none  [the longest x1 16.4 us: on_device(): near = lax.all_to_all(copies, 'quarter', 0, 0)]
    all_to_all x2 -> x0, starting transfers between devices: 10.5 us -> none  [the longest x1 6.06 us: on_device(): lax.all_to_all(jnp.broadcast_to(across, (4, rows, chans)), 'quarter', 0, 0)]
    ppermute x9 -> x8, waiting for transfers between devices: 14.3 us -> 19.2 us  [the longest x5 19.2 us: exchange(): return lax.ppermute(piece, 'tp', [(i, i ^ by) for i in range(8)])]
    ppermute x4, waiting for transfers between devices: 6.85 us -> 2.66 us  [around_y(): up = lax.ppermute(up, 'y', [(i, (i + 1) % 8) for i in range(8)])]
    ppermute x3, starting transfers between devices: 11.8 us -> 9.31 us  [on_device(): lax.ppermute(mine, 'x', [((i + by) % 4, i) for i in range(4)])]
  transfers between devices with their start and end apart: 23 -> 20, of which waited for: 6 -> 5; matrix products, arithmetic and copies ran while one was open for 0% -> 1% of each run, Pallas kernels for 3% -> 7%
where the time goes in v2:
time: 152 us; the launch traced here: 148 us
  starting transfers between devices  98.9 us (65%)
  waiting for transfers between devices  25.3 us (17%)
  Pallas kernels  17.8 us (12%)
  local copies, waits for them, and re-layouts  5.64 us (4%)
    ppermute x3, starting transfers between devices, on_device(): swapped.append(lax.ppermute(group, 'core', [(0, 1), (1, 0)]))  26.6 us
    ppermute x1, starting transfers between devices, on_device(): over = lax.ppermute(out_weight, 'zh', [(0, 1), (1, 0)])  19.9 us
    ppermute x5, waiting for transfers between devices, exchange(): return lax.ppermute(piece, 'tp', [(i, i ^ by) for i in range(8)])  19.2 us
    ppermute x5, starting transfers between devices, exchange(): return lax.ppermute(piece, 'tp', [(i, i ^ by) for i in range(8)])  17.2 us
    ppermute x3, starting transfers between devices, around_y(): down = lax.ppermute(down, 'y', [((i + 1) % 8, i) for i in range(8)])  13.1 us
    ppermute x3, starting transfers between devices, on_device(): lax.ppermute(mine, 'x', [((i + by) % 4, i) for i in range(4)])  9.31 us
    ppermute x4, starting transfers between devices, around_y(): up = lax.ppermute(up, 'y', [(i, (i + 1) % 8) for i in range(8)])  8.94 us
    pallas_call x1, Pallas kernels, on_device(): pl.pallas_call(final_kernel, out_shape=sds((rows, chans), BF16), in_specs...  6.19 us
  transfers between devices with their start and end apart: 20, of which 5 were waited for; matrix products, arithmetic and copies ran while one was open for 1% of the time, Pallas kernels for 7%

profile of v2, /device:TPU:1, one launch (start us, length us, event | category | flops | bytes accessed | tf_op | source)
XLA Modules:
  0.0 148.5 jit_solution(13846034261352736322)
XLA Ops:
  0.0 19.9 %collective-permute-start.1 = (bf16[32,512]{1,0:T(8,128)(2,1)}, bf16[32,512]{1,0:T(8,128)(2,1)S(1)}, u32[]{:S(2)}, u32[]{:S(2)}) collective-permute-start(bf16[32,512]{1,0:T(8,128)(2,1)} %mine.1), channel_id=1, source_target_pairs={{0,64},{64,0},{1,65},{65,1},{2,66},{66,2},{3,67},{67,3},{4,68},{68... | collective-permute-start | bytes 98312 | tf_op jit(solution)/shard_map/ppermute | solution.py:207
  19.9 3.6 %local.1 = (bf16[176,512]{1,0:T(8,128)(2,1)}, bf16[256,512]{1,0:T(8,128)(2,1)}, f32[256,512]{1,0:T(8,128)}) custom-call(bf16[3,256,512]{2,1,0:T(8,128)(2,1)} %bitcast.21, bf16[3,7,512]{2,1,0:T(8,128)(2,1)} %bitcast.36), custom_call_target="tpu_custom_call" | custom-call | flops 6000000 | bytes 2000000 | tf_op jit(solution)/shard_map/local/pallas_call | solution.py:209
  23.5 2.7 %late.1 = (bf16[112,512]{1,0:T(8,128)(2,1)}, f32[256,512]{1,0:T(8,128)}) custom-call(bf16[256,512]{1,0:T(8,128)(2,1)} %get-tuple-element.13.prod, f32[256,512]{1,0:T(8,128)} %get-tuple-element.14.q, bf16[128,512]{1,0:T(8,128)(2,1)} %mf.1, f32[1,512]{1,0:T(1,128)} %bitcast.38, bf16[512,256]{1,0:T(8,128)(2,1)} %constant.25.clone.fwd, ...), custom_call_target="tpu_custom_call" | custom-call | flops 300000000 | bytes 3000000 | tf_op jit(solution)/shard_map/late/pallas_call | solution.py:219
  26.2 0.0 collective-permute-done.1.over
  26.2 0.0 copy-done.17
  26.2 0.6 copy-done.18
  26.8 4.4 %collective-permute-start.7 = (bf16[2,32,512]{2,1,0:T(8,128)(2,1)S(1)}, bf16[2,32,512]{2,1,0:T(8,128)(2,1)S(1)}, u32[]{:S(2)}, u32[]{:S(2)}) collective-permute-start(bf16[2,32,512]{2,1,0:T(8,128)(2,1)S(1)} %pad_maximum_fusion.4), channel_id=1, source_target_pairs={{16,0},{32,16},{48,32},{0,48},{17,1},{33,17},{49,33},{1,49},{18,2}... | collective-permute-start | bytes 196616 | tf_op jit(solution)/shard_map/ppermute | solution.py:231
  31.2 2.4 %collective-permute-start.8 = (bf16[2,32,512]{2,1,0:T(8,128)(2,1)S(1)}, bf16[2,32,512]{2,1,0:T(8,128)(2,1)S(1)}, u32[]{:S(2)}, u32[]{:S(2)}) collective-permute-start(bf16[2,32,512]{2,1,0:T(8,128)(2,1)S(1)} %pad_maximum_fusion.4), channel_id=1, source_target_pairs={{32,0},{48,16},{0,32},{16,48},{33,1},{49,17},{1,33},{17,49},{34,2}... | collective-permute-start | bytes 196616 | tf_op jit(solution)/shard_map/ppermute | solution.py:231
  33.6 2.5 %collective-permute-start.9 = (bf16[2,32,512]{2,1,0:T(8,128)(2,1)S(1)}, bf16[2,32,512]{2,1,0:T(8,128)(2,1)S(1)}, u32[]{:S(2)}, u32[]{:S(2)}) collective-permute-start(bf16[2,32,512]{2,1,0:T(8,128)(2,1)S(1)} %pad_maximum_fusion.4), channel_id=1, source_target_pairs={{48,0},{0,16},{16,32},{32,48},{49,1},{1,17},{17,33},{33,49},{50,2}... | collective-permute-start | bytes 196616 | tf_op jit(solution)/shard_map/ppermute | solution.py:231
  36.1 0.6 stack.77.place
  36.8 0.0 collective-permute-done.7.refs_0_
  36.8 0.9 collective-permute-done.8.refs_1_
  37.7 2.5 %collective-permute-done.9.refs_2_ = bf16[2,32,512]{2,1,0:T(8,128)(2,1)S(1)} collective-permute-done((bf16[2,32,512]{2,1,0:T(8,128)(2,1)S(1)}, bf16[2,32,512]{2,1,0:T(8,128)(2,1)S(1)}, u32[]{:S(2)}, u32[]{:S(2)}) %collective-permute-start.9) | collective-permute-done | bytes 65568 | tf_op jit(solution)/shard_map/ppermute | solution.py:231
  40.2 0.6 copy-done.21
  40.8 1.7 %arrange.1.refs_0_ = bf16[2,4,32,512]{3,2,1,0:T(8,128)(2,1)} custom-call(s32[5]{0:T(128)} %stack.77.place, bf16[32,512]{1,0:T(8,128)(2,1)} %mine.1, bf16[32,512]{1,0:T(8,128)(2,1)} %copy-done.18, bf16[2,32,512]{2,1,0:T(8,128)(2,1)} %copy-done.19, bf16[2,32,512]{2,1,0:T(8,128)(2,1)} %copy-done.20, bf16[2,32,512]{2,1,0:T(8,128)(2,1)} %copy-done.21), custom_call_target="tpu_custom_call" | custom-call | bytes 500000 | tf_op jit(solution)/shard_map/arrange/pallas_call | solution.py:256
  42.5 3.2 %collective-permute-start.13 = (bf16[2,4,32,512]{3,2,1,0:T(8,128)(2,1)}, bf16[2,4,32,512]{3,2,1,0:T(8,128)(2,1)S(1)}, u32[]{:S(2)}, u32[]{:S(2)}) collective-permute-start(bf16[2,4,32,512]{3,2,1,0:T(8,128)(2,1)} %arrange.1.refs_0_), channel_id=1, source_target_pairs={{0,128},{128,256},{256,384},{384,512},{512,640},{640,768},{768,896... | collective-permute-start | bytes 786440 | tf_op jit(solution)/shard_map/ppermute | solution.py:190
  45.7 3.8 %collective-permute-start.10 = (bf16[2,4,32,512]{3,2,1,0:T(8,128)(2,1)}, bf16[2,4,32,512]{3,2,1,0:T(8,128)(2,1)S(1)}, u32[]{:S(2)}, u32[]{:S(2)}) collective-permute-start(bf16[2,4,32,512]{3,2,1,0:T(8,128)(2,1)} %arrange.1.refs_0_), channel_id=1, source_target_pairs={{128,0},{256,128},{384,256},{512,384},{640,512},{768,640},{896,768... | collective-permute-start | bytes 786440 | tf_op jit(solution)/shard_map/ppermute | solution.py:193
  49.5 2.7 %collective-permute-done.13.refs_7_ = bf16[2,4,32,512]{3,2,1,0:T(8,128)(2,1)S(1)} collective-permute-done((bf16[2,4,32,512]{3,2,1,0:T(8,128)(2,1)}, bf16[2,4,32,512]{3,2,1,0:T(8,128)(2,1)S(1)}, u32[]{:S(2)}, u32[]{:S(2)}) %collective-permute-start.13) | collective-permute-done | bytes 262176 | tf_op jit(solution)/shard_map/ppermute | solution.py:190
  52.2 1.9 %collective-permute-start.14 = (bf16[2,4,32,512]{3,2,1,0:T(8,128)(2,1)S(1)}, bf16[2,4,32,512]{3,2,1,0:T(8,128)(2,1)S(1)}, u32[]{:S(2)}, u32[]{:S(2)}) collective-permute-start(bf16[2,4,32,512]{3,2,1,0:T(8,128)(2,1)S(1)} %collective-permute-done.13.refs_7_), channel_id=1, source_target_pairs={{0,128},{128,256},{256,384},{384,512},{512,640},{640,768},{768,896... | collective-permute-start | bytes 786440 | tf_op jit(solution)/shard_map/ppermute | solution.py:190
  54.1 3.8 %collective-permute-start = (bf16[176,512]{1,0:T(8,128)(2,1)S(1)}, bf16[176,512]{1,0:T(8,128)(2,1)S(1)}, u32[]{:S(2)}, u32[]{:S(2)}) collective-permute-start(bf16[176,512]{1,0:T(8,128)(2,1)S(1)} %copy-done.22), channel_id=1, source_target_pairs={{0,8},{8,16},{16,24},{24,32},{32,40},{40,48},{48,56},{56,64},{64,7... | collective-permute-start | bytes 540680 | tf_op jit(solution)/shard_map/ppermute | solution.py:217
  58.0 0.0 collective-permute-done.10.refs_1_
  58.0 4.7 %collective-permute-start.11 = (bf16[2,4,32,512]{3,2,1,0:T(8,128)(2,1)S(1)}, bf16[2,4,32,512]{3,2,1,0:T(8,128)(2,1)S(1)}, u32[]{:S(2)}, u32[]{:S(2)}) collective-permute-start(bf16[2,4,32,512]{3,2,1,0:T(8,128)(2,1)S(1)} %collective-permute-done.10.refs_1_), channel_id=1, source_target_pairs={{128,0},{256,128},{384,256},{512,384},{640,512},{768,640},{896,768... | collective-permute-start | bytes 786440 | tf_op jit(solution)/shard_map/ppermute | solution.py:193
  62.7 0.0 collective-permute-done.14.refs_6_
  62.8 1.9 %collective-permute-start.15 = (bf16[2,4,32,512]{3,2,1,0:T(8,128)(2,1)S(1)}, bf16[2,4,32,512]{3,2,1,0:T(8,128)(2,1)S(1)}, u32[]{:S(2)}, u32[]{:S(2)}) collective-permute-start(bf16[2,4,32,512]{3,2,1,0:T(8,128)(2,1)S(1)} %collective-permute-done.14.refs_6_), channel_id=1, source_target_pairs={{0,128},{128,256},{256,384},{384,512},{512,640},{640,768},{768,896... | collective-permute-start | bytes 786440 | tf_op jit(solution)/shard_map/ppermute | solution.py:190
  64.7 0.0 collective-permute-done.halo
  64.7 0.7 copy-done.16
  65.4 3.7 %early.1.own = bf16[256,512]{1,0:T(8,128)(2,1)} custom-call(bf16[3,256,512]{2,1,0:T(8,128)(2,1)} %bitcast.22, bf16[176,512]{1,0:T(8,128)(2,1)} %copy-done.16, bf16[3,7,512]{2,1,0:T(8,128)(2,1)} %bitcast.37, bf16[256,512]{1,0:T(8,128)(2,1)} %get-tuple-element.13.prod, f32[256,512]{1,0:T(8,128)} %get-tuple-element.14.q, ...), custom_call_target="tpu_custom_call" | custom-call | flops 600000000 | bytes 3000000 | tf_op jit(solution)/shard_map/early/pallas_call | solution.py:233
  69.0 5.8 %collective-permute-start.2 = (bf16[256,512]{1,0:T(8,128)(2,1)}, bf16[256,512]{1,0:T(8,128)(2,1)S(1)}, u32[]{:S(2)}, u32[]{:S(2)}) collective-permute-start(bf16[256,512]{1,0:T(8,128)(2,1)} %early.1.own), channel_id=1, source_target_pairs={{0,4},{1,5},{2,6},{3,7},{4,0},{5,1},{6,2},{7,3},{8,12},{9,13},{10,... | collective-permute-start | bytes 786440 | tf_op jit(solution)/shard_map/ppermute | solution.py:245
  74.9 4.0 %collective-permute-start.3 = (bf16[256,512]{1,0:T(8,128)(2,1)}, bf16[256,512]{1,0:T(8,128)(2,1)S(1)}, u32[]{:S(2)}, u32[]{:S(2)}) collective-permute-start(bf16[256,512]{1,0:T(8,128)(2,1)} %early.1.own), channel_id=1, source_target_pairs={{0,2},{1,3},{2,0},{3,1},{4,6},{5,7},{6,4},{7,5},{8,10},{9,11},{10,... | collective-permute-start | bytes 786440 | tf_op jit(solution)/shard_map/ppermute | solution.py:245
  78.9 0.0 collective-permute-done.11.refs_2_
  78.9 4.6 %collective-permute-start.12 = (bf16[2,4,32,512]{3,2,1,0:T(8,128)(2,1)S(1)}, bf16[2,4,32,512]{3,2,1,0:T(8,128)(2,1)S(1)}, u32[]{:S(2)}, u32[]{:S(2)}) collective-permute-start(bf16[2,4,32,512]{3,2,1,0:T(8,128)(2,1)S(1)} %collective-permute-done.11.refs_2_), channel_id=1, source_target_pairs={{128,0},{256,128},{384,256},{512,384},{640,512},{768,640},{896,768... | collective-permute-start | bytes 786440 | tf_op jit(solution)/shard_map/ppermute | solution.py:193
  83.5 0.0 collective-permute-done.15.refs_5_
  83.5 0.0 copy-start.6
  83.5 1.9 %collective-permute-start.16 = (bf16[2,4,32,512]{3,2,1,0:T(8,128)(2,1)S(1)}, bf16[2,4,32,512]{3,2,1,0:T(8,128)(2,1)S(1)}, u32[]{:S(2)}, u32[]{:S(2)}) collective-permute-start(bf16[2,4,32,512]{3,2,1,0:T(8,128)(2,1)S(1)} %collective-permute-done.15.refs_5_), channel_id=1, source_target_pairs={{0,128},{128,256},{256,384},{384,512},{512,640},{640,768},{768,896... | collective-permute-start | bytes 786440 | tf_op jit(solution)/shard_map/ppermute | solution.py:190
  85.4 0.0 copy-done.2
  85.4 0.0 copy-done.3
  85.5 0.1 pad_maximum_fusion.1
  85.6 20.1 %collective-permute-start.17 = (bf16[3,2,4,32,512]{4,3,2,1,0:T(8,128)(2,1)S(1)}, bf16[3,2,4,32,512]{4,3,2,1,0:T(8,128)(2,1)S(1)}, u32[]{:S(2)}, u32[]{:S(2)}) collective-permute-start(bf16[3,2,4,32,512]{4,3,2,1,0:T(8,128)(2,1)S(1)} %pad_maximum_fusion.1), channel_id=1, source_target_pairs={{0,8},{8,0},{1,9},{9,1},{2,10},{10,2},{3,11},{11,3},{4,12},{12,4},... | collective-permute-start | bytes 2359304 | tf_op jit(solution)/shard_map/ppermute | solution.py:268
  105.7 0.0 collective-permute-done.2.four
  105.7 0.0 collective-permute-done.3.two
  105.7 0.1 pad_maximum_fusion
  105.8 0.6 copy-done.8
  106.5 1.9 %collective-permute-start.5 = (bf16[3,256,512]{2,1,0:T(8,128)(2,1)S(1)}, bf16[3,256,512]{2,1,0:T(8,128)(2,1)S(1)}, u32[]{:S(2)}, u32[]{:S(2)}) collective-permute-start(bf16[3,256,512]{2,1,0:T(8,128)(2,1)S(1)} %pad_maximum_fusion), channel_id=1, source_target_pairs={{0,1},{1,0},{2,3},{3,2},{4,5},{5,4},{6,7},{7,6},{8,9},{9,8},{10,11... | collective-permute-start | bytes 2359304 | tf_op jit(solution)/shard_map/ppermute | solution.py:245
  108.4 0.0 collective-permute-done.12.refs_3_
  108.4 0.0 collective-permute-done.16.refs_4_
  108.4 0.1 pad_maximum_fusion.2
  108.5 0.6 copy-done.9
  109.1 0.1 copy-done.10
  109.2 4.6 %collective-permute-start.19 = (bf16[3,2,4,32,512]{4,3,2,1,0:T(8,128)(2,1)S(1)}, bf16[3,2,4,32,512]{4,3,2,1,0:T(8,128)(2,1)}, u32[]{:S(2)}, u32[]{:S(2)}) collective-permute-start(bf16[3,2,4,32,512]{4,3,2,1,0:T(8,128)(2,1)S(1)} %pad_maximum_fusion.2), channel_id=1, source_target_pairs={{0,8},{8,0},{1,9},{9,1},{2,10},{10,2},{3,11},{11,3},{4,12},{12,4},... | collective-permute-start | bytes 2359304 | tf_op jit(solution)/shard_map/ppermute | solution.py:268
  113.8 1.9 %collective-permute-start.4 = (bf16[256,512]{1,0:T(8,128)(2,1)S(1)}, bf16[256,512]{1,0:T(8,128)(2,1)S(1)}, u32[]{:S(2)}, u32[]{:S(2)}) collective-permute-start(bf16[256,512]{1,0:T(8,128)(2,1)S(1)} %collective-permute-done.2.four), channel_id=1, source_target_pairs={{0,2},{1,3},{2,0},{3,1},{4,6},{5,7},{6,4},{7,5},{8,10},{9,11},{10,... | collective-permute-start | bytes 786440 | tf_op jit(solution)/shard_map/ppermute | solution.py:245
  115.8 0.1 pad_maximum_fusion.3
  115.8 1.9 %collective-permute-start.18 = (bf16[2,2,4,32,512]{4,3,2,1,0:T(8,128)(2,1)S(1)}, bf16[2,2,4,32,512]{4,3,2,1,0:T(8,128)(2,1)S(1)}, u32[]{:S(2)}, u32[]{:S(2)}) collective-permute-start(bf16[2,2,4,32,512]{4,3,2,1,0:T(8,128)(2,1)S(1)} %pad_maximum_fusion.3), channel_id=1, source_target_pairs={{0,8},{8,0},{1,9},{9,1},{2,10},{10,2},{3,11},{11,3},{4,12},{12,4},... | collective-permute-start | bytes 1572872 | tf_op jit(solution)/shard_map/ppermute | solution.py:268
  117.7 13.4 %collective-permute-done.4.six = bf16[256,512]{1,0:T(8,128)(2,1)S(1)} collective-permute-done((bf16[256,512]{1,0:T(8,128)(2,1)S(1)}, bf16[256,512]{1,0:T(8,128)(2,1)S(1)}, u32[]{:S(2)}, u32[]{:S(2)}) %collective-permute-start.4) | collective-permute-done | bytes 262176 | tf_op jit(solution)/shard_map/ppermute | solution.py:245
  131.1 3.5 %collective-permute-start.6 = (bf16[256,512]{1,0:T(8,128)(2,1)S(1)}, bf16[256,512]{1,0:T(8,128)(2,1)S(1)}, u32[]{:S(2)}, u32[]{:S(2)}) collective-permute-start(bf16[256,512]{1,0:T(8,128)(2,1)S(1)} %collective-permute-done.4.six), channel_id=1, source_target_pairs={{0,1},{1,0},{2,3},{3,2},{4,5},{5,4},{6,7},{7,6},{8,9},{9,8},{10,11... | collective-permute-start | bytes 786440 | tf_op jit(solution)/shard_map/ppermute | solution.py:245
  134.7 5.8 %collective-permute-done.6.seven = bf16[256,512]{1,0:T(8,128)(2,1)S(1)} collective-permute-done((bf16[256,512]{1,0:T(8,128)(2,1)S(1)}, bf16[256,512]{1,0:T(8,128)(2,1)S(1)}, u32[]{:S(2)}, u32[]{:S(2)}) %collective-permute-start.6) | collective-permute-done | bytes 262176 | tf_op jit(solution)/shard_map/ppermute | solution.py:245
  140.5 0.0 collective-permute-done.18.refs_9_
  140.5 0.0 collective-permute-done.17.refs_8_
  140.5 0.0 collective-permute-done.5.odd
  140.5 0.9 copy-done.11
  141.4 0.0 collective-permute-done.19.refs_10_
  141.4 0.0 copy-done.15
  141.4 0.2 copy-done.13
  141.6 0.7 copy-done.12
  142.3 6.2 %project.1 = bf16[256,512]{1,0:T(8,128)(2,1)} custom-call(s32[5]{0:T(128)} %stack.77.place, bf16[256,512]{1,0:T(8,128)(2,1)} %early.1.own, bf16[256,512]{1,0:T(8,128)(2,1)} %copy-done.7, bf16[256,512]{1,0:T(8,128)(2,1)} %copy-done.8, bf16[256,512]{1,0:T(8,128)(2,1)} %copy-done.14, bf16[3,256,512]{2,1,0:T(8,128)(2,1)} %copy-done.12, ...), custom_call_target="tpu_custom_call" | custom-call | flops 1073741824 | bytes 8000000 | tf_op jit(solution)/shard_map/project/pallas_call | solution.py:270
  (33 shorter events, 0.1 us)
Async XLA Ops:
  0.0 26.2 %collective-permute-start.1 = (bf16[32,512]{1,0:T(8,128)(2,1)}, bf16[32,512]{1,0:T(8,128)(2,1)S(1)}, u32[]{:S(2)}, u32[]{:S(2)}) collective-permute-start(bf16[32,512]{1,0:T(8,128)(2,1)} %mine.1), channel_id=1, source_target_pairs={{0,64},{64,0},{1,65},{65,1},{2,66},{66,2},{3,67},{67,3},{4,68},{68... | collective-permute-start | bytes 98312 | tf_op jit(solution)/shard_map/ppermute | solution.py:207
  23.5 2.7 %copy-start.17 = (bf16[32,512]{1,0:T(8,128)(2,1)S(1)}, bf16[32,512]{1,0:T(8,128)(2,1)}, u32[]{:S(2)}) copy-start(bf16[32,512]{1,0:T(8,128)(2,1)} %mine.1) | copy-start | bytes 98308
  26.2 0.6 copy-start.18
  26.8 10.0 %collective-permute-start.7 = (bf16[2,32,512]{2,1,0:T(8,128)(2,1)S(1)}, bf16[2,32,512]{2,1,0:T(8,128)(2,1)S(1)}, u32[]{:S(2)}, u32[]{:S(2)}) collective-permute-start(bf16[2,32,512]{2,1,0:T(8,128)(2,1)S(1)} %pad_maximum_fusion.4), channel_id=1, source_target_pairs={{16,0},{32,16},{48,32},{0,48},{17,1},{33,17},{49,33},{1,49},{18,2}... | collective-permute-start | bytes 196616 | tf_op jit(solution)/shard_map/ppermute | solution.py:231
  31.2 6.5 %collective-permute-start.8 = (bf16[2,32,512]{2,1,0:T(8,128)(2,1)S(1)}, bf16[2,32,512]{2,1,0:T(8,128)(2,1)S(1)}, u32[]{:S(2)}, u32[]{:S(2)}) collective-permute-start(bf16[2,32,512]{2,1,0:T(8,128)(2,1)S(1)} %pad_maximum_fusion.4), channel_id=1, source_target_pairs={{32,0},{48,16},{0,32},{16,48},{33,1},{49,17},{1,33},{17,49},{34,2}... | collective-permute-start | bytes 196616 | tf_op jit(solution)/shard_map/ppermute | solution.py:231
  33.6 6.6 %collective-permute-start.9 = (bf16[2,32,512]{2,1,0:T(8,128)(2,1)S(1)}, bf16[2,32,512]{2,1,0:T(8,128)(2,1)S(1)}, u32[]{:S(2)}, u32[]{:S(2)}) collective-permute-start(bf16[2,32,512]{2,1,0:T(8,128)(2,1)S(1)} %pad_maximum_fusion.4), channel_id=1, source_target_pairs={{48,0},{0,16},{16,32},{32,48},{49,1},{1,17},{17,33},{33,49},{50,2}... | collective-permute-start | bytes 196616 | tf_op jit(solution)/shard_map/ppermute | solution.py:231
  36.8 17.3 %copy-start.22 = (bf16[176,512]{1,0:T(8,128)(2,1)S(1)}, bf16[176,512]{1,0:T(8,128)(2,1)}, u32[]{:S(2)}) copy-start(bf16[176,512]{1,0:T(8,128)(2,1)} %get-tuple-element.12) | copy-start | bytes 540676
  36.8 3.4 %copy-start.19 = (bf16[2,32,512]{2,1,0:T(8,128)(2,1)}, bf16[2,32,512]{2,1,0:T(8,128)(2,1)S(1)}, u32[]{:S(2)}) copy-start(bf16[2,32,512]{2,1,0:T(8,128)(2,1)S(1)} %collective-permute-done.7.refs_0_) | copy-start | bytes 196612
  37.7 2.5 %copy-start.20 = (bf16[2,32,512]{2,1,0:T(8,128)(2,1)}, bf16[2,32,512]{2,1,0:T(8,128)(2,1)S(1)}, u32[]{:S(2)}) copy-start(bf16[2,32,512]{2,1,0:T(8,128)(2,1)S(1)} %collective-permute-done.8.refs_1_) | copy-start | bytes 196612
  40.2 0.6 copy-start.21
  42.5 9.7 %collective-permute-start.13 = (bf16[2,4,32,512]{3,2,1,0:T(8,128)(2,1)}, bf16[2,4,32,512]{3,2,1,0:T(8,128)(2,1)S(1)}, u32[]{:S(2)}, u32[]{:S(2)}) collective-permute-start(bf16[2,4,32,512]{3,2,1,0:T(8,128)(2,1)} %arrange.1.refs_0_), channel_id=1, source_target_pairs={{0,128},{128,256},{256,384},{384,512},{512,640},{640,768},{768,896... | collective-permute-start | bytes 786440 | tf_op jit(solution)/shard_map/ppermute | solution.py:190
  45.7 12.3 %collective-permute-start.10 = (bf16[2,4,32,512]{3,2,1,0:T(8,128)(2,1)}, bf16[2,4,32,512]{3,2,1,0:T(8,128)(2,1)S(1)}, u32[]{:S(2)}, u32[]{:S(2)}) collective-permute-start(bf16[2,4,32,512]{3,2,1,0:T(8,128)(2,1)} %arrange.1.refs_0_), channel_id=1, source_target_pairs={{128,0},{256,128},{384,256},{512,384},{640,512},{768,640},{896,768... | collective-permute-start | bytes 786440 | tf_op jit(solution)/shard_map/ppermute | solution.py:193
  52.2 33.2 %copy-start.2 = (bf16[2,4,32,512]{3,2,1,0:T(8,128)(2,1)}, bf16[2,4,32,512]{3,2,1,0:T(8,128)(2,1)S(1)}, u32[]{:S(2)}) copy-start(bf16[2,4,32,512]{3,2,1,0:T(8,128)(2,1)S(1)} %collective-permute-done.13.refs_7_) | copy-start | bytes 786436
  52.2 10.5 %collective-permute-start.14 = (bf16[2,4,32,512]{3,2,1,0:T(8,128)(2,1)S(1)}, bf16[2,4,32,512]{3,2,1,0:T(8,128)(2,1)S(1)}, u32[]{:S(2)}, u32[]{:S(2)}) collective-permute-start(bf16[2,4,32,512]{3,2,1,0:T(8,128)(2,1)S(1)} %collective-permute-done.13.refs_7_), channel_id=1, source_target_pairs={{0,128},{128,256},{256,384},{384,512},{512,640},{640,768},{768,896... | collective-permute-start | bytes 786440 | tf_op jit(solution)/shard_map/ppermute | solution.py:190
  54.1 10.6 %collective-permute-start = (bf16[176,512]{1,0:T(8,128)(2,1)S(1)}, bf16[176,512]{1,0:T(8,128)(2,1)S(1)}, u32[]{:S(2)}, u32[]{:S(2)}) collective-permute-start(bf16[176,512]{1,0:T(8,128)(2,1)S(1)} %copy-done.22), channel_id=1, source_target_pairs={{0,8},{8,16},{16,24},{24,32},{32,40},{40,48},{48,56},{56,64},{64,7... | collective-permute-start | bytes 540680 | tf_op jit(solution)/shard_map/ppermute | solution.py:217
  58.0 27.4 %copy-start.3 = (bf16[2,4,32,512]{3,2,1,0:T(8,128)(2,1)}, bf16[2,4,32,512]{3,2,1,0:T(8,128)(2,1)S(1)}, u32[]{:S(2)}) copy-start(bf16[2,4,32,512]{3,2,1,0:T(8,128)(2,1)S(1)} %collective-permute-done.10.refs_1_) | copy-start | bytes 786436
  58.0 20.9 %collective-permute-start.11 = (bf16[2,4,32,512]{3,2,1,0:T(8,128)(2,1)S(1)}, bf16[2,4,32,512]{3,2,1,0:T(8,128)(2,1)S(1)}, u32[]{:S(2)}, u32[]{:S(2)}) collective-permute-start(bf16[2,4,32,512]{3,2,1,0:T(8,128)(2,1)S(1)} %collective-permute-done.10.refs_1_), channel_id=1, source_target_pairs={{128,0},{256,128},{384,256},{512,384},{640,512},{768,640},{896,768... | collective-permute-start | bytes 786440 | tf_op jit(solution)/shard_map/ppermute | solution.py:193
  62.8 53.0 %copy-start.4 = (bf16[2,4,32,512]{3,2,1,0:T(8,128)(2,1)}, bf16[2,4,32,512]{3,2,1,0:T(8,128)(2,1)S(1)}, u32[]{:S(2)}) copy-start(bf16[2,4,32,512]{3,2,1,0:T(8,128)(2,1)S(1)} %collective-permute-done.14.refs_6_) | copy-start | bytes 786436
  62.8 20.7 %collective-permute-start.15 = (bf16[2,4,32,512]{3,2,1,0:T(8,128)(2,1)S(1)}, bf16[2,4,32,512]{3,2,1,0:T(8,128)(2,1)S(1)}, u32[]{:S(2)}, u32[]{:S(2)}) collective-permute-start(bf16[2,4,32,512]{3,2,1,0:T(8,128)(2,1)S(1)} %collective-permute-done.14.refs_6_), channel_id=1, source_target_pairs={{0,128},{128,256},{256,384},{384,512},{512,640},{640,768},{768,896... | collective-permute-start | bytes 786440 | tf_op jit(solution)/shard_map/ppermute | solution.py:190
  64.7 0.7 copy-start.16
  65.4 20.1 %copy-start = (bf16[2,4,32,512]{3,2,1,0:T(8,128)(2,1)S(1)}, bf16[2,4,32,512]{3,2,1,0:T(8,128)(2,1)}, u32[]{:S(2)}) copy-start(bf16[2,4,32,512]{3,2,1,0:T(8,128)(2,1)} %arrange.1.refs_0_) | copy-start | bytes 786436
  69.0 36.7 %collective-permute-start.2 = (bf16[256,512]{1,0:T(8,128)(2,1)}, bf16[256,512]{1,0:T(8,128)(2,1)S(1)}, u32[]{:S(2)}, u32[]{:S(2)}) collective-permute-start(bf16[256,512]{1,0:T(8,128)(2,1)} %early.1.own), channel_id=1, source_target_pairs={{0,4},{1,5},{2,6},{3,7},{4,0},{5,1},{6,2},{7,3},{8,12},{9,13},{10,... | collective-permute-start | bytes 786440 | tf_op jit(solution)/shard_map/ppermute | solution.py:245
  74.9 30.8 %collective-permute-start.3 = (bf16[256,512]{1,0:T(8,128)(2,1)}, bf16[256,512]{1,0:T(8,128)(2,1)S(1)}, u32[]{:S(2)}, u32[]{:S(2)}) collective-permute-start(bf16[256,512]{1,0:T(8,128)(2,1)} %early.1.own), channel_id=1, source_target_pairs={{0,2},{1,3},{2,0},{3,1},{4,6},{5,7},{6,4},{7,5},{8,10},{9,11},{10,... | collective-permute-start | bytes 786440 | tf_op jit(solution)/shard_map/ppermute | solution.py:245
  78.9 36.9 %copy-start.5 = (bf16[2,4,32,512]{3,2,1,0:T(8,128)(2,1)}, bf16[2,4,32,512]{3,2,1,0:T(8,128)(2,1)S(1)}, u32[]{:S(2)}) copy-start(bf16[2,4,32,512]{3,2,1,0:T(8,128)(2,1)S(1)} %collective-permute-done.11.refs_2_) | copy-start | bytes 786436
  78.9 29.5 %collective-permute-start.12 = (bf16[2,4,32,512]{3,2,1,0:T(8,128)(2,1)S(1)}, bf16[2,4,32,512]{3,2,1,0:T(8,128)(2,1)S(1)}, u32[]{:S(2)}, u32[]{:S(2)}) collective-permute-start(bf16[2,4,32,512]{3,2,1,0:T(8,128)(2,1)S(1)} %collective-permute-done.11.refs_2_), channel_id=1, source_target_pairs={{128,0},{256,128},{384,256},{512,384},{640,512},{768,640},{896,768... | collective-permute-start | bytes 786440 | tf_op jit(solution)/shard_map/ppermute | solution.py:193
  83.5 24.9 %copy-start.6 = (bf16[2,4,32,512]{3,2,1,0:T(8,128)(2,1)}, bf16[2,4,32,512]{3,2,1,0:T(8,128)(2,1)S(1)}, u32[]{:S(2)}) copy-start(bf16[2,4,32,512]{3,2,1,0:T(8,128)(2,1)S(1)} %collective-permute-done.15.refs_5_) | copy-start | bytes 786436
  83.5 24.9 %collective-permute-start.16 = (bf16[2,4,32,512]{3,2,1,0:T(8,128)(2,1)S(1)}, bf16[2,4,32,512]{3,2,1,0:T(8,128)(2,1)S(1)}, u32[]{:S(2)}, u32[]{:S(2)}) collective-permute-start(bf16[2,4,32,512]{3,2,1,0:T(8,128)(2,1)S(1)} %collective-permute-done.15.refs_5_), channel_id=1, source_target_pairs={{0,128},{128,256},{256,384},{384,512},{512,640},{640,768},{768,896... | collective-permute-start | bytes 786440 | tf_op jit(solution)/shard_map/ppermute | solution.py:190
  85.4 20.3 %copy-start.1 = (bf16[256,512]{1,0:T(8,128)(2,1)S(1)}, bf16[256,512]{1,0:T(8,128)(2,1)}, u32[]{:S(2)}) copy-start(bf16[256,512]{1,0:T(8,128)(2,1)} %early.1.own) | copy-start | bytes 786436
  85.6 54.9 %collective-permute-start.17 = (bf16[3,2,4,32,512]{4,3,2,1,0:T(8,128)(2,1)S(1)}, bf16[3,2,4,32,512]{4,3,2,1,0:T(8,128)(2,1)S(1)}, u32[]{:S(2)}, u32[]{:S(2)}) collective-permute-start(bf16[3,2,4,32,512]{4,3,2,1,0:T(8,128)(2,1)S(1)} %pad_maximum_fusion.1), channel_id=1, source_target_pairs={{0,8},{8,0},{1,9},{9,1},{2,10},{10,2},{3,11},{11,3},{4,12},{12,4},... | collective-permute-start | bytes 2359304 | tf_op jit(solution)/shard_map/ppermute | solution.py:268
  105.7 8.1 %copy-start.7 = (bf16[256,512]{1,0:T(8,128)(2,1)}, bf16[256,512]{1,0:T(8,128)(2,1)S(1)}, u32[]{:S(2)}) copy-start(bf16[256,512]{1,0:T(8,128)(2,1)S(1)} %collective-permute-done.2.four) | copy-start | bytes 786436
  105.7 0.7 copy-start.8
  106.5 34.0 %collective-permute-start.5 = (bf16[3,256,512]{2,1,0:T(8,128)(2,1)S(1)}, bf16[3,256,512]{2,1,0:T(8,128)(2,1)S(1)}, u32[]{:S(2)}, u32[]{:S(2)}) collective-permute-start(bf16[3,256,512]{2,1,0:T(8,128)(2,1)S(1)} %pad_maximum_fusion), channel_id=1, source_target_pairs={{0,1},{1,0},{2,3},{3,2},{4,5},{5,4},{6,7},{7,6},{8,9},{9,8},{10,11... | collective-permute-start | bytes 2359304 | tf_op jit(solution)/shard_map/ppermute | solution.py:245
  108.4 0.7 copy-start.9
  108.4 0.8 copy-start.10
  109.2 32.2 %collective-permute-start.19 = (bf16[3,2,4,32,512]{4,3,2,1,0:T(8,128)(2,1)S(1)}, bf16[3,2,4,32,512]{4,3,2,1,0:T(8,128)(2,1)}, u32[]{:S(2)}, u32[]{:S(2)}) collective-permute-start(bf16[3,2,4,32,512]{4,3,2,1,0:T(8,128)(2,1)S(1)} %pad_maximum_fusion.2), channel_id=1, source_target_pairs={{0,8},{8,0},{1,9},{9,1},{2,10},{10,2},{3,11},{11,3},{4,12},{12,4},... | collective-permute-start | bytes 2359304 | tf_op jit(solution)/shard_map/ppermute | solution.py:268
  113.8 17.3 %collective-permute-start.4 = (bf16[256,512]{1,0:T(8,128)(2,1)S(1)}, bf16[256,512]{1,0:T(8,128)(2,1)S(1)}, u32[]{:S(2)}, u32[]{:S(2)}) collective-permute-start(bf16[256,512]{1,0:T(8,128)(2,1)S(1)} %collective-permute-done.2.four), channel_id=1, source_target_pairs={{0,2},{1,3},{2,0},{3,1},{4,6},{5,7},{6,4},{7,5},{8,10},{9,11},{10,... | collective-permute-start | bytes 786440 | tf_op jit(solution)/shard_map/ppermute | solution.py:245
  115.8 24.7 %collective-permute-start.18 = (bf16[2,2,4,32,512]{4,3,2,1,0:T(8,128)(2,1)S(1)}, bf16[2,2,4,32,512]{4,3,2,1,0:T(8,128)(2,1)S(1)}, u32[]{:S(2)}, u32[]{:S(2)}) collective-permute-start(bf16[2,2,4,32,512]{4,3,2,1,0:T(8,128)(2,1)S(1)} %pad_maximum_fusion.3), channel_id=1, source_target_pairs={{0,8},{8,0},{1,9},{9,1},{2,10},{10,2},{3,11},{11,3},{4,12},{12,4},... | collective-permute-start | bytes 1572872 | tf_op jit(solution)/shard_map/ppermute | solution.py:268
  131.1 10.3 %copy-start.14 = (bf16[256,512]{1,0:T(8,128)(2,1)}, bf16[256,512]{1,0:T(8,128)(2,1)S(1)}, u32[]{:S(2)}) copy-start(bf16[256,512]{1,0:T(8,128)(2,1)S(1)} %collective-permute-done.4.six) | copy-start | bytes 786436
  131.1 9.3 %collective-permute-start.6 = (bf16[256,512]{1,0:T(8,128)(2,1)S(1)}, bf16[256,512]{1,0:T(8,128)(2,1)S(1)}, u32[]{:S(2)}, u32[]{:S(2)}) collective-permute-start(bf16[256,512]{1,0:T(8,128)(2,1)S(1)} %collective-permute-done.4.six), channel_id=1, source_target_pairs={{0,1},{1,0},{2,3},{3,2},{4,5},{5,4},{6,7},{7,6},{8,9},{9,8},{10,11... | collective-permute-start | bytes 786440 | tf_op jit(solution)/shard_map/ppermute | solution.py:245
  140.5 1.0 copy-start.15
  140.5 1.1 copy-start.13
  140.5 0.9 copy-start.11
  141.4 0.9 copy-start.12

commit v3 on v2

--- a/solution.py
+++ b/solution.py
@@ -1,3 +1,5 @@
+import functools
+
 import jax
 import jax.numpy as jnp
 import numpy as np
@@ -124,56 +126,48 @@
         out[pl.ds(at, count), :] = value.astype(BF16)
 
 
-def arrange_kernel(place, mine, over, *refs):
-    arrived, out = refs[:3], refs[3]
-    zh, x = place[1], place[3]
-    for rel in range(4):
-        for other in range(2):
-            piece = (mine, over)[other][...] if rel == 0 else arrived[rel - 1][other]
-            out[lax.rem(zh + other, 2), lax.rem(x + rel, 4)] = piece
-
-
-ORDER = ((0, 7, 1), (6, 2), (5, 3, 4))
-
-
-def final_kernel(place, own, four, two, six, odd, seven, residual, *refs):
-    weights, swapped = refs[:8], refs[8:11]
-    out, gv, wv, gsem, wsem = refs[11:]
-    me, y, core = place[0], place[2], place[4]
-    pieces = [(own, 0), (four, 4), (two, 2), (six, 6), (seven, 7)]
-    pieces += [(odd.at[i], by) for i, by in enumerate((1, 5, 3))]
+ORDER = ((0, 7, 1), (6, 2, 4), (5, 3))
+
+
+def project_kernel(batches, place, *refs):
+    pieces = refs[:6]
+    count = sum(len(ORDER[batch]) for batch in batches)
+    weights = refs[6 : 6 + count]
+    swapped = refs[6 + count : 6 + count + len(batches)]
+    start, out, gv, wv, gsem, wsem = refs[6 + count + len(batches) :]
+    me, y, x, core = place[0], place[2], place[3], place[4]
+    own, four, two, six, odd, seven = pieces
+    gated = [(own, 0), (four, 4), (two, 2), (six, 6), (seven, 7)]
+    gated += [(odd.at[i], by) for i, by in enumerate((1, 5, 3))]
     gated = [
         pltpu.make_async_copy(piece, gv.at[lax.bitwise_xor(me, by)], gsem.at[by])
-        for piece, by in pieces
+        for piece, by in gated
     ]
-    rows = []
-    for batch, order in enumerate(ORDER):
-        for i, by in enumerate(order):
-            at = lax.rem(y + by, 8)
-            rows.append(
-                [
+    places = [(batch, i) for batch in batches for i in range(len(ORDER[batch]))]
+    blocks = []
+    for n, (batch, i) in enumerate(places):
+        parts = []
+        for rel in range(4):
+            at = lax.rem(x + rel, 4)
+            for other, source in enumerate((weights[n], swapped[batches.index(batch)].at[i])):
+                to = core if other == 0 else 1 - core
+                parts.append(
                     pltpu.make_async_copy(
-                        weights[by], wv.at[at, :, :, core], wsem.at[by, 0]
-                    ),
-                    pltpu.make_async_copy(
-                        swapped[batch].at[i], wv.at[at, :, :, 1 - core], wsem.at[by, 1]
-                    ),
-                ]
-            )
-    for copy in gated:
+                        source.at[rel], wv.at[n, :, at, to], wsem.at[n, rel * 2 + other]
+                    )
+                )
+        blocks.append(parts)
+    for copy in gated + sum(blocks, []):
         copy.start()
-    for pair in rows:
-        for copy in pair:
-            copy.start()
-    total = residual[...].astype(F32)
+    total = start[...].astype(F32)
     for copy in gated:
         copy.wait()
-    for by, pair in zip(sum(ORDER, ()), rows):
-        for copy in pair:
+    for n, (batch, i) in enumerate(places):
+        for copy in blocks[n]:
             copy.wait()
-        k = lax.rem(y + by, 8)
-        total = total + dot(gv[k], wv[k].reshape(512, 512))
-    out[...] = total.astype(BF16)
+        k = lax.rem(y + ORDER[batch][i], 8)
+        total = total + dot(gv[k], wv[n].reshape(512, 512))
+    out[...] = total.astype(out.dtype)
 
 
 def sds(shape, dtype):
@@ -185,14 +179,15 @@
 
 
 def around_y(own):
+    def shift(piece, by):
+        return lax.ppermute(piece, "y", [((i + by) % 8, i) for i in range(8)])
+
     up, down, ups, downs = own, own, [], []
-    for step in range(4):
-        up = lax.ppermute(up, "y", [(i, (i + 1) % 8) for i in range(8)])
+    for _ in range(3):
+        up, down = shift(up, 7), shift(down, 1)
         ups.append(up)
-        if step < 3:
-            down = lax.ppermute(down, "y", [((i + 1) % 8, i) for i in range(8)])
-            downs.append(down)
-    return [own] + downs + ups[::-1]
+        downs.append(down)
+    return [own] + downs + [shift(own, 4)] + ups[::-1]
 
 
 def on_device(residual, proj, short_filter, medium_filter, skip, out_weight):
@@ -225,7 +220,11 @@
 
     over, late = lax.optimization_barrier((over, late))
 
-    mine = jnp.stack([out_weight, over])
+    mine = jnp.where(
+        lax.axis_index("zh") == 0,
+        jnp.stack([out_weight, over]),
+        jnp.stack([over, out_weight]),
+    )
     arrived = []
     for by in (1, 2, 3):
         arrived.append(lax.ppermute(mine, "x", [((i + by) % 4, i) for i in range(4)]))
@@ -253,34 +252,34 @@
     smem = pl.BlockSpec(memory_space=pltpu.SMEM)
     vmem = pl.BlockSpec(memory_space=pltpu.VMEM)
     anywhere = pl.BlockSpec(memory_space=pl.ANY)
-    block = pl.pallas_call(
-        arrange_kernel,
-        out_shape=sds((2, 4, WROWS, chans), BF16),
-        in_specs=[smem] + [vmem] * 5,
-        out_specs=vmem,
-        cost_estimate=cost(0, 500_000),
-        name="arrange",
-    )(place, out_weight, over, *arrived)
+    block = jnp.stack([mine] + arrived)
     weights = around_y(block)
     swapped = []
     for order in ORDER:
         group = jnp.stack([weights[by] for by in order])
         swapped.append(lax.ppermute(group, "core", [(0, 1), (1, 0)]))
 
-    return pl.pallas_call(
-        final_kernel,
-        out_shape=sds((rows, chans), BF16),
-        in_specs=[smem] + [anywhere] * 6 + [vmem] + [anywhere] * 11,
-        out_specs=vmem,
-        scratch_shapes=[
-            pltpu.VMEM((8, rows, chans), BF16),
-            pltpu.VMEM((8, 2, 4, 2, WROWS, chans), BF16),
-            pltpu.SemaphoreType.DMA((8,)),
-            pltpu.SemaphoreType.DMA((8, 2)),
-        ],
-        cost_estimate=cost(2 * rows * 8 * chans * chans, 8_000_000),
-        name="project",
-    )(place, gated, four, two, six, odd, seven, residual, *weights, *swapped)
+    def project(batches, start, dtype):
+        count = sum(len(ORDER[batch]) for batch in batches)
+        used = [weights[by] for batch in batches for by in ORDER[batch]]
+        used += [swapped[batch] for batch in batches]
+        return pl.pallas_call(
+            functools.partial(project_kernel, batches),
+            out_shape=sds((rows, chans), dtype),
+            in_specs=[smem] + [anywhere] * (6 + len(used)) + [vmem],
+            out_specs=vmem,
+            scratch_shapes=[
+                pltpu.VMEM((8, rows, chans), BF16),
+                pltpu.VMEM((count, 2, 4, 2, WROWS, chans), BF16),
+                pltpu.SemaphoreType.DMA((8,)),
+                pltpu.SemaphoreType.DMA((count, 8)),
+            ],
+            cost_estimate=cost(2 * rows * count * chans * chans, 8_000_000),
+            name="project",
+        )(place, gated, four, two, six, odd, seven, *used, start)
+
+    most = project((0, 1), residual, F32)
+    return project((2,), most, BF16)
 
 
 def solution(mesh):

time: 152 us -> 140 us (0.921); the launches traced: 148 us -> 140 us
  starting transfers between devices: 98.9 us -> 84.7 us
  other arithmetic: 0.33 us -> 3.03 us
  Pallas kernels: 17.8 us -> 20.4 us
  waiting for transfers between devices: 25.3 us -> 27.3 us
  local copies, waits for them, and re-layouts: 5.64 us -> 3.73 us
    ppermute x3, starting transfers between devices: 26.6 us -> 8.15 us  [on_device(): swapped.append(lax.ppermute(group, 'core', [(0, 1), (1, 0)]))]
    ppermute x7, starting transfers between devices: 22.1 us -> 26.4 us  [shift(): return lax.ppermute(piece, 'y', [((i + by) % 8, i) for i in range(8)])]
    ppermute x5, starting transfers between devices: 17.2 us -> 13.2 us  [exchange(): return lax.ppermute(piece, 'tp', [(i, i ^ by) for i in range(8)])]
    ppermute x3, starting transfers between devices: 9.31 us -> 13.1 us  [on_device(): lax.ppermute(mine, 'x', [((i + by) % 4, i) for i in range(4)])]
    ppermute x5, waiting for transfers between devices: 19.2 us -> 22.7 us  [exchange(): return lax.ppermute(piece, 'tp', [(i, i ^ by) for i in range(8)])]
    pallas_call x2, Pallas kernels: 7.88 us -> 10.5 us  [project(): pl.pallas_call(functools.partial(project_kernel, batches), out_shape=sds(...]
    unnamed x46 -> x34, local copies, waits for them, and re-layouts: 5.01 us -> 3.05 us
    ppermute x7, waiting for transfers between devices: 2.67 us -> 0.86 us  [shift(): return lax.ppermute(piece, 'y', [((i + by) % 8, i) for i in range(8)])]
  transfers between devices with their start and end apart: 20 -> 20, of which waited for: 5 -> 6; matrix products, arithmetic and copies ran while one was open for 1% -> 3% of each run, Pallas kernels for 7% -> 11%
where the time goes in v3:
time: 140 us
  starting transfers between devices  84.7 us (60%)
  waiting for transfers between devices  27.3 us (20%)
  Pallas kernels  20.4 us (15%)
  local copies, waits for them, and re-layouts  3.73 us (3%)
  other arithmetic  3.03 us (2%)
    ppermute x7, starting transfers between devices, shift(): return lax.ppermute(piece, 'y', [((i + by) % 8, i) for i in range(8)])  26.4 us
    ppermute x5, waiting for transfers between devices, exchange(): return lax.ppermute(piece, 'tp', [(i, i ^ by) for i in range(8)])  22.7 us
    ppermute x1, starting transfers between devices, on_device(): over = lax.ppermute(out_weight, 'zh', [(0, 1), (1, 0)])  19.9 us
    ppermute x5, starting transfers between devices, exchange(): return lax.ppermute(piece, 'tp', [(i, i ^ by) for i in range(8)])  13.2 us
    ppermute x3, starting transfers between devices, on_device(): lax.ppermute(mine, 'x', [((i + by) % 4, i) for i in range(4)])  13.1 us
    pallas_call x2, Pallas kernels, project(): pl.pallas_call(functools.partial(project_kernel, batches), out_shape=sds(...  10.5 us
    ppermute x3, starting transfers between devices, on_device(): swapped.append(lax.ppermute(group, 'core', [(0, 1), (1, 0)]))  8.15 us
    ppermute x1, starting transfers between devices, on_device(): lax.ppermute(pack, ('y', 'zh', 'x', 'core'), [(i, i + 1) for i in range(1...  3.95 us
  transfers between devices with their start and end apart: 20, of which 6 were waited for; matrix products, arithmetic and copies ran while one was open for 3% of the time, Pallas kernels for 11%

profile of v3, /device:TPU:1, one launch (start us, length us, event | category | flops | bytes accessed | tf_op | source)
XLA Modules:
  0.0 139.6 jit_solution(17781883207642362154)
XLA Ops:
  0.0 19.9 %collective-permute-start.1 = (bf16[32,512]{1,0:T(8,128)(2,1)}, bf16[32,512]{1,0:T(8,128)(2,1)S(1)}, u32[]{:S(2)}, u32[]{:S(2)}) collective-permute-start(bf16[32,512]{1,0:T(8,128)(2,1)} %param.13), channel_id=1, source_target_pairs={{0,64},{64,0},{1,65},{65,1},{2,66},{66,2},{3,67},{67,3},{4,68},{68... | collective-permute-start | bytes 98312 | tf_op jit(solution)/shard_map/ppermute | solution.py:202
  19.9 3.6 %local.1 = (bf16[176,512]{1,0:T(8,128)(2,1)}, bf16[256,512]{1,0:T(8,128)(2,1)}, f32[256,512]{1,0:T(8,128)}) custom-call(bf16[3,256,512]{2,1,0:T(8,128)(2,1)} %bitcast.28, bf16[3,7,512]{2,1,0:T(8,128)(2,1)} %bitcast.43), custom_call_target="tpu_custom_call" | custom-call | flops 6000000 | bytes 2000000 | tf_op jit(solution)/shard_map/local/pallas_call | solution.py:204
  23.5 3.9 %collective-permute-start = (bf16[176,512]{1,0:T(8,128)(2,1)}, bf16[176,512]{1,0:T(8,128)(2,1)S(1)}, u32[]{:S(2)}, u32[]{:S(2)}) collective-permute-start(bf16[176,512]{1,0:T(8,128)(2,1)} %get-tuple-element.12), channel_id=1, source_target_pairs={{0,8},{8,16},{16,24},{24,32},{32,40},{40,48},{48,56},{56,64},{64,7... | collective-permute-start | bytes 540680 | tf_op jit(solution)/shard_map/ppermute | solution.py:212
  27.4 0.0 copy-start.16
  27.5 2.7 %late.1 = (bf16[112,512]{1,0:T(8,128)(2,1)}, f32[256,512]{1,0:T(8,128)}) custom-call(bf16[256,512]{1,0:T(8,128)(2,1)} %get-tuple-element.13.prod, f32[256,512]{1,0:T(8,128)} %get-tuple-element.14.q, bf16[128,512]{1,0:T(8,128)(2,1)} %mf.1, f32[1,512]{1,0:T(1,128)} %bitcast.48, bf16[512,256]{1,0:T(8,128)(2,1)} %constant.27.clone.fwd, ...), custom_call_target="tpu_custom_call" | custom-call | flops 300000000 | bytes 3000000 | tf_op jit(solution)/shard_map/late/pallas_call | solution.py:214
  30.1 0.0 collective-permute-done.1
  30.1 0.0 copy-done.16
  30.2 8.7 %collective-permute-start.7 = (bf16[2,32,512]{2,1,0:T(8,128)(2,1)S(1)}, bf16[2,32,512]{2,1,0:T(8,128)(2,1)S(1)}, u32[]{:S(2)}, u32[]{:S(2)}) collective-permute-start(bf16[2,32,512]{2,1,0:T(8,128)(2,1)S(1)} %maximum_select_fusion.1), channel_id=1, source_target_pairs={{16,0},{32,16},{48,32},{0,48},{17,1},{33,17},{49,33},{1,49},{18,2}... | collective-permute-start | bytes 196616 | tf_op jit(solution)/shard_map/ppermute | solution.py:230
  38.9 1.9 %collective-permute-start.8 = (bf16[2,32,512]{2,1,0:T(8,128)(2,1)S(1)}, bf16[2,32,512]{2,1,0:T(8,128)(2,1)S(1)}, u32[]{:S(2)}, u32[]{:S(2)}) collective-permute-start(bf16[2,32,512]{2,1,0:T(8,128)(2,1)S(1)} %maximum_select_fusion.1), channel_id=1, source_target_pairs={{32,0},{48,16},{0,32},{16,48},{33,1},{49,17},{1,33},{17,49},{34,2}... | collective-permute-start | bytes 196616 | tf_op jit(solution)/shard_map/ppermute | solution.py:230
  40.8 2.5 %collective-permute-start.9 = (bf16[2,32,512]{2,1,0:T(8,128)(2,1)S(1)}, bf16[2,32,512]{2,1,0:T(8,128)(2,1)S(1)}, u32[]{:S(2)}, u32[]{:S(2)}) collective-permute-start(bf16[2,32,512]{2,1,0:T(8,128)(2,1)S(1)} %maximum_select_fusion.1), channel_id=1, source_target_pairs={{48,0},{0,16},{16,32},{32,48},{49,1},{1,17},{17,33},{33,49},{50,2}... | collective-permute-start | bytes 196616 | tf_op jit(solution)/shard_map/ppermute | solution.py:230
  43.3 0.0 collective-permute-done.7
  43.3 2.1 %collective-permute-done.8 = bf16[2,32,512]{2,1,0:T(8,128)(2,1)S(1)} collective-permute-done((bf16[2,32,512]{2,1,0:T(8,128)(2,1)S(1)}, bf16[2,32,512]{2,1,0:T(8,128)(2,1)S(1)}, u32[]{:S(2)}, u32[]{:S(2)}) %collective-permute-start.8) | collective-permute-done | bytes 65568 | tf_op jit(solution)/shard_map/ppermute | solution.py:230
  45.4 1.6 %collective-permute-done.9 = bf16[2,32,512]{2,1,0:T(8,128)(2,1)S(1)} collective-permute-done((bf16[2,32,512]{2,1,0:T(8,128)(2,1)S(1)}, bf16[2,32,512]{2,1,0:T(8,128)(2,1)S(1)}, u32[]{:S(2)}, u32[]{:S(2)}) %collective-permute-start.9) | collective-permute-done | bytes 65568 | tf_op jit(solution)/shard_map/ppermute | solution.py:230
  47.1 0.0 copy-start.4
  47.1 1.9 %collective-permute-start.10 = (bf16[4,2,32,512]{3,2,1,0:T(8,128)(2,1)S(1)}, bf16[4,2,32,512]{3,2,1,0:T(8,128)(2,1)S(1)}, u32[]{:S(2)}, u32[]{:S(2)}) collective-permute-start(bf16[4,2,32,512]{3,2,1,0:T(8,128)(2,1)S(1)} %get-tuple-element.20.refs_6_), channel_id=1, source_target_pairs={{896,0},{0,128},{128,256},{256,384},{384,512},{512,640},{640,768},... | collective-permute-start | bytes 786440 | tf_op jit(solution)/shard_map/ppermute | solution.py:183
  49.0 4.6 %collective-permute-start.13 = (bf16[4,2,32,512]{3,2,1,0:T(8,128)(2,1)S(1)}, bf16[4,2,32,512]{3,2,1,0:T(8,128)(2,1)S(1)}, u32[]{:S(2)}, u32[]{:S(2)}) collective-permute-start(bf16[4,2,32,512]{3,2,1,0:T(8,128)(2,1)S(1)} %get-tuple-element.20.refs_6_), channel_id=1, source_target_pairs={{128,0},{256,128},{384,256},{512,384},{640,512},{768,640},{896,768... | collective-permute-start | bytes 786440 | tf_op jit(solution)/shard_map/ppermute | solution.py:183
  53.6 0.0 collective-permute-done.halo
  53.6 0.7 copy-done.15
  54.3 3.6 %early.1.refs_0_ = bf16[256,512]{1,0:T(8,128)(2,1)} custom-call(bf16[3,256,512]{2,1,0:T(8,128)(2,1)} %bitcast.29, bf16[176,512]{1,0:T(8,128)(2,1)} %copy-done.15, bf16[3,7,512]{2,1,0:T(8,128)(2,1)} %bitcast.44, bf16[256,512]{1,0:T(8,128)(2,1)} %get-tuple-element.13.prod, f32[256,512]{1,0:T(8,128)} %get-tuple-element.14.q, ...), custom_call_target="tpu_custom_call" | custom-call | flops 600000000 | bytes 3000000 | tf_op jit(solution)/shard_map/early/pallas_call | solution.py:232
  57.9 3.5 %collective-permute-start.2 = (bf16[256,512]{1,0:T(8,128)(2,1)}, bf16[256,512]{1,0:T(8,128)(2,1)S(1)}, u32[]{:S(2)}, u32[]{:S(2)}) collective-permute-start(bf16[256,512]{1,0:T(8,128)(2,1)} %early.1.refs_0_), channel_id=1, source_target_pairs={{0,4},{1,5},{2,6},{3,7},{4,0},{5,1},{6,2},{7,3},{8,12},{9,13},{10,... | collective-permute-start | bytes 786440 | tf_op jit(solution)/shard_map/ppermute | solution.py:244
  61.4 4.0 %collective-permute-start.3 = (bf16[256,512]{1,0:T(8,128)(2,1)}, bf16[256,512]{1,0:T(8,128)(2,1)S(1)}, u32[]{:S(2)}, u32[]{:S(2)}) collective-permute-start(bf16[256,512]{1,0:T(8,128)(2,1)} %early.1.refs_0_), channel_id=1, source_target_pairs={{0,2},{1,3},{2,0},{3,1},{4,6},{5,7},{6,4},{7,5},{8,10},{9,11},{10,... | collective-permute-start | bytes 786440 | tf_op jit(solution)/shard_map/ppermute | solution.py:244
  65.4 7.0 %collective-permute-start.17 = (bf16[4,2,32,512]{3,2,1,0:T(8,128)(2,1)S(1)}, bf16[4,2,32,512]{3,2,1,0:T(8,128)(2,1)S(1)}, u32[]{:S(2)}, u32[]{:S(2)}) collective-permute-start(bf16[4,2,32,512]{3,2,1,0:T(8,128)(2,1)S(1)} %get-tuple-element.20.refs_6_), channel_id=1, source_target_pairs={{512,0},{640,128},{768,256},{896,384},{0,512},{128,640},{256,768},... | collective-permute-start | bytes 786440 | tf_op jit(solution)/shard_map/ppermute | solution.py:183
  72.4 0.0 collective-permute-done.10.refs_7_
  72.4 0.0 copy-start.7
  72.4 1.9 %collective-permute-start.11 = (bf16[4,2,32,512]{3,2,1,0:T(8,128)(2,1)S(1)}, bf16[4,2,32,512]{3,2,1,0:T(8,128)(2,1)S(1)}, u32[]{:S(2)}, u32[]{:S(2)}) collective-permute-start(bf16[4,2,32,512]{3,2,1,0:T(8,128)(2,1)S(1)} %collective-permute-done.10.refs_7_), channel_id=1, source_target_pairs={{896,0},{0,128},{128,256},{256,384},{384,512},{512,640},{640,768},... | collective-permute-start | bytes 786440 | tf_op jit(solution)/shard_map/ppermute | solution.py:183
  74.3 0.0 collective-permute-done.13.refs_8_
  74.3 4.6 %collective-permute-start.14 = (bf16[4,2,32,512]{3,2,1,0:T(8,128)(2,1)S(1)}, bf16[4,2,32,512]{3,2,1,0:T(8,128)(2,1)S(1)}, u32[]{:S(2)}, u32[]{:S(2)}) collective-permute-start(bf16[4,2,32,512]{3,2,1,0:T(8,128)(2,1)S(1)} %collective-permute-done.13.refs_8_), channel_id=1, source_target_pairs={{128,0},{256,128},{384,256},{512,384},{640,512},{768,640},{896,768... | collective-permute-start | bytes 786440 | tf_op jit(solution)/shard_map/ppermute | solution.py:183
  78.9 1.0 pad_maximum_fusion.1
  79.9 7.8 %collective-permute-done.2.refs_1_ = bf16[256,512]{1,0:T(8,128)(2,1)S(1)} collective-permute-done((bf16[256,512]{1,0:T(8,128)(2,1)}, bf16[256,512]{1,0:T(8,128)(2,1)S(1)}, u32[]{:S(2)}, u32[]{:S(2)}) %collective-permute-start.2) | collective-permute-done | bytes 262176 | tf_op jit(solution)/shard_map/ppermute | solution.py:244
  87.7 2.4 %collective-permute-start.18 = (bf16[3,4,2,32,512]{4,3,2,1,0:T(8,128)(2,1)}, bf16[3,4,2,32,512]{4,3,2,1,0:T(8,128)(2,1)}, u32[]{:S(2)}, u32[]{:S(2)}) collective-permute-start(bf16[3,4,2,32,512]{4,3,2,1,0:T(8,128)(2,1)} %pad_maximum_fusion.1), channel_id=1, source_target_pairs={{0,8},{8,0},{1,9},{9,1},{2,10},{10,2},{3,11},{11,3},{4,12},{12,4},... | collective-permute-start | bytes 2359304 | tf_op jit(solution)/shard_map/ppermute | solution.py:260
  90.0 0.0 collective-permute-done.3.refs_2_
  90.1 1.0 pad_maximum_fusion
  91.0 1.9 %collective-permute-start.5 = (bf16[3,256,512]{2,1,0:T(8,128)(2,1)}, bf16[3,256,512]{2,1,0:T(8,128)(2,1)S(1)}, u32[]{:S(2)}, u32[]{:S(2)}) collective-permute-start(bf16[3,256,512]{2,1,0:T(8,128)(2,1)} %pad_maximum_fusion), channel_id=1, source_target_pairs={{0,1},{1,0},{2,3},{3,2},{4,5},{5,4},{6,7},{7,6},{8,9},{9,8},{10,11... | collective-permute-start | bytes 2359304 | tf_op jit(solution)/shard_map/ppermute | solution.py:244
  93.0 0.0 collective-permute-done.11.refs_9_
  93.0 0.0 copy-start.10
  93.0 1.9 %collective-permute-start.12 = (bf16[4,2,32,512]{3,2,1,0:T(8,128)(2,1)S(1)}, bf16[4,2,32,512]{3,2,1,0:T(8,128)(2,1)S(1)}, u32[]{:S(2)}, u32[]{:S(2)}) collective-permute-start(bf16[4,2,32,512]{3,2,1,0:T(8,128)(2,1)S(1)} %collective-permute-done.11.refs_9_), channel_id=1, source_target_pairs={{896,0},{0,128},{128,256},{256,384},{384,512},{512,640},{640,768},... | collective-permute-start | bytes 786440 | tf_op jit(solution)/shard_map/ppermute | solution.py:183
  94.9 0.0 collective-permute-done.14.refs_10_
  94.9 4.6 %collective-permute-start.15 = (bf16[4,2,32,512]{3,2,1,0:T(8,128)(2,1)S(1)}, bf16[4,2,32,512]{3,2,1,0:T(8,128)(2,1)S(1)}, u32[]{:S(2)}, u32[]{:S(2)}) collective-permute-start(bf16[4,2,32,512]{3,2,1,0:T(8,128)(2,1)S(1)} %collective-permute-done.14.refs_10_), channel_id=1, source_target_pairs={{128,0},{256,128},{384,256},{512,384},{640,512},{768,640},{896,768... | collective-permute-start | bytes 786440 | tf_op jit(solution)/shard_map/ppermute | solution.py:183
  99.5 0.0 collective-permute-done.17.refs_11_
  99.5 0.0 copy-start.9
  99.5 1.0 pad_maximum_fusion.2
  100.5 0.0 copy-done.10
  100.5 2.5 %collective-permute-start.19 = (bf16[3,4,2,32,512]{4,3,2,1,0:T(8,128)(2,1)}, bf16[3,4,2,32,512]{4,3,2,1,0:T(8,128)(2,1)}, u32[]{:S(2)}, u32[]{:S(2)}) collective-permute-start(bf16[3,4,2,32,512]{4,3,2,1,0:T(8,128)(2,1)} %pad_maximum_fusion.2), channel_id=1, source_target_pairs={{0,8},{8,0},{1,9},{9,1},{2,10},{10,2},{3,11},{11,3},{4,12},{12,4},... | collective-permute-start | bytes 2359304 | tf_op jit(solution)/shard_map/ppermute | solution.py:260
  103.0 0.8 collective-permute-done.12.refs_6_
  103.9 0.0 copy-done.2
  103.9 1.9 %collective-permute-start.4 = (bf16[256,512]{1,0:T(8,128)(2,1)S(1)}, bf16[256,512]{1,0:T(8,128)(2,1)S(1)}, u32[]{:S(2)}, u32[]{:S(2)}) collective-permute-start(bf16[256,512]{1,0:T(8,128)(2,1)S(1)} %collective-permute-done.2.refs_1_), channel_id=1, source_target_pairs={{0,2},{1,3},{2,0},{3,1},{4,6},{5,7},{6,4},{7,5},{8,10},{9,11},{10,... | collective-permute-start | bytes 786440 | tf_op jit(solution)/shard_map/ppermute | solution.py:244
  105.8 0.0 collective-permute-done.15.refs_7_
  105.8 0.1 pad_maximum_fusion.3
  105.9 0.0 copy-done.12
  105.9 0.6 copy-done.13
  106.5 3.3 %collective-permute-start.16 = (bf16[2,4,2,32,512]{4,3,2,1,0:T(8,128)(2,1)S(1)}, bf16[2,4,2,32,512]{4,3,2,1,0:T(8,128)(2,1)S(1)}, u32[]{:S(2)}, u32[]{:S(2)}) collective-permute-start(bf16[2,4,2,32,512]{4,3,2,1,0:T(8,128)(2,1)S(1)} %pad_maximum_fusion.3), channel_id=1, source_target_pairs={{0,8},{8,0},{1,9},{9,1},{2,10},{10,2},{3,11},{11,3},{4,12},{12,4},... | collective-permute-start | bytes 1572872 | tf_op jit(solution)/shard_map/ppermute | solution.py:260
  109.8 9.5 %collective-permute-done.4.refs_3_ = bf16[256,512]{1,0:T(8,128)(2,1)S(1)} collective-permute-done((bf16[256,512]{1,0:T(8,128)(2,1)S(1)}, bf16[256,512]{1,0:T(8,128)(2,1)S(1)}, u32[]{:S(2)}, u32[]{:S(2)}) %collective-permute-start.4) | collective-permute-done | bytes 262176 | tf_op jit(solution)/shard_map/ppermute | solution.py:244
  119.3 1.9 %collective-permute-start.6 = (bf16[256,512]{1,0:T(8,128)(2,1)S(1)}, bf16[256,512]{1,0:T(8,128)(2,1)S(1)}, u32[]{:S(2)}, u32[]{:S(2)}) collective-permute-start(bf16[256,512]{1,0:T(8,128)(2,1)S(1)} %collective-permute-done.4.refs_3_), channel_id=1, source_target_pairs={{0,1},{1,0},{2,3},{3,2},{4,5},{5,4},{6,7},{7,6},{8,9},{9,8},{10,11... | collective-permute-start | bytes 786440 | tf_op jit(solution)/shard_map/ppermute | solution.py:244
  121.3 0.7 stack.103.place
  121.9 5.4 %collective-permute-done.6.refs_5_ = bf16[256,512]{1,0:T(8,128)(2,1)S(1)} collective-permute-done((bf16[256,512]{1,0:T(8,128)(2,1)S(1)}, bf16[256,512]{1,0:T(8,128)(2,1)S(1)}, u32[]{:S(2)}, u32[]{:S(2)}) %collective-permute-start.6) | collective-permute-done | bytes 262176 | tf_op jit(solution)/shard_map/ppermute | solution.py:244
  127.4 0.0 collective-permute-done.18.refs_12_
  127.4 0.0 collective-permute-done.5.refs_4_
  127.4 0.0 collective-permute-done.19.refs_13_
  127.4 0.6 copy-done.6
  128.1 0.3 copy-done.1
  128.3 6.1 %project.2.refs_9_ = f32[256,512]{1,0:T(8,128)} custom-call(s32[5]{0:T(128)} %stack.103.place, bf16[256,512]{1,0:T(8,128)(2,1)} %early.1.refs_0_, bf16[256,512]{1,0:T(8,128)(2,1)} %copy-done.2, bf16[256,512]{1,0:T(8,128)(2,1)} %copy-done.3, bf16[256,512]{1,0:T(8,128)(2,1)} %copy-done.5, bf16[3,256,512]{2,1,0:T(8,128)(2,1)} %copy-done.1, ...), custom_call_target="tpu_custom_call" | custom-call | flops 805306368 | bytes 8000000 | tf_op jit(solution)/shard_map/project/pallas_call | solution.py:266
  134.4 0.0 collective-permute-done.16.refs_8_
  134.5 0.8 copy-done.14
  135.2 4.4 %project.3 = bf16[256,512]{1,0:T(8,128)(2,1)} custom-call(s32[5]{0:T(128)} %stack.103.place, bf16[256,512]{1,0:T(8,128)(2,1)} %early.1.refs_0_, bf16[256,512]{1,0:T(8,128)(2,1)} %copy-done.2, bf16[256,512]{1,0:T(8,128)(2,1)} %copy-done.3, bf16[256,512]{1,0:T(8,128)(2,1)} %copy-done.5, bf16[3,256,512]{2,1,0:T(8,128)(2,1)} %copy-done.1, ...), custom_call_target="tpu_custom_call" | custom-call | flops 268435456 | bytes 8000000 | tf_op jit(solution)/shard_map/project/pallas_call | solution.py:266
  (23 shorter events, 0.1 us)
Async XLA Ops:
  0.0 30.1 %collective-permute-start.1 = (bf16[32,512]{1,0:T(8,128)(2,1)}, bf16[32,512]{1,0:T(8,128)(2,1)S(1)}, u32[]{:S(2)}, u32[]{:S(2)}) collective-permute-start(bf16[32,512]{1,0:T(8,128)(2,1)} %param.13), channel_id=1, source_target_pairs={{0,64},{64,0},{1,65},{65,1},{2,66},{66,2},{3,67},{67,3},{4,68},{68... | collective-permute-start | bytes 98312 | tf_op jit(solution)/shard_map/ppermute | solution.py:202
  23.5 30.1 %collective-permute-start = (bf16[176,512]{1,0:T(8,128)(2,1)}, bf16[176,512]{1,0:T(8,128)(2,1)S(1)}, u32[]{:S(2)}, u32[]{:S(2)}) collective-permute-start(bf16[176,512]{1,0:T(8,128)(2,1)} %get-tuple-element.12), channel_id=1, source_target_pairs={{0,8},{8,16},{16,24},{24,32},{32,40},{40,48},{48,56},{56,64},{64,7... | collective-permute-start | bytes 540680 | tf_op jit(solution)/shard_map/ppermute | solution.py:212
  27.4 2.7 %copy-start.16 = (bf16[32,512]{1,0:T(8,128)(2,1)S(1)}, bf16[32,512]{1,0:T(8,128)(2,1)}, u32[]{:S(2)}) copy-start(bf16[32,512]{1,0:T(8,128)(2,1)} %param.13) | copy-start | bytes 98308
  30.2 13.2 %collective-permute-start.7 = (bf16[2,32,512]{2,1,0:T(8,128)(2,1)S(1)}, bf16[2,32,512]{2,1,0:T(8,128)(2,1)S(1)}, u32[]{:S(2)}, u32[]{:S(2)}) collective-permute-start(bf16[2,32,512]{2,1,0:T(8,128)(2,1)S(1)} %maximum_select_fusion.1), channel_id=1, source_target_pairs={{16,0},{32,16},{48,32},{0,48},{17,1},{33,17},{49,33},{1,49},{18,2}... | collective-permute-start | bytes 196616 | tf_op jit(solution)/shard_map/ppermute | solution.py:230
  38.9 6.5 %collective-permute-start.8 = (bf16[2,32,512]{2,1,0:T(8,128)(2,1)S(1)}, bf16[2,32,512]{2,1,0:T(8,128)(2,1)S(1)}, u32[]{:S(2)}, u32[]{:S(2)}) collective-permute-start(bf16[2,32,512]{2,1,0:T(8,128)(2,1)S(1)} %maximum_select_fusion.1), channel_id=1, source_target_pairs={{32,0},{48,16},{0,32},{16,48},{33,1},{49,17},{1,33},{17,49},{34,2}... | collective-permute-start | bytes 196616 | tf_op jit(solution)/shard_map/ppermute | solution.py:230
  40.8 6.2 %collective-permute-start.9 = (bf16[2,32,512]{2,1,0:T(8,128)(2,1)S(1)}, bf16[2,32,512]{2,1,0:T(8,128)(2,1)S(1)}, u32[]{:S(2)}, u32[]{:S(2)}) collective-permute-start(bf16[2,32,512]{2,1,0:T(8,128)(2,1)S(1)} %maximum_select_fusion.1), channel_id=1, source_target_pairs={{48,0},{0,16},{16,32},{32,48},{49,1},{1,17},{17,33},{33,49},{50,2}... | collective-permute-start | bytes 196616 | tf_op jit(solution)/shard_map/ppermute | solution.py:230
  47.1 18.3 %copy-start.4 = (bf16[4,2,32,512]{3,2,1,0:T(8,128)(2,1)}, bf16[4,2,32,512]{3,2,1,0:T(8,128)(2,1)S(1)}, u32[]{:S(2)}) copy-start(bf16[4,2,32,512]{3,2,1,0:T(8,128)(2,1)S(1)} %get-tuple-element.20.refs_6_) | copy-start | bytes 786436
  47.1 25.3 %collective-permute-start.10 = (bf16[4,2,32,512]{3,2,1,0:T(8,128)(2,1)S(1)}, bf16[4,2,32,512]{3,2,1,0:T(8,128)(2,1)S(1)}, u32[]{:S(2)}, u32[]{:S(2)}) collective-permute-start(bf16[4,2,32,512]{3,2,1,0:T(8,128)(2,1)S(1)} %get-tuple-element.20.refs_6_), channel_id=1, source_target_pairs={{896,0},{0,128},{128,256},{256,384},{384,512},{512,640},{640,768},... | collective-permute-start | bytes 786440 | tf_op jit(solution)/shard_map/ppermute | solution.py:183
  49.0 25.3 %collective-permute-start.13 = (bf16[4,2,32,512]{3,2,1,0:T(8,128)(2,1)S(1)}, bf16[4,2,32,512]{3,2,1,0:T(8,128)(2,1)S(1)}, u32[]{:S(2)}, u32[]{:S(2)}) collective-permute-start(bf16[4,2,32,512]{3,2,1,0:T(8,128)(2,1)S(1)} %get-tuple-element.20.refs_6_), channel_id=1, source_target_pairs={{128,0},{256,128},{384,256},{512,384},{640,512},{768,640},{896,768... | collective-permute-start | bytes 786440 | tf_op jit(solution)/shard_map/ppermute | solution.py:183
  53.6 0.7 copy-start.15
  57.9 29.8 %collective-permute-start.2 = (bf16[256,512]{1,0:T(8,128)(2,1)}, bf16[256,512]{1,0:T(8,128)(2,1)S(1)}, u32[]{:S(2)}, u32[]{:S(2)}) collective-permute-start(bf16[256,512]{1,0:T(8,128)(2,1)} %early.1.refs_0_), channel_id=1, source_target_pairs={{0,4},{1,5},{2,6},{3,7},{4,0},{5,1},{6,2},{7,3},{8,12},{9,13},{10,... | collective-permute-start | bytes 786440 | tf_op jit(solution)/shard_map/ppermute | solution.py:244
  61.4 28.7 %collective-permute-start.3 = (bf16[256,512]{1,0:T(8,128)(2,1)}, bf16[256,512]{1,0:T(8,128)(2,1)S(1)}, u32[]{:S(2)}, u32[]{:S(2)}) collective-permute-start(bf16[256,512]{1,0:T(8,128)(2,1)} %early.1.refs_0_), channel_id=1, source_target_pairs={{0,2},{1,3},{2,0},{3,1},{4,6},{5,7},{6,4},{7,5},{8,10},{9,11},{10,... | collective-permute-start | bytes 786440 | tf_op jit(solution)/shard_map/ppermute | solution.py:244
  65.4 34.1 %collective-permute-start.17 = (bf16[4,2,32,512]{3,2,1,0:T(8,128)(2,1)S(1)}, bf16[4,2,32,512]{3,2,1,0:T(8,128)(2,1)S(1)}, u32[]{:S(2)}, u32[]{:S(2)}) collective-permute-start(bf16[4,2,32,512]{3,2,1,0:T(8,128)(2,1)S(1)} %get-tuple-element.20.refs_6_), channel_id=1, source_target_pairs={{512,0},{640,128},{768,256},{896,384},{0,512},{128,640},{256,768},... | collective-permute-start | bytes 786440 | tf_op jit(solution)/shard_map/ppermute | solution.py:183
  72.4 7.5 %copy-start.7 = (bf16[4,2,32,512]{3,2,1,0:T(8,128)(2,1)}, bf16[4,2,32,512]{3,2,1,0:T(8,128)(2,1)S(1)}, u32[]{:S(2)}) copy-start(bf16[4,2,32,512]{3,2,1,0:T(8,128)(2,1)S(1)} %collective-permute-done.10.refs_7_) | copy-start | bytes 786436
  72.4 20.6 %collective-permute-start.11 = (bf16[4,2,32,512]{3,2,1,0:T(8,128)(2,1)S(1)}, bf16[4,2,32,512]{3,2,1,0:T(8,128)(2,1)S(1)}, u32[]{:S(2)}, u32[]{:S(2)}) collective-permute-start(bf16[4,2,32,512]{3,2,1,0:T(8,128)(2,1)S(1)} %collective-permute-done.10.refs_7_), channel_id=1, source_target_pairs={{896,0},{0,128},{128,256},{256,384},{384,512},{512,640},{640,768},... | collective-permute-start | bytes 786440 | tf_op jit(solution)/shard_map/ppermute | solution.py:183
  74.3 5.6 %copy-start.8 = (bf16[4,2,32,512]{3,2,1,0:T(8,128)(2,1)}, bf16[4,2,32,512]{3,2,1,0:T(8,128)(2,1)S(1)}, u32[]{:S(2)}) copy-start(bf16[4,2,32,512]{3,2,1,0:T(8,128)(2,1)S(1)} %collective-permute-done.13.refs_8_) | copy-start | bytes 786436
  74.3 20.6 %collective-permute-start.14 = (bf16[4,2,32,512]{3,2,1,0:T(8,128)(2,1)S(1)}, bf16[4,2,32,512]{3,2,1,0:T(8,128)(2,1)S(1)}, u32[]{:S(2)}, u32[]{:S(2)}) collective-permute-start(bf16[4,2,32,512]{3,2,1,0:T(8,128)(2,1)S(1)} %collective-permute-done.13.refs_8_), channel_id=1, source_target_pairs={{128,0},{256,128},{384,256},{512,384},{640,512},{768,640},{896,768... | collective-permute-start | bytes 786440 | tf_op jit(solution)/shard_map/ppermute | solution.py:183
  78.9 11.1 %copy-start = (bf16[256,512]{1,0:T(8,128)(2,1)S(1)}, bf16[256,512]{1,0:T(8,128)(2,1)}, u32[]{:S(2)}) copy-start(bf16[256,512]{1,0:T(8,128)(2,1)} %early.1.refs_0_) | copy-start | bytes 786436
  87.7 16.2 %copy-start.2 = (bf16[256,512]{1,0:T(8,128)(2,1)}, bf16[256,512]{1,0:T(8,128)(2,1)S(1)}, u32[]{:S(2)}) copy-start(bf16[256,512]{1,0:T(8,128)(2,1)S(1)} %collective-permute-done.2.refs_1_) | copy-start | bytes 786436
  87.7 39.7 %collective-permute-start.18 = (bf16[3,4,2,32,512]{4,3,2,1,0:T(8,128)(2,1)}, bf16[3,4,2,32,512]{4,3,2,1,0:T(8,128)(2,1)}, u32[]{:S(2)}, u32[]{:S(2)}) collective-permute-start(bf16[3,4,2,32,512]{4,3,2,1,0:T(8,128)(2,1)} %pad_maximum_fusion.1), channel_id=1, source_target_pairs={{0,8},{8,0},{1,9},{9,1},{2,10},{10,2},{3,11},{11,3},{4,12},{12,4},... | collective-permute-start | bytes 2359304 | tf_op jit(solution)/shard_map/ppermute | solution.py:260
  90.0 1.0 copy-start.3
  91.0 36.3 %collective-permute-start.5 = (bf16[3,256,512]{2,1,0:T(8,128)(2,1)}, bf16[3,256,512]{2,1,0:T(8,128)(2,1)S(1)}, u32[]{:S(2)}, u32[]{:S(2)}) collective-permute-start(bf16[3,256,512]{2,1,0:T(8,128)(2,1)} %pad_maximum_fusion), channel_id=1, source_target_pairs={{0,1},{1,0},{2,3},{3,2},{4,5},{5,4},{6,7},{7,6},{8,9},{9,8},{10,11... | collective-permute-start | bytes 2359304 | tf_op jit(solution)/shard_map/ppermute | solution.py:244
  93.0 7.5 %copy-start.10 = (bf16[4,2,32,512]{3,2,1,0:T(8,128)(2,1)}, bf16[4,2,32,512]{3,2,1,0:T(8,128)(2,1)S(1)}, u32[]{:S(2)}) copy-start(bf16[4,2,32,512]{3,2,1,0:T(8,128)(2,1)S(1)} %collective-permute-done.11.refs_9_) | copy-start | bytes 786436
  93.0 10.9 %collective-permute-start.12 = (bf16[4,2,32,512]{3,2,1,0:T(8,128)(2,1)S(1)}, bf16[4,2,32,512]{3,2,1,0:T(8,128)(2,1)S(1)}, u32[]{:S(2)}, u32[]{:S(2)}) collective-permute-start(bf16[4,2,32,512]{3,2,1,0:T(8,128)(2,1)S(1)} %collective-permute-done.11.refs_9_), channel_id=1, source_target_pairs={{896,0},{0,128},{128,256},{256,384},{384,512},{512,640},{640,768},... | collective-permute-start | bytes 786440 | tf_op jit(solution)/shard_map/ppermute | solution.py:183
  94.9 5.6 %copy-start.11 = (bf16[4,2,32,512]{3,2,1,0:T(8,128)(2,1)}, bf16[4,2,32,512]{3,2,1,0:T(8,128)(2,1)S(1)}, u32[]{:S(2)}) copy-start(bf16[4,2,32,512]{3,2,1,0:T(8,128)(2,1)S(1)} %collective-permute-done.14.refs_10_) | copy-start | bytes 786436
  94.9 10.9 %collective-permute-start.15 = (bf16[4,2,32,512]{3,2,1,0:T(8,128)(2,1)S(1)}, bf16[4,2,32,512]{3,2,1,0:T(8,128)(2,1)S(1)}, u32[]{:S(2)}, u32[]{:S(2)}) collective-permute-start(bf16[4,2,32,512]{3,2,1,0:T(8,128)(2,1)S(1)} %collective-permute-done.14.refs_10_), channel_id=1, source_target_pairs={{128,0},{256,128},{384,256},{512,384},{640,512},{768,640},{896,768... | collective-permute-start | bytes 786440 | tf_op jit(solution)/shard_map/ppermute | solution.py:183
  99.5 1.0 copy-start.9
  100.5 26.9 %collective-permute-start.19 = (bf16[3,4,2,32,512]{4,3,2,1,0:T(8,128)(2,1)}, bf16[3,4,2,32,512]{4,3,2,1,0:T(8,128)(2,1)}, u32[]{:S(2)}, u32[]{:S(2)}) collective-permute-start(bf16[3,4,2,32,512]{4,3,2,1,0:T(8,128)(2,1)} %pad_maximum_fusion.2), channel_id=1, source_target_pairs={{0,8},{8,0},{1,9},{9,1},{2,10},{10,2},{3,11},{11,3},{4,12},{12,4},... | collective-permute-start | bytes 2359304 | tf_op jit(solution)/shard_map/ppermute | solution.py:260
  103.9 2.0 %copy-start.12 = (bf16[4,2,32,512]{3,2,1,0:T(8,128)(2,1)}, bf16[4,2,32,512]{3,2,1,0:T(8,128)(2,1)S(1)}, u32[]{:S(2)}) copy-start(bf16[4,2,32,512]{3,2,1,0:T(8,128)(2,1)S(1)} %collective-permute-done.12.refs_6_) | copy-start | bytes 786436
  103.9 15.4 %collective-permute-start.4 = (bf16[256,512]{1,0:T(8,128)(2,1)S(1)}, bf16[256,512]{1,0:T(8,128)(2,1)S(1)}, u32[]{:S(2)}, u32[]{:S(2)}) collective-permute-start(bf16[256,512]{1,0:T(8,128)(2,1)S(1)} %collective-permute-done.2.refs_1_), channel_id=1, source_target_pairs={{0,2},{1,3},{2,0},{3,1},{4,6},{5,7},{6,4},{7,5},{8,10},{9,11},{10,... | collective-permute-start | bytes 786440 | tf_op jit(solution)/shard_map/ppermute | solution.py:244
  105.8 0.7 copy-start.13
  106.5 27.9 %collective-permute-start.16 = (bf16[2,4,2,32,512]{4,3,2,1,0:T(8,128)(2,1)S(1)}, bf16[2,4,2,32,512]{4,3,2,1,0:T(8,128)(2,1)S(1)}, u32[]{:S(2)}, u32[]{:S(2)}) collective-permute-start(bf16[2,4,2,32,512]{4,3,2,1,0:T(8,128)(2,1)S(1)} %pad_maximum_fusion.3), channel_id=1, source_target_pairs={{0,8},{8,0},{1,9},{9,1},{2,10},{10,2},{3,11},{11,3},{4,12},{12,4},... | collective-permute-start | bytes 1572872 | tf_op jit(solution)/shard_map/ppermute | solution.py:260
  119.3 8.1 %copy-start.5 = (bf16[256,512]{1,0:T(8,128)(2,1)}, bf16[256,512]{1,0:T(8,128)(2,1)S(1)}, u32[]{:S(2)}) copy-start(bf16[256,512]{1,0:T(8,128)(2,1)S(1)} %collective-permute-done.4.refs_3_) | copy-start | bytes 786436
  119.3 8.0 %collective-permute-start.6 = (bf16[256,512]{1,0:T(8,128)(2,1)S(1)}, bf16[256,512]{1,0:T(8,128)(2,1)S(1)}, u32[]{:S(2)}, u32[]{:S(2)}) collective-permute-start(bf16[256,512]{1,0:T(8,128)(2,1)S(1)} %collective-permute-done.4.refs_3_), channel_id=1, source_target_pairs={{0,1},{1,0},{2,3},{3,2},{4,5},{5,4},{6,7},{7,6},{8,9},{9,8},{10,11... | collective-permute-start | bytes 786440 | tf_op jit(solution)/shard_map/ppermute | solution.py:244
  127.4 0.7 copy-start.6
  127.4 1.0 copy-start.1
  134.5 0.8 copy-start.14

commit v4 on v2

--- a/solution.py
+++ b/solution.py
@@ -11,7 +11,6 @@
 HALF = 128
 HEAD = 144
 TAIL = 16
-WROWS = 32
 PACK = HALF + 3 * TAIL
 
 F32 = jnp.float32
@@ -124,55 +123,42 @@
         out[pl.ds(at, count), :] = value.astype(BF16)
 
 
-def arrange_kernel(place, mine, over, *refs):
-    arrived, out = refs[:3], refs[3]
-    zh, x = place[1], place[3]
-    for rel in range(4):
-        for other in range(2):
-            piece = (mine, over)[other][...] if rel == 0 else arrived[rel - 1][other]
-            out[lax.rem(zh + other, 2), lax.rem(x + rel, 4)] = piece
-
-
-ORDER = ((0, 7, 1), (6, 2), (5, 3, 4))
-
-
-def final_kernel(place, own, four, two, six, odd, seven, residual, *refs):
-    weights, swapped = refs[:8], refs[8:11]
-    out, gv, wv, gsem, wsem = refs[11:]
-    me, y, core = place[0], place[2], place[4]
+FIRST = (0, 7, 1, 6, 2)
+LAST = (5, 3, 4)
+
+
+def most_kernel(place, own, four, two, six, odd, seven, residual, *refs):
+    weights, (out, kept, gv, wv, gsem, wsem) = refs[:5], refs[5:]
+    me, y = place[0], place[1]
     pieces = [(own, 0), (four, 4), (two, 2), (six, 6), (seven, 7)]
     pieces += [(odd.at[i], by) for i, by in enumerate((1, 5, 3))]
     gated = [
         pltpu.make_async_copy(piece, gv.at[lax.bitwise_xor(me, by)], gsem.at[by])
         for piece, by in pieces
     ]
-    rows = []
-    for batch, order in enumerate(ORDER):
-        for i, by in enumerate(order):
-            at = lax.rem(y + by, 8)
-            rows.append(
-                [
-                    pltpu.make_async_copy(
-                        weights[by], wv.at[at, :, :, core], wsem.at[by, 0]
-                    ),
-                    pltpu.make_async_copy(
-                        swapped[batch].at[i], wv.at[at, :, :, 1 - core], wsem.at[by, 1]
-                    ),
-                ]
-            )
-    for copy in gated:
+    rows = [pltpu.make_async_copy(w, wv.at[n], wsem.at[n]) for n, w in enumerate(weights)]
+    for copy in gated + rows:
         copy.start()
-    for pair in rows:
-        for copy in pair:
-            copy.start()
     total = residual[...].astype(F32)
     for copy in gated:
         copy.wait()
-    for by, pair in zip(sum(ORDER, ()), rows):
-        for copy in pair:
-            copy.wait()
-        k = lax.rem(y + by, 8)
-        total = total + dot(gv[k], wv[k].reshape(512, 512))
+    for n, by in enumerate(LAST):
+        kept[n] = gv[lax.rem(y + by, 8)]
+    for n, by in enumerate(FIRST):
+        rows[n].wait()
+        total = total + dot(gv[lax.rem(y + by, 8)], wv[n])
+    out[...] = total
+
+
+def rest_kernel(start, kept, *refs):
+    weights, (out, wv, wsem) = refs[:3], refs[3:]
+    rows = [pltpu.make_async_copy(w, wv.at[n], wsem.at[n]) for n, w in enumerate(weights)]
+    for copy in rows:
+        copy.start()
+    total = start[...]
+    for n, copy in enumerate(rows):
+        copy.wait()
+        total = total + dot(kept[n], wv[n])
     out[...] = total.astype(BF16)
 
 
@@ -185,14 +171,15 @@
 
 
 def around_y(own):
-    up, down, ups, downs = own, own, [], []
+    def shift(piece, by):
+        return lax.ppermute(piece, "y", [((i + by) % 8, i) for i in range(8)])
+
+    blocks = {0: own}
     for step in range(4):
-        up = lax.ppermute(up, "y", [(i, (i + 1) % 8) for i in range(8)])
-        ups.append(up)
+        blocks[7 - step] = shift(blocks[(8 - step) % 8], 7)
         if step < 3:
-            down = lax.ppermute(down, "y", [((i + 1) % 8, i) for i in range(8)])
-            downs.append(down)
-    return [own] + downs + ups[::-1]
+            blocks[step + 1] = shift(blocks[step], 1)
+    return blocks
 
 
 def on_device(residual, proj, short_filter, medium_filter, skip, out_weight):
@@ -201,10 +188,10 @@
     p = jnp.transpose(proj, (1, 0, 2))
     sf = jnp.transpose(short_filter, (1, 0, 2))
     skip = skip.reshape(1, chans)
-    place = jnp.stack([lax.axis_index(a) for a in ("tp", "zh", "y", "x", "core")])
-    place = place.astype(jnp.int32)
-
-    over = lax.ppermute(out_weight, "zh", [(0, 1), (1, 0)])
+    place = jnp.stack([lax.axis_index("tp"), lax.axis_index("y")]).astype(jnp.int32)
+
+    mine = jnp.broadcast_to(out_weight, (16,) + out_weight.shape)
+    block = lax.all_to_all(mine, ("zh", "x", "core"), 0, 0).reshape(chans, chans)
 
     pack, prod, q = pl.pallas_call(
         local_kernel,
@@ -222,13 +209,6 @@
         cost_estimate=cost(300_000_000, 3_000_000),
         name="late",
     )(prod, q, medium_filter, skip, fwd, inv)
-
-    over, late = lax.optimization_barrier((over, late))
-
-    mine = jnp.stack([out_weight, over])
-    arrived = []
-    for by in (1, 2, 3):
-        arrived.append(lax.ppermute(mine, "x", [((i + by) % 4, i) for i in range(4)]))
 
     gated = pl.pallas_call(
         early_kernel,
@@ -253,34 +233,33 @@
     smem = pl.BlockSpec(memory_space=pltpu.SMEM)
     vmem = pl.BlockSpec(memory_space=pltpu.VMEM)
     anywhere = pl.BlockSpec(memory_space=pl.ANY)
-    block = pl.pallas_call(
-        arrange_kernel,
-        out_shape=sds((2, 4, WROWS, chans), BF16),
-        in_specs=[smem] + [vmem] * 5,
-        out_specs=vmem,
-        cost_estimate=cost(0, 500_000),
-        name="arrange",
-    )(place, out_weight, over, *arrived)
     weights = around_y(block)
-    swapped = []
-    for order in ORDER:
-        group = jnp.stack([weights[by] for by in order])
-        swapped.append(lax.ppermute(group, "core", [(0, 1), (1, 0)]))
-
+    most, kept = pl.pallas_call(
+        most_kernel,
+        out_shape=(sds((rows, chans), F32), sds((3, rows, chans), BF16)),
+        in_specs=[smem] + [anywhere] * 6 + [vmem] + [anywhere] * 5,
+        out_specs=(vmem, vmem),
+        scratch_shapes=[
+            pltpu.VMEM((8, rows, chans), BF16),
+            pltpu.VMEM((5, chans, chans), BF16),
+            pltpu.SemaphoreType.DMA((8,)),
+            pltpu.SemaphoreType.DMA((5,)),
+        ],
+        cost_estimate=cost(10 * rows * chans * chans, 6_000_000),
+        name="most",
+    )(place, gated, four, two, six, odd, seven, residual, *[weights[i] for i in FIRST])
     return pl.pallas_call(
-        final_kernel,
+        rest_kernel,
         out_shape=sds((rows, chans), BF16),
-        in_specs=[smem] + [anywhere] * 6 + [vmem] + [anywhere] * 11,
+        in_specs=[vmem, vmem] + [anywhere] * 3,
         out_specs=vmem,
         scratch_shapes=[
-            pltpu.VMEM((8, rows, chans), BF16),
-            pltpu.VMEM((8, 2, 4, 2, WROWS, chans), BF16),
-            pltpu.SemaphoreType.DMA((8,)),
-            pltpu.SemaphoreType.DMA((8, 2)),
+            pltpu.VMEM((3, chans, chans), BF16),
+            pltpu.SemaphoreType.DMA((3,)),
         ],
-        cost_estimate=cost(2 * rows * 8 * chans * chans, 8_000_000),
-        name="project",
-    )(place, gated, four, two, six, odd, seven, residual, *weights, *swapped)
+        cost_estimate=cost(6 * rows * chans * chans, 3_000_000),
+        name="rest",
+    )(most, kept, *[weights[i] for i in LAST])
 
 
 def solution(mesh):

time: 152 us -> 173 us (1.14)
  the two profiles are of different devices: /device:TPU:1 before, /device:TPU:24 now
where the time goes in v4:
time: 173 us; the launch traced here: 172 us
  starting transfers between devices  75.4 us (44%)
  blocking collectives  41 us (24%)
  waiting for transfers between devices  32.2 us (19%)
  Pallas kernels  18.7 us (11%)
  local copies, waits for them, and re-layouts  3.1 us (2%)
  other arithmetic  1.74 us (1%)
    ppermute x5, starting transfers between devices, exchange(): return lax.ppermute(piece, 'tp', [(i, i ^ by) for i in range(8)])  47.2 us
    all_to_all x1, blocking collectives, on_device(): lax.all_to_all(mine, ('zh', 'x', 'core'), 0, 0).reshape(chans, chans)  41 us
    ppermute x7, starting transfers between devices, shift(): return lax.ppermute(piece, 'y', [((i + by) % 8, i) for i in range(8)])  26.3 us
    ppermute x1, waiting for transfers between devices, on_device(): lax.ppermute(pack, ('y', 'zh', 'x', 'core'), [(i, i + 1) for i in range(1...  14.1 us
    ppermute x5, waiting for transfers between devices, exchange(): return lax.ppermute(piece, 'tp', [(i, i ^ by) for i in range(8)])  9.12 us
    ppermute x7, waiting for transfers between devices, shift(): return lax.ppermute(piece, 'y', [((i + by) % 8, i) for i in range(8)])  8.88 us
    pallas_call x1, Pallas kernels, on_device(): pl.pallas_call(most_kernel, out_shape=(sds((rows, chans), F32), sds((3, r...  5.11 us
    pallas_call x1, Pallas kernels, on_device(): pl.pallas_call(rest_kernel, out_shape=sds((rows, chans), BF16), in_specs=...  3.74 us
  transfers between devices with their start and end apart: 13, of which 5 were waited for; matrix products, arithmetic and copies ran while one was open for 1% of the time, Pallas kernels for 9%

profile of v4, /device:TPU:24, one launch (start us, length us, event | category | flops | bytes accessed | tf_op | source)
XLA Modules:
  0.0 172.4 jit_solution(4252977324034255770)
XLA Ops:
  0.0 0.8 broadcast_in_dim.3
  0.8 41.0 %all_to_all.5 = bf16[16,32,512]{2,1,0:T(8,128)(2,1)S(1)} all-to-all(bf16[16,32,512]{2,1,0:T(8,128)(2,1)S(1)} %broadcast_in_dim.3), channel_id=1, replica_groups=mesh['y'=8,'zh'=2,'x'=4,'core'=2,'tp'=8] {'zh','x','core'}, dimensions={0} | all-to-all | bytes 1048576 | tf_op jit(solution)/shard_map/all_to_all | solution.py:194
  41.8 0.0 copy-start
  41.8 4.7 %collective-permute-start.6 = (bf16[512,512]{1,0:T(8,128)(2,1)S(1)}, bf16[512,512]{1,0:T(8,128)(2,1)S(1)}, u32[]{:S(2)}, u32[]{:S(2)}) collective-permute-start(bf16[512,512]{1,0:T(8,128)(2,1)S(1)} %bitcast.12), channel_id=1, source_target_pairs={{896,0},{0,128},{128,256},{256,384},{384,512},{512,640},{640,768},... | collective-permute-start | bytes 1572872 | tf_op jit(solution)/shard_map/ppermute | solution.py:175
  46.5 1.9 %collective-permute-start.7 = (bf16[512,512]{1,0:T(8,128)(2,1)S(1)}, bf16[512,512]{1,0:T(8,128)(2,1)}, u32[]{:S(2)}, u32[]{:S(2)}) collective-permute-start(bf16[512,512]{1,0:T(8,128)(2,1)S(1)} %bitcast.13), channel_id=1, source_target_pairs={{128,0},{256,128},{384,256},{512,384},{640,512},{768,640},{896,768... | collective-permute-start | bytes 1572872 | tf_op jit(solution)/shard_map/ppermute | solution.py:175
  48.5 8.9 %collective-permute-done.6.refs_1_ = bf16[512,512]{1,0:T(8,128)(2,1)S(1)} collective-permute-done((bf16[512,512]{1,0:T(8,128)(2,1)S(1)}, bf16[512,512]{1,0:T(8,128)(2,1)S(1)}, u32[]{:S(2)}, u32[]{:S(2)}) %collective-permute-start.6) | collective-permute-done | bytes 524320 | tf_op jit(solution)/shard_map/ppermute | solution.py:175
  57.3 0.0 copy-start.4
  57.3 5.6 %collective-permute-start.8 = (bf16[512,512]{1,0:T(8,128)(2,1)S(1)}, bf16[512,512]{1,0:T(8,128)(2,1)}, u32[]{:S(2)}, u32[]{:S(2)}) collective-permute-start(bf16[512,512]{1,0:T(8,128)(2,1)S(1)} %collective-permute-done.6.refs_1_), channel_id=1, source_target_pairs={{896,0},{0,128},{128,256},{256,384},{384,512},{512,640},{640,768},... | collective-permute-start | bytes 1572872 | tf_op jit(solution)/shard_map/ppermute | solution.py:175
  62.9 3.6 %local.1 = (bf16[176,512]{1,0:T(8,128)(2,1)}, bf16[256,512]{1,0:T(8,128)(2,1)}, f32[256,512]{1,0:T(8,128)}) custom-call(bf16[3,256,512]{2,1,0:T(8,128)(2,1)} %bitcast.9, bf16[3,7,512]{2,1,0:T(8,128)(2,1)} %bitcast.17), custom_call_target="tpu_custom_call" | custom-call | flops 6000000 | bytes 2000000 | tf_op jit(solution)/shard_map/local/pallas_call | solution.py:196
  66.5 1.9 %collective-permute-start = (bf16[176,512]{1,0:T(8,128)(2,1)}, bf16[176,512]{1,0:T(8,128)(2,1)S(1)}, u32[]{:S(2)}, u32[]{:S(2)}) collective-permute-start(bf16[176,512]{1,0:T(8,128)(2,1)} %get-tuple-element.12), channel_id=1, source_target_pairs={{0,8},{8,16},{16,24},{24,32},{32,40},{40,48},{48,56},{56,64},{64,7... | collective-permute-start | bytes 540680 | tf_op jit(solution)/shard_map/ppermute | solution.py:204
  68.4 2.7 %late.1 = (bf16[112,512]{1,0:T(8,128)(2,1)}, f32[256,512]{1,0:T(8,128)}) custom-call(bf16[256,512]{1,0:T(8,128)(2,1)} %get-tuple-element.13.prod, f32[256,512]{1,0:T(8,128)} %get-tuple-element.14.q, bf16[128,512]{1,0:T(8,128)(2,1)} %mf.1, f32[1,512]{1,0:T(1,128)} %bitcast.19, bf16[512,256]{1,0:T(8,128)(2,1)} %constant.11.clone.fwd, ...), custom_call_target="tpu_custom_call" | custom-call | flops 300000000 | bytes 3000000 | tf_op jit(solution)/shard_map/late/pallas_call | solution.py:206
  71.1 0.0 copy-done
  71.1 0.0 copy-done.4
  71.1 14.1 %collective-permute-done.halo = bf16[176,512]{1,0:T(8,128)(2,1)S(1)} collective-permute-done((bf16[176,512]{1,0:T(8,128)(2,1)}, bf16[176,512]{1,0:T(8,128)(2,1)S(1)}, u32[]{:S(2)}, u32[]{:S(2)}) %collective-permute-start) | collective-permute-done | bytes 180256 | tf_op jit(solution)/shard_map/ppermute | solution.py:204
  85.3 0.0 copy-start.9
  85.3 0.7 copy-done.9
  85.9 3.6 %early.1.own = bf16[256,512]{1,0:T(8,128)(2,1)} custom-call(bf16[3,256,512]{2,1,0:T(8,128)(2,1)} %bitcast.10, bf16[176,512]{1,0:T(8,128)(2,1)} %copy-done.9, bf16[3,7,512]{2,1,0:T(8,128)(2,1)} %bitcast.18, bf16[256,512]{1,0:T(8,128)(2,1)} %get-tuple-element.13.prod, f32[256,512]{1,0:T(8,128)} %get-tuple-element.14.q, ...), custom_call_target="tpu_custom_call" | custom-call | flops 600000000 | bytes 3000000 | tf_op jit(solution)/shard_map/early/pallas_call | solution.py:213
  89.6 17.9 %collective-permute-start.1 = (bf16[256,512]{1,0:T(8,128)(2,1)}, bf16[256,512]{1,0:T(8,128)(2,1)S(1)}, u32[]{:S(2)}, u32[]{:S(2)}) collective-permute-start(bf16[256,512]{1,0:T(8,128)(2,1)} %early.1.own), channel_id=1, source_target_pairs={{0,4},{1,5},{2,6},{3,7},{4,0},{5,1},{6,2},{7,3},{8,12},{9,13},{10,... | collective-permute-start | bytes 786440 | tf_op jit(solution)/shard_map/ppermute | solution.py:225
  107.4 15.2 %collective-permute-start.2 = (bf16[256,512]{1,0:T(8,128)(2,1)}, bf16[256,512]{1,0:T(8,128)(2,1)S(1)}, u32[]{:S(2)}, u32[]{:S(2)}) collective-permute-start(bf16[256,512]{1,0:T(8,128)(2,1)} %early.1.own), channel_id=1, source_target_pairs={{0,2},{1,3},{2,0},{3,1},{4,6},{5,7},{6,4},{7,5},{8,10},{9,11},{10,... | collective-permute-start | bytes 786440 | tf_op jit(solution)/shard_map/ppermute | solution.py:225
  122.6 0.0 collective-permute-done.7.refs_2_
  122.6 1.9 %collective-permute-start.9 = (bf16[512,512]{1,0:T(8,128)(2,1)}, bf16[512,512]{1,0:T(8,128)(2,1)S(1)}, u32[]{:S(2)}, u32[]{:S(2)}) collective-permute-start(bf16[512,512]{1,0:T(8,128)(2,1)} %collective-permute-done.7.refs_2_), channel_id=1, source_target_pairs={{128,0},{256,128},{384,256},{512,384},{640,512},{768,640},{896,768... | collective-permute-start | bytes 1572872 | tf_op jit(solution)/shard_map/ppermute | solution.py:175
  124.5 0.0 collective-permute-done.8.refs_3_
  124.6 5.1 %collective-permute-start.10 = (bf16[512,512]{1,0:T(8,128)(2,1)}, bf16[512,512]{1,0:T(8,128)(2,1)S(1)}, u32[]{:S(2)}, u32[]{:S(2)}) collective-permute-start(bf16[512,512]{1,0:T(8,128)(2,1)} %collective-permute-done.8.refs_3_), channel_id=1, source_target_pairs={{896,0},{0,128},{128,256},{256,384},{384,512},{512,640},{640,768},... | collective-permute-start | bytes 1572872 | tf_op jit(solution)/shard_map/ppermute | solution.py:175
  129.7 0.0 collective-permute-done.1.four
  129.7 0.0 copy-start.1
  129.7 2.9 %collective-permute-done.2.two = bf16[256,512]{1,0:T(8,128)(2,1)S(1)} collective-permute-done((bf16[256,512]{1,0:T(8,128)(2,1)}, bf16[256,512]{1,0:T(8,128)(2,1)S(1)}, u32[]{:S(2)}, u32[]{:S(2)}) %collective-permute-start.2) | collective-permute-done | bytes 262176 | tf_op jit(solution)/shard_map/ppermute | solution.py:225
  132.6 0.0 copy-start.2
  132.6 1.1 pad_maximum_fusion
  133.7 0.0 copy-done.2
  133.7 7.6 %collective-permute-start.4 = (bf16[3,256,512]{2,1,0:T(8,128)(2,1)S(1)}, bf16[3,256,512]{2,1,0:T(8,128)(2,1)S(1)}, u32[]{:S(2)}, u32[]{:S(2)}) collective-permute-start(bf16[3,256,512]{2,1,0:T(8,128)(2,1)S(1)} %pad_maximum_fusion), channel_id=1, source_target_pairs={{0,1},{1,0},{2,3},{3,2},{4,5},{5,4},{6,7},{7,6},{8,9},{9,8},{10,11... | collective-permute-start | bytes 2359304 | tf_op jit(solution)/shard_map/ppermute | solution.py:225
  141.4 0.0 copy-done.1
  141.4 3.0 %collective-permute-start.3 = (bf16[256,512]{1,0:T(8,128)(2,1)S(1)}, bf16[256,512]{1,0:T(8,128)(2,1)S(1)}, u32[]{:S(2)}, u32[]{:S(2)}) collective-permute-start(bf16[256,512]{1,0:T(8,128)(2,1)S(1)} %collective-permute-done.1.four), channel_id=1, source_target_pairs={{0,2},{1,3},{2,0},{3,1},{4,6},{5,7},{6,4},{7,5},{8,10},{9,11},{10,... | collective-permute-start | bytes 786440 | tf_op jit(solution)/shard_map/ppermute | solution.py:225
  144.4 0.0 collective-permute-done.9.refs_4_
  144.5 0.0 copy-start.5
  144.5 1.9 %collective-permute-start.11 = (bf16[512,512]{1,0:T(8,128)(2,1)S(1)}, bf16[512,512]{1,0:T(8,128)(2,1)}, u32[]{:S(2)}, u32[]{:S(2)}) collective-permute-start(bf16[512,512]{1,0:T(8,128)(2,1)S(1)} %collective-permute-done.9.refs_4_), channel_id=1, source_target_pairs={{128,0},{256,128},{384,256},{512,384},{640,512},{768,640},{896,768... | collective-permute-start | bytes 1572872 | tf_op jit(solution)/shard_map/ppermute | solution.py:175
  146.4 0.0 collective-permute-done.10.refs_0_
  146.4 0.0 copy-start.6
  146.4 5.1 %collective-permute-start.12 = (bf16[512,512]{1,0:T(8,128)(2,1)S(1)}, bf16[512,512]{1,0:T(8,128)(2,1)}, u32[]{:S(2)}, u32[]{:S(2)}) collective-permute-start(bf16[512,512]{1,0:T(8,128)(2,1)S(1)} %collective-permute-done.10.refs_0_), channel_id=1, source_target_pairs={{896,0},{0,128},{128,256},{256,384},{384,512},{512,640},{640,768},... | collective-permute-start | bytes 1572872 | tf_op jit(solution)/shard_map/ppermute | solution.py:175
  151.6 2.1 %collective-permute-done.3.six = bf16[256,512]{1,0:T(8,128)(2,1)S(1)} collective-permute-done((bf16[256,512]{1,0:T(8,128)(2,1)S(1)}, bf16[256,512]{1,0:T(8,128)(2,1)S(1)}, u32[]{:S(2)}, u32[]{:S(2)}) %collective-permute-start.3) | collective-permute-done | bytes 262176 | tf_op jit(solution)/shard_map/ppermute | solution.py:225
  153.7 0.0 copy-start.7
  153.7 3.5 %collective-permute-start.5 = (bf16[256,512]{1,0:T(8,128)(2,1)S(1)}, bf16[256,512]{1,0:T(8,128)(2,1)S(1)}, u32[]{:S(2)}, u32[]{:S(2)}) collective-permute-start(bf16[256,512]{1,0:T(8,128)(2,1)S(1)} %collective-permute-done.3.six), channel_id=1, source_target_pairs={{0,1},{1,0},{2,3},{3,2},{4,5},{5,4},{6,7},{7,6},{8,9},{9,8},{10,11... | collective-permute-start | bytes 786440 | tf_op jit(solution)/shard_map/ppermute | solution.py:225
  157.2 0.6 pad_add_fusion.place
  157.8 4.1 %collective-permute-done.5.seven = bf16[256,512]{1,0:T(8,128)(2,1)S(1)} collective-permute-done((bf16[256,512]{1,0:T(8,128)(2,1)S(1)}, bf16[256,512]{1,0:T(8,128)(2,1)S(1)}, u32[]{:S(2)}, u32[]{:S(2)}) %collective-permute-start.5) | collective-permute-done | bytes 262176 | tf_op jit(solution)/shard_map/ppermute | solution.py:225
  161.9 0.0 copy-start.8
  161.9 0.0 collective-permute-done.4.odd
  161.9 0.0 copy-done.5
  161.9 0.0 copy-done.7
  161.9 0.7 copy-done.8
  162.6 0.0 copy-start.3
  162.6 0.9 copy-done.3
  163.6 5.1 %most.1 = (f32[256,512]{1,0:T(8,128)}, bf16[3,256,512]{2,1,0:T(8,128)(2,1)}) custom-call(s32[2]{0:T(128)} %pad_add_fusion.place, bf16[256,512]{1,0:T(8,128)(2,1)} %early.1.own, bf16[256,512]{1,0:T(8,128)(2,1)} %copy-done.1, bf16[256,512]{1,0:T(8,128)(2,1)} %copy-done.2, bf16[256,512]{1,0:T(8,128)(2,1)} %copy-done.7, bf16[3,256,512]{2,1,0:T(8,128)(2,1)} %copy-done.3, ...), custom_call_target="tpu_custom_call" | custom-call | flops 671088640 | bytes 6000000 | tf_op jit(solution)/shard_map/most/pallas_call | solution.py:237
  168.7 0.0 copy-done.6
  168.7 0.0 collective-permute-done.11.refs_1_
  168.7 0.0 collective-permute-done.12.refs_2_
  168.7 3.7 %rest.1 = bf16[256,512]{1,0:T(8,128)(2,1)} custom-call(f32[256,512]{1,0:T(8,128)} %get-tuple-element.17.start, bf16[3,256,512]{2,1,0:T(8,128)(2,1)} %get-tuple-element.18.kept, bf16[512,512]{1,0:T(8,128)(2,1)} %copy-done.6, bf16[512,512]{1,0:T(8,128)(2,1)} %collective-permute-done.11.refs_1_, bf16[512,512]{1,0:T(8,128)(2,1)} %collective-permute-done.12.refs_2_), custom_call_target="tpu_custom_call" | custom-call | flops 402653184 | bytes 3000000 | tf_op jit(solution)/shard_map/rest/pallas_call | solution.py:251
Async XLA Ops:
  41.8 29.3 %copy-start = (bf16[16,32,512]{2,1,0:T(8,128)(2,1)}, bf16[16,32,512]{2,1,0:T(8,128)(2,1)S(1)}, u32[]{:S(2)}) copy-start(bf16[16,32,512]{2,1,0:T(8,128)(2,1)S(1)} %all_to_all.5) | copy-start | bytes 1572868
  41.8 15.5 %collective-permute-start.6 = (bf16[512,512]{1,0:T(8,128)(2,1)S(1)}, bf16[512,512]{1,0:T(8,128)(2,1)S(1)}, u32[]{:S(2)}, u32[]{:S(2)}) collective-permute-start(bf16[512,512]{1,0:T(8,128)(2,1)S(1)} %bitcast.12), channel_id=1, source_target_pairs={{896,0},{0,128},{128,256},{256,384},{384,512},{512,640},{640,768},... | collective-permute-start | bytes 1572872 | tf_op jit(solution)/shard_map/ppermute | solution.py:175
  46.5 76.1 %collective-permute-start.7 = (bf16[512,512]{1,0:T(8,128)(2,1)S(1)}, bf16[512,512]{1,0:T(8,128)(2,1)}, u32[]{:S(2)}, u32[]{:S(2)}) collective-permute-start(bf16[512,512]{1,0:T(8,128)(2,1)S(1)} %bitcast.13), channel_id=1, source_target_pairs={{128,0},{256,128},{384,256},{512,384},{640,512},{768,640},{896,768... | collective-permute-start | bytes 1572872 | tf_op jit(solution)/shard_map/ppermute | solution.py:175
  57.3 13.8 %copy-start.4 = (bf16[512,512]{1,0:T(8,128)(2,1)}, bf16[512,512]{1,0:T(8,128)(2,1)S(1)}, u32[]{:S(2)}) copy-start(bf16[512,512]{1,0:T(8,128)(2,1)S(1)} %collective-permute-done.6.refs_1_) | copy-start | bytes 1572868
  57.3 67.2 %collective-permute-start.8 = (bf16[512,512]{1,0:T(8,128)(2,1)S(1)}, bf16[512,512]{1,0:T(8,128)(2,1)}, u32[]{:S(2)}, u32[]{:S(2)}) collective-permute-start(bf16[512,512]{1,0:T(8,128)(2,1)S(1)} %collective-permute-done.6.refs_1_), channel_id=1, source_target_pairs={{896,0},{0,128},{128,256},{256,384},{384,512},{512,640},{640,768},... | collective-permute-start | bytes 1572872 | tf_op jit(solution)/shard_map/ppermute | solution.py:175
  66.5 18.7 %collective-permute-start = (bf16[176,512]{1,0:T(8,128)(2,1)}, bf16[176,512]{1,0:T(8,128)(2,1)S(1)}, u32[]{:S(2)}, u32[]{:S(2)}) collective-permute-start(bf16[176,512]{1,0:T(8,128)(2,1)} %get-tuple-element.12), channel_id=1, source_target_pairs={{0,8},{8,16},{16,24},{24,32},{32,40},{40,48},{48,56},{56,64},{64,7... | collective-permute-start | bytes 540680 | tf_op jit(solution)/shard_map/ppermute | solution.py:204
  85.3 0.7 copy-start.9
  89.6 40.1 %collective-permute-start.1 = (bf16[256,512]{1,0:T(8,128)(2,1)}, bf16[256,512]{1,0:T(8,128)(2,1)S(1)}, u32[]{:S(2)}, u32[]{:S(2)}) collective-permute-start(bf16[256,512]{1,0:T(8,128)(2,1)} %early.1.own), channel_id=1, source_target_pairs={{0,4},{1,5},{2,6},{3,7},{4,0},{5,1},{6,2},{7,3},{8,12},{9,13},{10,... | collective-permute-start | bytes 786440 | tf_op jit(solution)/shard_map/ppermute | solution.py:225
  107.4 25.2 %collective-permute-start.2 = (bf16[256,512]{1,0:T(8,128)(2,1)}, bf16[256,512]{1,0:T(8,128)(2,1)S(1)}, u32[]{:S(2)}, u32[]{:S(2)}) collective-permute-start(bf16[256,512]{1,0:T(8,128)(2,1)} %early.1.own), channel_id=1, source_target_pairs={{0,2},{1,3},{2,0},{3,1},{4,6},{5,7},{6,4},{7,5},{8,10},{9,11},{10,... | collective-permute-start | bytes 786440 | tf_op jit(solution)/shard_map/ppermute | solution.py:225
  122.6 21.8 %collective-permute-start.9 = (bf16[512,512]{1,0:T(8,128)(2,1)}, bf16[512,512]{1,0:T(8,128)(2,1)S(1)}, u32[]{:S(2)}, u32[]{:S(2)}) collective-permute-start(bf16[512,512]{1,0:T(8,128)(2,1)} %collective-permute-done.7.refs_2_), channel_id=1, source_target_pairs={{128,0},{256,128},{384,256},{512,384},{640,512},{768,640},{896,768... | collective-permute-start | bytes 1572872 | tf_op jit(solution)/shard_map/ppermute | solution.py:175
  124.6 21.8 %collective-permute-start.10 = (bf16[512,512]{1,0:T(8,128)(2,1)}, bf16[512,512]{1,0:T(8,128)(2,1)S(1)}, u32[]{:S(2)}, u32[]{:S(2)}) collective-permute-start(bf16[512,512]{1,0:T(8,128)(2,1)} %collective-permute-done.8.refs_3_), channel_id=1, source_target_pairs={{896,0},{0,128},{128,256},{256,384},{384,512},{512,640},{640,768},... | collective-permute-start | bytes 1572872 | tf_op jit(solution)/shard_map/ppermute | solution.py:175
  129.7 11.7 %copy-start.1 = (bf16[256,512]{1,0:T(8,128)(2,1)}, bf16[256,512]{1,0:T(8,128)(2,1)S(1)}, u32[]{:S(2)}) copy-start(bf16[256,512]{1,0:T(8,128)(2,1)S(1)} %collective-permute-done.1.four) | copy-start | bytes 786436
  132.6 1.1 copy-start.2
  133.7 28.2 %collective-permute-start.4 = (bf16[3,256,512]{2,1,0:T(8,128)(2,1)S(1)}, bf16[3,256,512]{2,1,0:T(8,128)(2,1)S(1)}, u32[]{:S(2)}, u32[]{:S(2)}) collective-permute-start(bf16[3,256,512]{2,1,0:T(8,128)(2,1)S(1)} %pad_maximum_fusion), channel_id=1, source_target_pairs={{0,1},{1,0},{2,3},{3,2},{4,5},{5,4},{6,7},{7,6},{8,9},{9,8},{10,11... | collective-permute-start | bytes 2359304 | tf_op jit(solution)/shard_map/ppermute | solution.py:225
  141.4 12.3 %collective-permute-start.3 = (bf16[256,512]{1,0:T(8,128)(2,1)S(1)}, bf16[256,512]{1,0:T(8,128)(2,1)S(1)}, u32[]{:S(2)}, u32[]{:S(2)}) collective-permute-start(bf16[256,512]{1,0:T(8,128)(2,1)S(1)} %collective-permute-done.1.four), channel_id=1, source_target_pairs={{0,2},{1,3},{2,0},{3,1},{4,6},{5,7},{6,4},{7,5},{8,10},{9,11},{10,... | collective-permute-start | bytes 786440 | tf_op jit(solution)/shard_map/ppermute | solution.py:225
  144.5 17.5 %copy-start.5 = (bf16[512,512]{1,0:T(8,128)(2,1)}, bf16[512,512]{1,0:T(8,128)(2,1)S(1)}, u32[]{:S(2)}) copy-start(bf16[512,512]{1,0:T(8,128)(2,1)S(1)} %collective-permute-done.9.refs_4_) | copy-start | bytes 1572868
  144.5 24.2 %collective-permute-start.11 = (bf16[512,512]{1,0:T(8,128)(2,1)S(1)}, bf16[512,512]{1,0:T(8,128)(2,1)}, u32[]{:S(2)}, u32[]{:S(2)}) collective-permute-start(bf16[512,512]{1,0:T(8,128)(2,1)S(1)} %collective-permute-done.9.refs_4_), channel_id=1, source_target_pairs={{128,0},{256,128},{384,256},{512,384},{640,512},{768,640},{896,768... | collective-permute-start | bytes 1572872 | tf_op jit(solution)/shard_map/ppermute | solution.py:175
  146.4 22.3 %copy-start.6 = (bf16[512,512]{1,0:T(8,128)(2,1)}, bf16[512,512]{1,0:T(8,128)(2,1)S(1)}, u32[]{:S(2)}) copy-start(bf16[512,512]{1,0:T(8,128)(2,1)S(1)} %collective-permute-done.10.refs_0_) | copy-start | bytes 1572868
  146.4 22.3 %collective-permute-start.12 = (bf16[512,512]{1,0:T(8,128)(2,1)S(1)}, bf16[512,512]{1,0:T(8,128)(2,1)}, u32[]{:S(2)}, u32[]{:S(2)}) collective-permute-start(bf16[512,512]{1,0:T(8,128)(2,1)S(1)} %collective-permute-done.10.refs_0_), channel_id=1, source_target_pairs={{896,0},{0,128},{128,256},{256,384},{384,512},{512,640},{640,768},... | collective-permute-start | bytes 1572872 | tf_op jit(solution)/shard_map/ppermute | solution.py:175
  153.7 8.3 %copy-start.7 = (bf16[256,512]{1,0:T(8,128)(2,1)}, bf16[256,512]{1,0:T(8,128)(2,1)S(1)}, u32[]{:S(2)}) copy-start(bf16[256,512]{1,0:T(8,128)(2,1)S(1)} %collective-permute-done.3.six) | copy-start | bytes 786436
  153.7 8.3 %collective-permute-start.5 = (bf16[256,512]{1,0:T(8,128)(2,1)S(1)}, bf16[256,512]{1,0:T(8,128)(2,1)S(1)}, u32[]{:S(2)}, u32[]{:S(2)}) collective-permute-start(bf16[256,512]{1,0:T(8,128)(2,1)S(1)} %collective-permute-done.3.six), channel_id=1, source_target_pairs={{0,1},{1,0},{2,3},{3,2},{4,5},{5,4},{6,7},{7,6},{8,9},{9,8},{10,11... | collective-permute-start | bytes 786440 | tf_op jit(solution)/shard_map/ppermute | solution.py:225
  161.9 0.7 copy-start.8
  162.6 0.9 copy-start.3

commit v5 on v3

--- a/solution.py
+++ b/solution.py
@@ -218,7 +218,7 @@
         name="late",
     )(prod, q, medium_filter, skip, fwd, inv)
 
-    over, late = lax.optimization_barrier((over, late))
+    over, late, place = lax.optimization_barrier((over, late, place))
 
     mine = jnp.where(
         lax.axis_index("zh") == 0,
@@ -278,8 +278,7 @@
             name="project",
         )(place, gated, four, two, six, odd, seven, *used, start)
 
-    most = project((0, 1), residual, F32)
-    return project((2,), most, BF16)
+    return project((0, 1, 2), residual, BF16)
 
 
 def solution(mesh):

time: 140 us -> 137 us (0.979)
  Pallas kernels: 20.4 us -> 16.8 us
  other arithmetic: 3.03 us -> 0.39 us
  waiting for transfers between devices: 27.3 us -> 29.2 us
    pallas_call x2 -> x1, Pallas kernels: 10.5 us -> 6.88 us  [project(): pl.pallas_call(functools.partial(project_kernel, batches), out_shape=sds(...]
    another operation x4, other arithmetic: 2.03 us -> 0.27 us  [on_device(): group = jnp.stack([weights[by] for by in order])]
    ppermute x5, waiting for transfers between devices: 22.7 us -> 24.3 us  [exchange(): return lax.ppermute(piece, 'tp', [(i, i ^ by) for i in range(8)])]
    unnamed x34 -> x36, local copies, waits for them, and re-layouts: 3.05 us -> 4.23 us
  transfers between devices with their start and end apart: 20 -> 20, of which waited for: 6 -> 6; matrix products, arithmetic and copies ran while one was open for 3% -> 1% of each run, Pallas kernels for 11% -> 7%
where the time goes in v5:
time: 137 us; the launch traced here: 136 us
  starting transfers between devices  84.7 us (62%)
  waiting for transfers between devices  29.2 us (21%)
  Pallas kernels  16.8 us (12%)
  local copies, waits for them, and re-layouts  4.86 us (4%)
    ppermute x7, starting transfers between devices, shift(): return lax.ppermute(piece, 'y', [((i + by) % 8, i) for i in range(8)])  26.4 us
    ppermute x5, waiting for transfers between devices, exchange(): return lax.ppermute(piece, 'tp', [(i, i ^ by) for i in range(8)])  24.3 us
    ppermute x1, starting transfers between devices, on_device(): over = lax.ppermute(out_weight, 'zh', [(0, 1), (1, 0)])  19.9 us
    ppermute x5, starting transfers between devices, exchange(): return lax.ppermute(piece, 'tp', [(i, i ^ by) for i in range(8)])  13.2 us
    ppermute x3, starting transfers between devices, on_device(): lax.ppermute(mine, 'x', [((i + by) % 4, i) for i in range(4)])  13.1 us
    ppermute x3, starting transfers between devices, on_device(): swapped.append(lax.ppermute(group, 'core', [(0, 1), (1, 0)]))  8.16 us
    pallas_call x1, Pallas kernels, project(): pl.pallas_call(functools.partial(project_kernel, batches), out_shape=sds(...  6.88 us
    unnamed x36, local copies, waits for them, and re-layouts  4.23 us
  transfers between devices with their start and end apart: 20, of which 6 were waited for; matrix products, arithmetic and copies ran while one was open for 1% of the time, Pallas kernels for 7%

profile of v5, /device:TPU:1, one launch (start us, length us, event | category | flops | bytes accessed | tf_op | source)
XLA Modules:
  0.0 136.3 jit_solution(2580676181463826755)
XLA Ops:
  0.0 19.9 %collective-permute-start = (bf16[32,512]{1,0:T(8,128)(2,1)}, bf16[32,512]{1,0:T(8,128)(2,1)S(1)}, u32[]{:S(2)}, u32[]{:S(2)}) collective-permute-start(bf16[32,512]{1,0:T(8,128)(2,1)} %param.13), channel_id=1, source_target_pairs={{0,64},{64,0},{1,65},{65,1},{2,66},{66,2},{3,67},{67,3},{4,68},{68... | collective-permute-start | bytes 98312 | tf_op jit(solution)/shard_map/ppermute | solution.py:202
  19.9 3.6 %local.1 = (bf16[176,512]{1,0:T(8,128)(2,1)}, bf16[256,512]{1,0:T(8,128)(2,1)}, f32[256,512]{1,0:T(8,128)}) custom-call(bf16[3,256,512]{2,1,0:T(8,128)(2,1)} %bitcast.27, bf16[3,7,512]{2,1,0:T(8,128)(2,1)} %bitcast.43), custom_call_target="tpu_custom_call" | custom-call | flops 6000000 | bytes 2000000 | tf_op jit(solution)/shard_map/local/pallas_call | solution.py:204
  23.5 3.9 %collective-permute-start.1 = (bf16[176,512]{1,0:T(8,128)(2,1)}, bf16[176,512]{1,0:T(8,128)(2,1)S(1)}, u32[]{:S(2)}, u32[]{:S(2)}) collective-permute-start(bf16[176,512]{1,0:T(8,128)(2,1)} %get-tuple-element.17), channel_id=1, source_target_pairs={{0,8},{8,16},{16,24},{24,32},{32,40},{40,48},{48,56},{56,64},{64,7... | collective-permute-start | bytes 540680 | tf_op jit(solution)/shard_map/ppermute | solution.py:212
  27.5 0.6 stack.103.place
  28.1 2.7 %late.1 = (bf16[112,512]{1,0:T(8,128)(2,1)}, f32[256,512]{1,0:T(8,128)}) custom-call(bf16[256,512]{1,0:T(8,128)(2,1)} %get-tuple-element.13.prod, f32[256,512]{1,0:T(8,128)} %get-tuple-element.14.q, bf16[128,512]{1,0:T(8,128)(2,1)} %mf.1, f32[1,512]{1,0:T(1,128)} %bitcast.48, bf16[512,256]{1,0:T(8,128)(2,1)} %constant.27.clone.fwd, ...), custom_call_target="tpu_custom_call" | custom-call | flops 300000000 | bytes 3000000 | tf_op jit(solution)/shard_map/late/pallas_call | solution.py:214
  30.8 0.0 collective-permute-done
  30.8 0.0 copy-done.17
  30.8 8.7 %collective-permute-start.7 = (bf16[2,32,512]{2,1,0:T(8,128)(2,1)S(1)}, bf16[2,32,512]{2,1,0:T(8,128)(2,1)S(1)}, u32[]{:S(2)}, u32[]{:S(2)}) collective-permute-start(bf16[2,32,512]{2,1,0:T(8,128)(2,1)S(1)} %maximum_select_fusion.1), channel_id=1, source_target_pairs={{16,0},{32,16},{48,32},{0,48},{17,1},{33,17},{49,33},{1,49},{18,2}... | collective-permute-start | bytes 196616 | tf_op jit(solution)/shard_map/ppermute | solution.py:230
  39.5 1.9 %collective-permute-start.8 = (bf16[2,32,512]{2,1,0:T(8,128)(2,1)S(1)}, bf16[2,32,512]{2,1,0:T(8,128)(2,1)S(1)}, u32[]{:S(2)}, u32[]{:S(2)}) collective-permute-start(bf16[2,32,512]{2,1,0:T(8,128)(2,1)S(1)} %maximum_select_fusion.1), channel_id=1, source_target_pairs={{32,0},{48,16},{0,32},{16,48},{33,1},{49,17},{1,33},{17,49},{34,2}... | collective-permute-start | bytes 196616 | tf_op jit(solution)/shard_map/ppermute | solution.py:230
  41.5 2.5 %collective-permute-start.9 = (bf16[2,32,512]{2,1,0:T(8,128)(2,1)S(1)}, bf16[2,32,512]{2,1,0:T(8,128)(2,1)S(1)}, u32[]{:S(2)}, u32[]{:S(2)}) collective-permute-start(bf16[2,32,512]{2,1,0:T(8,128)(2,1)S(1)} %maximum_select_fusion.1), channel_id=1, source_target_pairs={{48,0},{0,16},{16,32},{32,48},{49,1},{1,17},{17,33},{33,49},{50,2}... | collective-permute-start | bytes 196616 | tf_op jit(solution)/shard_map/ppermute | solution.py:230
  44.0 0.0 collective-permute-done.7
  44.0 2.1 %collective-permute-done.8 = bf16[2,32,512]{2,1,0:T(8,128)(2,1)S(1)} collective-permute-done((bf16[2,32,512]{2,1,0:T(8,128)(2,1)S(1)}, bf16[2,32,512]{2,1,0:T(8,128)(2,1)S(1)}, u32[]{:S(2)}, u32[]{:S(2)}) %collective-permute-start.8) | collective-permute-done | bytes 65568 | tf_op jit(solution)/shard_map/ppermute | solution.py:230
  46.0 1.6 %collective-permute-done.9 = bf16[2,32,512]{2,1,0:T(8,128)(2,1)S(1)} collective-permute-done((bf16[2,32,512]{2,1,0:T(8,128)(2,1)S(1)}, bf16[2,32,512]{2,1,0:T(8,128)(2,1)S(1)}, u32[]{:S(2)}, u32[]{:S(2)}) %collective-permute-start.9) | collective-permute-done | bytes 65568 | tf_op jit(solution)/shard_map/ppermute | solution.py:230
  47.7 0.0 copy-start.1
  47.7 2.1 %collective-permute-start.10 = (bf16[4,2,32,512]{3,2,1,0:T(8,128)(2,1)S(1)}, bf16[4,2,32,512]{3,2,1,0:T(8,128)(2,1)S(1)}, u32[]{:S(2)}, u32[]{:S(2)}) collective-permute-start(bf16[4,2,32,512]{3,2,1,0:T(8,128)(2,1)S(1)} %get-tuple-element.22.refs_6_), channel_id=1, source_target_pairs={{896,0},{0,128},{128,256},{256,384},{384,512},{512,640},{640,768},... | collective-permute-start | bytes 786440 | tf_op jit(solution)/shard_map/ppermute | solution.py:183
  49.8 4.4 %collective-permute-start.11 = (bf16[4,2,32,512]{3,2,1,0:T(8,128)(2,1)S(1)}, bf16[4,2,32,512]{3,2,1,0:T(8,128)(2,1)S(1)}, u32[]{:S(2)}, u32[]{:S(2)}) collective-permute-start(bf16[4,2,32,512]{3,2,1,0:T(8,128)(2,1)S(1)} %get-tuple-element.22.refs_6_), channel_id=1, source_target_pairs={{128,0},{256,128},{384,256},{512,384},{640,512},{768,640},{896,768... | collective-permute-start | bytes 786440 | tf_op jit(solution)/shard_map/ppermute | solution.py:183
  54.2 0.0 collective-permute-done.1.halo
  54.3 0.0 copy-start.16
  54.3 0.7 copy-done.16
  54.9 3.6 %early.1.refs_0_ = bf16[256,512]{1,0:T(8,128)(2,1)} custom-call(bf16[3,256,512]{2,1,0:T(8,128)(2,1)} %bitcast.28, bf16[176,512]{1,0:T(8,128)(2,1)} %copy-done.16, bf16[3,7,512]{2,1,0:T(8,128)(2,1)} %bitcast.44, bf16[256,512]{1,0:T(8,128)(2,1)} %get-tuple-element.13.prod, f32[256,512]{1,0:T(8,128)} %get-tuple-element.14.q, ...), custom_call_target="tpu_custom_call" | custom-call | flops 600000000 | bytes 3000000 | tf_op jit(solution)/shard_map/early/pallas_call | solution.py:232
  58.6 3.5 %collective-permute-start.2 = (bf16[256,512]{1,0:T(8,128)(2,1)}, bf16[256,512]{1,0:T(8,128)(2,1)S(1)}, u32[]{:S(2)}, u32[]{:S(2)}) collective-permute-start(bf16[256,512]{1,0:T(8,128)(2,1)} %early.1.refs_0_), channel_id=1, source_target_pairs={{0,4},{1,5},{2,6},{3,7},{4,0},{5,1},{6,2},{7,3},{8,12},{9,13},{10,... | collective-permute-start | bytes 786440 | tf_op jit(solution)/shard_map/ppermute | solution.py:244
  62.0 4.0 %collective-permute-start.3 = (bf16[256,512]{1,0:T(8,128)(2,1)}, bf16[256,512]{1,0:T(8,128)(2,1)S(1)}, u32[]{:S(2)}, u32[]{:S(2)}) collective-permute-start(bf16[256,512]{1,0:T(8,128)(2,1)} %early.1.refs_0_), channel_id=1, source_target_pairs={{0,2},{1,3},{2,0},{3,1},{4,6},{5,7},{6,4},{7,5},{8,10},{9,11},{10,... | collective-permute-start | bytes 786440 | tf_op jit(solution)/shard_map/ppermute | solution.py:244
  66.0 0.0 copy-done.1
  66.0 6.9 %collective-permute-start.14 = (bf16[4,2,32,512]{3,2,1,0:T(8,128)(2,1)S(1)}, bf16[4,2,32,512]{3,2,1,0:T(8,128)(2,1)S(1)}, u32[]{:S(2)}, u32[]{:S(2)}) collective-permute-start(bf16[4,2,32,512]{3,2,1,0:T(8,128)(2,1)S(1)} %get-tuple-element.22.refs_6_), channel_id=1, source_target_pairs={{512,0},{640,128},{768,256},{896,384},{0,512},{128,640},{256,768},... | collective-permute-start | bytes 786440 | tf_op jit(solution)/shard_map/ppermute | solution.py:183
  73.0 0.0 collective-permute-done.10.refs_7_
  73.0 0.0 copy-start.2
  73.0 1.9 %collective-permute-start.12 = (bf16[4,2,32,512]{3,2,1,0:T(8,128)(2,1)S(1)}, bf16[4,2,32,512]{3,2,1,0:T(8,128)(2,1)S(1)}, u32[]{:S(2)}, u32[]{:S(2)}) collective-permute-start(bf16[4,2,32,512]{3,2,1,0:T(8,128)(2,1)S(1)} %collective-permute-done.10.refs_7_), channel_id=1, source_target_pairs={{896,0},{0,128},{128,256},{256,384},{384,512},{512,640},{640,768},... | collective-permute-start | bytes 786440 | tf_op jit(solution)/shard_map/ppermute | solution.py:183
  74.9 0.0 collective-permute-done.11.refs_8_
  74.9 0.0 copy-start.3
  74.9 4.6 %collective-permute-start.13 = (bf16[4,2,32,512]{3,2,1,0:T(8,128)(2,1)S(1)}, bf16[4,2,32,512]{3,2,1,0:T(8,128)(2,1)S(1)}, u32[]{:S(2)}, u32[]{:S(2)}) collective-permute-start(bf16[4,2,32,512]{3,2,1,0:T(8,128)(2,1)S(1)} %collective-permute-done.11.refs_8_), channel_id=1, source_target_pairs={{128,0},{256,128},{384,256},{512,384},{640,512},{768,640},{896,768... | collective-permute-start | bytes 786440 | tf_op jit(solution)/shard_map/ppermute | solution.py:183
  79.5 0.0 copy-start
  79.5 0.1 pad_maximum_fusion.1
  79.6 8.7 %collective-permute-done.2.refs_1_ = bf16[256,512]{1,0:T(8,128)(2,1)S(1)} collective-permute-done((bf16[256,512]{1,0:T(8,128)(2,1)}, bf16[256,512]{1,0:T(8,128)(2,1)S(1)}, u32[]{:S(2)}, u32[]{:S(2)}) %collective-permute-start.2) | collective-permute-done | bytes 262176 | tf_op jit(solution)/shard_map/ppermute | solution.py:244
  88.3 2.3 %collective-permute-start.17 = (bf16[3,4,2,32,512]{4,3,2,1,0:T(8,128)(2,1)S(1)}, bf16[3,4,2,32,512]{4,3,2,1,0:T(8,128)(2,1)S(1)}, u32[]{:S(2)}, u32[]{:S(2)}) collective-permute-start(bf16[3,4,2,32,512]{4,3,2,1,0:T(8,128)(2,1)S(1)} %pad_maximum_fusion.1), channel_id=1, source_target_pairs={{0,8},{8,0},{1,9},{9,1},{2,10},{10,2},{3,11},{11,3},{4,12},{12,4},... | collective-permute-start | bytes 2359304 | tf_op jit(solution)/shard_map/ppermute | solution.py:260
  90.7 0.0 collective-permute-done.3.refs_2_
  90.7 0.1 pad_maximum_fusion
  90.8 0.6 copy-done.5
  91.4 1.9 %collective-permute-start.5 = (bf16[3,256,512]{2,1,0:T(8,128)(2,1)S(1)}, bf16[3,256,512]{2,1,0:T(8,128)(2,1)S(1)}, u32[]{:S(2)}, u32[]{:S(2)}) collective-permute-start(bf16[3,256,512]{2,1,0:T(8,128)(2,1)S(1)} %pad_maximum_fusion), channel_id=1, source_target_pairs={{0,1},{1,0},{2,3},{3,2},{4,5},{5,4},{6,7},{7,6},{8,9},{9,8},{10,11... | collective-permute-start | bytes 2359304 | tf_op jit(solution)/shard_map/ppermute | solution.py:244
  93.3 0.0 collective-permute-done.12.refs_9_
  93.3 1.9 %collective-permute-start.15 = (bf16[4,2,32,512]{3,2,1,0:T(8,128)(2,1)S(1)}, bf16[4,2,32,512]{3,2,1,0:T(8,128)(2,1)S(1)}, u32[]{:S(2)}, u32[]{:S(2)}) collective-permute-start(bf16[4,2,32,512]{3,2,1,0:T(8,128)(2,1)S(1)} %collective-permute-done.12.refs_9_), channel_id=1, source_target_pairs={{896,0},{0,128},{128,256},{256,384},{384,512},{512,640},{640,768},... | collective-permute-start | bytes 786440 | tf_op jit(solution)/shard_map/ppermute | solution.py:183
  95.2 0.0 collective-permute-done.13.refs_10_
  95.3 0.0 copy-start.8
  95.3 4.6 %collective-permute-start.16 = (bf16[4,2,32,512]{3,2,1,0:T(8,128)(2,1)S(1)}, bf16[4,2,32,512]{3,2,1,0:T(8,128)(2,1)S(1)}, u32[]{:S(2)}, u32[]{:S(2)}) collective-permute-start(bf16[4,2,32,512]{3,2,1,0:T(8,128)(2,1)S(1)} %collective-permute-done.13.refs_10_), channel_id=1, source_target_pairs={{128,0},{256,128},{384,256},{512,384},{640,512},{768,640},{896,768... | collective-permute-start | bytes 786440 | tf_op jit(solution)/shard_map/ppermute | solution.py:183
  99.8 0.0 collective-permute-done.14.refs_11_
  99.9 0.1 pad_maximum_fusion.2
  100.0 0.6 copy-done.6
  100.6 2.5 %collective-permute-start.18 = (bf16[3,4,2,32,512]{4,3,2,1,0:T(8,128)(2,1)S(1)}, bf16[3,4,2,32,512]{4,3,2,1,0:T(8,128)(2,1)}, u32[]{:S(2)}, u32[]{:S(2)}) collective-permute-start(bf16[3,4,2,32,512]{4,3,2,1,0:T(8,128)(2,1)S(1)} %pad_maximum_fusion.2), channel_id=1, source_target_pairs={{0,8},{8,0},{1,9},{9,1},{2,10},{10,2},{3,11},{11,3},{4,12},{12,4},... | collective-permute-start | bytes 2359304 | tf_op jit(solution)/shard_map/ppermute | solution.py:260
  103.1 1.1 collective-permute-done.15.refs_12_
  104.2 1.9 %collective-permute-start.4 = (bf16[256,512]{1,0:T(8,128)(2,1)S(1)}, bf16[256,512]{1,0:T(8,128)(2,1)S(1)}, u32[]{:S(2)}, u32[]{:S(2)}) collective-permute-start(bf16[256,512]{1,0:T(8,128)(2,1)S(1)} %collective-permute-done.2.refs_1_), channel_id=1, source_target_pairs={{0,2},{1,3},{2,0},{3,1},{4,6},{5,7},{6,4},{7,5},{8,10},{9,11},{10,... | collective-permute-start | bytes 786440 | tf_op jit(solution)/shard_map/ppermute | solution.py:244
  106.1 0.0 collective-permute-done.16.refs_13_
  106.2 0.1 pad_maximum_fusion.3
  106.2 0.6 copy-done.10
  106.9 3.3 %collective-permute-start.19 = (bf16[2,4,2,32,512]{4,3,2,1,0:T(8,128)(2,1)S(1)}, bf16[2,4,2,32,512]{4,3,2,1,0:T(8,128)(2,1)S(1)}, u32[]{:S(2)}, u32[]{:S(2)}) collective-permute-start(bf16[2,4,2,32,512]{4,3,2,1,0:T(8,128)(2,1)S(1)} %pad_maximum_fusion.3), channel_id=1, source_target_pairs={{0,8},{8,0},{1,9},{9,1},{2,10},{10,2},{3,11},{11,3},{4,12},{12,4},... | collective-permute-start | bytes 1572872 | tf_op jit(solution)/shard_map/ppermute | solution.py:260
  110.2 9.5 %collective-permute-done.4.refs_3_ = bf16[256,512]{1,0:T(8,128)(2,1)S(1)} collective-permute-done((bf16[256,512]{1,0:T(8,128)(2,1)S(1)}, bf16[256,512]{1,0:T(8,128)(2,1)S(1)}, u32[]{:S(2)}, u32[]{:S(2)}) %collective-permute-start.4) | collective-permute-done | bytes 262176 | tf_op jit(solution)/shard_map/ppermute | solution.py:244
  119.7 1.9 %collective-permute-start.6 = (bf16[256,512]{1,0:T(8,128)(2,1)S(1)}, bf16[256,512]{1,0:T(8,128)(2,1)S(1)}, u32[]{:S(2)}, u32[]{:S(2)}) collective-permute-start(bf16[256,512]{1,0:T(8,128)(2,1)S(1)} %collective-permute-done.4.refs_3_), channel_id=1, source_target_pairs={{0,1},{1,0},{2,3},{3,2},{4,5},{5,4},{6,7},{7,6},{8,9},{9,8},{10,11... | collective-permute-start | bytes 786440 | tf_op jit(solution)/shard_map/ppermute | solution.py:244
  121.6 6.1 %collective-permute-done.6.refs_5_ = bf16[256,512]{1,0:T(8,128)(2,1)S(1)} collective-permute-done((bf16[256,512]{1,0:T(8,128)(2,1)S(1)}, bf16[256,512]{1,0:T(8,128)(2,1)S(1)}, u32[]{:S(2)}, u32[]{:S(2)}) %collective-permute-start.6) | collective-permute-done | bytes 262176 | tf_op jit(solution)/shard_map/ppermute | solution.py:244
  127.7 0.0 collective-permute-done.17.refs_14_
  127.7 0.0 collective-permute-done.5.refs_4_
  127.7 0.9 copy-done.12
  128.6 0.0 collective-permute-done.19.refs_16_
  128.6 0.8 copy-done.13
  129.4 0.0 collective-permute-done.18.refs_15_
  129.4 0.0 copy-done.14
  129.5 6.9 %project.1 = bf16[256,512]{1,0:T(8,128)(2,1)} custom-call(s32[5]{0:T(128)} %stack.103.place, bf16[256,512]{1,0:T(8,128)(2,1)} %early.1.refs_0_, bf16[256,512]{1,0:T(8,128)(2,1)} %copy-done.4, bf16[256,512]{1,0:T(8,128)(2,1)} %copy-done.5, bf16[256,512]{1,0:T(8,128)(2,1)} %copy-done.14, bf16[3,256,512]{2,1,0:T(8,128)(2,1)} %copy-done.12, ...), custom_call_target="tpu_custom_call" | custom-call | flops 1073741824 | bytes 8000000 | tf_op jit(solution)/shard_map/project/pallas_call | solution.py:266
  (24 shorter events, 0.1 us)
Async XLA Ops:
  0.0 30.8 %collective-permute-start = (bf16[32,512]{1,0:T(8,128)(2,1)}, bf16[32,512]{1,0:T(8,128)(2,1)S(1)}, u32[]{:S(2)}, u32[]{:S(2)}) collective-permute-start(bf16[32,512]{1,0:T(8,128)(2,1)} %param.13), channel_id=1, source_target_pairs={{0,64},{64,0},{1,65},{65,1},{2,66},{66,2},{3,67},{67,3},{4,68},{68... | collective-permute-start | bytes 98312 | tf_op jit(solution)/shard_map/ppermute | solution.py:202
  23.5 30.8 %collective-permute-start.1 = (bf16[176,512]{1,0:T(8,128)(2,1)}, bf16[176,512]{1,0:T(8,128)(2,1)S(1)}, u32[]{:S(2)}, u32[]{:S(2)}) collective-permute-start(bf16[176,512]{1,0:T(8,128)(2,1)} %get-tuple-element.17), channel_id=1, source_target_pairs={{0,8},{8,16},{16,24},{24,32},{32,40},{40,48},{48,56},{56,64},{64,7... | collective-permute-start | bytes 540680 | tf_op jit(solution)/shard_map/ppermute | solution.py:212
  28.1 2.7 %copy-start.17 = (bf16[32,512]{1,0:T(8,128)(2,1)S(1)}, bf16[32,512]{1,0:T(8,128)(2,1)}, u32[]{:S(2)}) copy-start(bf16[32,512]{1,0:T(8,128)(2,1)} %param.13) | copy-start | bytes 98308
  30.8 13.2 %collective-permute-start.7 = (bf16[2,32,512]{2,1,0:T(8,128)(2,1)S(1)}, bf16[2,32,512]{2,1,0:T(8,128)(2,1)S(1)}, u32[]{:S(2)}, u32[]{:S(2)}) collective-permute-start(bf16[2,32,512]{2,1,0:T(8,128)(2,1)S(1)} %maximum_select_fusion.1), channel_id=1, source_target_pairs={{16,0},{32,16},{48,32},{0,48},{17,1},{33,17},{49,33},{1,49},{18,2}... | collective-permute-start | bytes 196616 | tf_op jit(solution)/shard_map/ppermute | solution.py:230
  39.5 6.5 %collective-permute-start.8 = (bf16[2,32,512]{2,1,0:T(8,128)(2,1)S(1)}, bf16[2,32,512]{2,1,0:T(8,128)(2,1)S(1)}, u32[]{:S(2)}, u32[]{:S(2)}) collective-permute-start(bf16[2,32,512]{2,1,0:T(8,128)(2,1)S(1)} %maximum_select_fusion.1), channel_id=1, source_target_pairs={{32,0},{48,16},{0,32},{16,48},{33,1},{49,17},{1,33},{17,49},{34,2}... | collective-permute-start | bytes 196616 | tf_op jit(solution)/shard_map/ppermute | solution.py:230
  41.5 6.2 %collective-permute-start.9 = (bf16[2,32,512]{2,1,0:T(8,128)(2,1)S(1)}, bf16[2,32,512]{2,1,0:T(8,128)(2,1)S(1)}, u32[]{:S(2)}, u32[]{:S(2)}) collective-permute-start(bf16[2,32,512]{2,1,0:T(8,128)(2,1)S(1)} %maximum_select_fusion.1), channel_id=1, source_target_pairs={{48,0},{0,16},{16,32},{32,48},{49,1},{1,17},{17,33},{33,49},{50,2}... | collective-permute-start | bytes 196616 | tf_op jit(solution)/shard_map/ppermute | solution.py:230
  47.7 18.3 %copy-start.1 = (bf16[4,2,32,512]{3,2,1,0:T(8,128)(2,1)}, bf16[4,2,32,512]{3,2,1,0:T(8,128)(2,1)S(1)}, u32[]{:S(2)}) copy-start(bf16[4,2,32,512]{3,2,1,0:T(8,128)(2,1)S(1)} %get-tuple-element.22.refs_6_) | copy-start | bytes 786436
  47.7 25.2 %collective-permute-start.10 = (bf16[4,2,32,512]{3,2,1,0:T(8,128)(2,1)S(1)}, bf16[4,2,32,512]{3,2,1,0:T(8,128)(2,1)S(1)}, u32[]{:S(2)}, u32[]{:S(2)}) collective-permute-start(bf16[4,2,32,512]{3,2,1,0:T(8,128)(2,1)S(1)} %get-tuple-element.22.refs_6_), channel_id=1, source_target_pairs={{896,0},{0,128},{128,256},{256,384},{384,512},{512,640},{640,768},... | collective-permute-start | bytes 786440 | tf_op jit(solution)/shard_map/ppermute | solution.py:183
  49.8 25.1 %collective-permute-start.11 = (bf16[4,2,32,512]{3,2,1,0:T(8,128)(2,1)S(1)}, bf16[4,2,32,512]{3,2,1,0:T(8,128)(2,1)S(1)}, u32[]{:S(2)}, u32[]{:S(2)}) collective-permute-start(bf16[4,2,32,512]{3,2,1,0:T(8,128)(2,1)S(1)} %get-tuple-element.22.refs_6_), channel_id=1, source_target_pairs={{128,0},{256,128},{384,256},{512,384},{640,512},{768,640},{896,768... | collective-permute-start | bytes 786440 | tf_op jit(solution)/shard_map/ppermute | solution.py:183
  54.3 0.7 copy-start.16
  58.6 29.8 %collective-permute-start.2 = (bf16[256,512]{1,0:T(8,128)(2,1)}, bf16[256,512]{1,0:T(8,128)(2,1)S(1)}, u32[]{:S(2)}, u32[]{:S(2)}) collective-permute-start(bf16[256,512]{1,0:T(8,128)(2,1)} %early.1.refs_0_), channel_id=1, source_target_pairs={{0,4},{1,5},{2,6},{3,7},{4,0},{5,1},{6,2},{7,3},{8,12},{9,13},{10,... | collective-permute-start | bytes 786440 | tf_op jit(solution)/shard_map/ppermute | solution.py:244
  62.0 28.7 %collective-permute-start.3 = (bf16[256,512]{1,0:T(8,128)(2,1)}, bf16[256,512]{1,0:T(8,128)(2,1)S(1)}, u32[]{:S(2)}, u32[]{:S(2)}) collective-permute-start(bf16[256,512]{1,0:T(8,128)(2,1)} %early.1.refs_0_), channel_id=1, source_target_pairs={{0,2},{1,3},{2,0},{3,1},{4,6},{5,7},{6,4},{7,5},{8,10},{9,11},{10,... | collective-permute-start | bytes 786440 | tf_op jit(solution)/shard_map/ppermute | solution.py:244
  66.0 33.8 %collective-permute-start.14 = (bf16[4,2,32,512]{3,2,1,0:T(8,128)(2,1)S(1)}, bf16[4,2,32,512]{3,2,1,0:T(8,128)(2,1)S(1)}, u32[]{:S(2)}, u32[]{:S(2)}) collective-permute-start(bf16[4,2,32,512]{3,2,1,0:T(8,128)(2,1)S(1)} %get-tuple-element.22.refs_6_), channel_id=1, source_target_pairs={{512,0},{640,128},{768,256},{896,384},{0,512},{128,640},{256,768},... | collective-permute-start | bytes 786440 | tf_op jit(solution)/shard_map/ppermute | solution.py:183
  73.0 6.6 %copy-start.2 = (bf16[4,2,32,512]{3,2,1,0:T(8,128)(2,1)}, bf16[4,2,32,512]{3,2,1,0:T(8,128)(2,1)S(1)}, u32[]{:S(2)}) copy-start(bf16[4,2,32,512]{3,2,1,0:T(8,128)(2,1)S(1)} %collective-permute-done.10.refs_7_) | copy-start | bytes 786436
  73.0 20.3 %collective-permute-start.12 = (bf16[4,2,32,512]{3,2,1,0:T(8,128)(2,1)S(1)}, bf16[4,2,32,512]{3,2,1,0:T(8,128)(2,1)S(1)}, u32[]{:S(2)}, u32[]{:S(2)}) collective-permute-start(bf16[4,2,32,512]{3,2,1,0:T(8,128)(2,1)S(1)} %collective-permute-done.10.refs_7_), channel_id=1, source_target_pairs={{896,0},{0,128},{128,256},{256,384},{384,512},{512,640},{640,768},... | collective-permute-start | bytes 786440 | tf_op jit(solution)/shard_map/ppermute | solution.py:183
  74.9 4.7 %copy-start.3 = (bf16[4,2,32,512]{3,2,1,0:T(8,128)(2,1)}, bf16[4,2,32,512]{3,2,1,0:T(8,128)(2,1)S(1)}, u32[]{:S(2)}) copy-start(bf16[4,2,32,512]{3,2,1,0:T(8,128)(2,1)S(1)} %collective-permute-done.11.refs_8_) | copy-start | bytes 786436
  74.9 20.3 %collective-permute-start.13 = (bf16[4,2,32,512]{3,2,1,0:T(8,128)(2,1)S(1)}, bf16[4,2,32,512]{3,2,1,0:T(8,128)(2,1)S(1)}, u32[]{:S(2)}, u32[]{:S(2)}) collective-permute-start(bf16[4,2,32,512]{3,2,1,0:T(8,128)(2,1)S(1)} %collective-permute-done.11.refs_8_), channel_id=1, source_target_pairs={{128,0},{256,128},{384,256},{512,384},{640,512},{768,640},{896,768... | collective-permute-start | bytes 786440 | tf_op jit(solution)/shard_map/ppermute | solution.py:183
  79.5 11.2 %copy-start = (bf16[256,512]{1,0:T(8,128)(2,1)S(1)}, bf16[256,512]{1,0:T(8,128)(2,1)}, u32[]{:S(2)}) copy-start(bf16[256,512]{1,0:T(8,128)(2,1)} %early.1.refs_0_) | copy-start | bytes 786436
  88.3 15.9 %copy-start.4 = (bf16[256,512]{1,0:T(8,128)(2,1)}, bf16[256,512]{1,0:T(8,128)(2,1)S(1)}, u32[]{:S(2)}) copy-start(bf16[256,512]{1,0:T(8,128)(2,1)S(1)} %collective-permute-done.2.refs_1_) | copy-start | bytes 786436
  88.3 39.4 %collective-permute-start.17 = (bf16[3,4,2,32,512]{4,3,2,1,0:T(8,128)(2,1)S(1)}, bf16[3,4,2,32,512]{4,3,2,1,0:T(8,128)(2,1)S(1)}, u32[]{:S(2)}, u32[]{:S(2)}) collective-permute-start(bf16[3,4,2,32,512]{4,3,2,1,0:T(8,128)(2,1)S(1)} %pad_maximum_fusion.1), channel_id=1, source_target_pairs={{0,8},{8,0},{1,9},{9,1},{2,10},{10,2},{3,11},{11,3},{4,12},{12,4},... | collective-permute-start | bytes 2359304 | tf_op jit(solution)/shard_map/ppermute | solution.py:260
  90.7 0.7 copy-start.5
  91.4 36.3 %collective-permute-start.5 = (bf16[3,256,512]{2,1,0:T(8,128)(2,1)S(1)}, bf16[3,256,512]{2,1,0:T(8,128)(2,1)S(1)}, u32[]{:S(2)}, u32[]{:S(2)}) collective-permute-start(bf16[3,256,512]{2,1,0:T(8,128)(2,1)S(1)} %pad_maximum_fusion), channel_id=1, source_target_pairs={{0,1},{1,0},{2,3},{3,2},{4,5},{5,4},{6,7},{7,6},{8,9},{9,8},{10,11... | collective-permute-start | bytes 2359304 | tf_op jit(solution)/shard_map/ppermute | solution.py:244
  93.3 6.7 %copy-start.7 = (bf16[4,2,32,512]{3,2,1,0:T(8,128)(2,1)}, bf16[4,2,32,512]{3,2,1,0:T(8,128)(2,1)S(1)}, u32[]{:S(2)}) copy-start(bf16[4,2,32,512]{3,2,1,0:T(8,128)(2,1)S(1)} %collective-permute-done.12.refs_9_) | copy-start | bytes 786436
  93.3 10.9 %collective-permute-start.15 = (bf16[4,2,32,512]{3,2,1,0:T(8,128)(2,1)S(1)}, bf16[4,2,32,512]{3,2,1,0:T(8,128)(2,1)S(1)}, u32[]{:S(2)}, u32[]{:S(2)}) collective-permute-start(bf16[4,2,32,512]{3,2,1,0:T(8,128)(2,1)S(1)} %collective-permute-done.12.refs_9_), channel_id=1, source_target_pairs={{896,0},{0,128},{128,256},{256,384},{384,512},{512,640},{640,768},... | collective-permute-start | bytes 786440 | tf_op jit(solution)/shard_map/ppermute | solution.py:183
  95.3 4.7 %copy-start.8 = (bf16[4,2,32,512]{3,2,1,0:T(8,128)(2,1)}, bf16[4,2,32,512]{3,2,1,0:T(8,128)(2,1)S(1)}, u32[]{:S(2)}) copy-start(bf16[4,2,32,512]{3,2,1,0:T(8,128)(2,1)S(1)} %collective-permute-done.13.refs_10_) | copy-start | bytes 786436
  95.3 10.9 %collective-permute-start.16 = (bf16[4,2,32,512]{3,2,1,0:T(8,128)(2,1)S(1)}, bf16[4,2,32,512]{3,2,1,0:T(8,128)(2,1)S(1)}, u32[]{:S(2)}, u32[]{:S(2)}) collective-permute-start(bf16[4,2,32,512]{3,2,1,0:T(8,128)(2,1)S(1)} %collective-permute-done.13.refs_10_), channel_id=1, source_target_pairs={{128,0},{256,128},{384,256},{512,384},{640,512},{768,640},{896,768... | collective-permute-start | bytes 786440 | tf_op jit(solution)/shard_map/ppermute | solution.py:183
  99.9 0.7 copy-start.6
  100.6 28.9 %collective-permute-start.18 = (bf16[3,4,2,32,512]{4,3,2,1,0:T(8,128)(2,1)S(1)}, bf16[3,4,2,32,512]{4,3,2,1,0:T(8,128)(2,1)}, u32[]{:S(2)}, u32[]{:S(2)}) collective-permute-start(bf16[3,4,2,32,512]{4,3,2,1,0:T(8,128)(2,1)S(1)} %pad_maximum_fusion.2), channel_id=1, source_target_pairs={{0,8},{8,0},{1,9},{9,1},{2,10},{10,2},{3,11},{11,3},{4,12},{12,4},... | collective-permute-start | bytes 2359304 | tf_op jit(solution)/shard_map/ppermute | solution.py:260
  104.2 2.0 %copy-start.9 = (bf16[4,2,32,512]{3,2,1,0:T(8,128)(2,1)}, bf16[4,2,32,512]{3,2,1,0:T(8,128)(2,1)S(1)}, u32[]{:S(2)}) copy-start(bf16[4,2,32,512]{3,2,1,0:T(8,128)(2,1)S(1)} %collective-permute-done.15.refs_12_) | copy-start | bytes 786436
  104.2 15.4 %collective-permute-start.4 = (bf16[256,512]{1,0:T(8,128)(2,1)S(1)}, bf16[256,512]{1,0:T(8,128)(2,1)S(1)}, u32[]{:S(2)}, u32[]{:S(2)}) collective-permute-start(bf16[256,512]{1,0:T(8,128)(2,1)S(1)} %collective-permute-done.2.refs_1_), channel_id=1, source_target_pairs={{0,2},{1,3},{2,0},{3,1},{4,6},{5,7},{6,4},{7,5},{8,10},{9,11},{10,... | collective-permute-start | bytes 786440 | tf_op jit(solution)/shard_map/ppermute | solution.py:244
  106.2 0.7 copy-start.10
  106.9 21.8 %collective-permute-start.19 = (bf16[2,4,2,32,512]{4,3,2,1,0:T(8,128)(2,1)S(1)}, bf16[2,4,2,32,512]{4,3,2,1,0:T(8,128)(2,1)S(1)}, u32[]{:S(2)}, u32[]{:S(2)}) collective-permute-start(bf16[2,4,2,32,512]{4,3,2,1,0:T(8,128)(2,1)S(1)} %pad_maximum_fusion.3), channel_id=1, source_target_pairs={{0,8},{8,0},{1,9},{9,1},{2,10},{10,2},{3,11},{11,3},{4,12},{12,4},... | collective-permute-start | bytes 1572872 | tf_op jit(solution)/shard_map/ppermute | solution.py:260
  119.7 9.8 %copy-start.14 = (bf16[256,512]{1,0:T(8,128)(2,1)}, bf16[256,512]{1,0:T(8,128)(2,1)S(1)}, u32[]{:S(2)}) copy-start(bf16[256,512]{1,0:T(8,128)(2,1)S(1)} %collective-permute-done.4.refs_3_) | copy-start | bytes 786436
  119.7 8.0 %collective-permute-start.6 = (bf16[256,512]{1,0:T(8,128)(2,1)S(1)}, bf16[256,512]{1,0:T(8,128)(2,1)S(1)}, u32[]{:S(2)}, u32[]{:S(2)}) collective-permute-start(bf16[256,512]{1,0:T(8,128)(2,1)S(1)} %collective-permute-done.4.refs_3_), channel_id=1, source_target_pairs={{0,1},{1,0},{2,3},{3,2},{4,5},{5,4},{6,7},{7,6},{8,9},{9,8},{10,11... | collective-permute-start | bytes 786440 | tf_op jit(solution)/shard_map/ppermute | solution.py:244
  127.7 1.8 %copy-start.15 = (bf16[256,512]{1,0:T(8,128)(2,1)}, bf16[256,512]{1,0:T(8,128)(2,1)S(1)}, u32[]{:S(2)}) copy-start(bf16[256,512]{1,0:T(8,128)(2,1)S(1)} %collective-permute-done.6.refs_5_) | copy-start | bytes 786436
  127.7 1.8 %copy-start.11 = (bf16[3,4,2,32,512]{4,3,2,1,0:T(8,128)(2,1)}, bf16[3,4,2,32,512]{4,3,2,1,0:T(8,128)(2,1)S(1)}, u32[]{:S(2)}) copy-start(bf16[3,4,2,32,512]{4,3,2,1,0:T(8,128)(2,1)S(1)} %collective-permute-done.17.refs_14_) | copy-start | bytes 2359300
  127.7 0.9 copy-start.12
  128.6 0.8 copy-start.13
